TPU v7x, 32 devices: a whole 2x2x4 slice. The times are simulated.
32 devices in a mesh: grp: 2 (over x), seq: 16 (over z, y, core).
Axes of the slice: x: 2, y: 2, z: 4, core: 2. Of those that a mesh axis runs over, the one named last changes fastest.
Arguments:
- hidden_in: bfloat16 [2, 3, 2, 2048, 512], P('grp', None, None, 'seq'), may hold values from -6 to 6
- cotangent: bfloat16 [2, 3, 2, 2048, 512], P('grp', None, None, 'seq'), may hold values from -6 to 6
- cont_prompt: int32 [2, 12], P('grp'), may hold values from 0 to 2
- value_proj: bfloat16 [512, 1024], P('seq'), may hold values from -0.25 to 0.25
- shared_proj: bfloat16 [512, 128], P('seq'), may hold values from -0.25 to 0.25
- reset_proj: bfloat16 [512, 1024], P('seq'), may hold values from -0.25 to 0.25
- hidden_proj: bfloat16 [1024, 512], P('seq'), may hold values from -2 to 2
- inner_proj: bfloat16 [512, 1024], P('seq'), may hold values from -0.25 to 0.25
- outer_proj: bfloat16 [1024, 512], P('seq'), may hold values from -0.1875 to 0.1875
- ema_alpha: bfloat16 [512, 16], P('seq'), may hold values from 5e-05 to 0.3
- ema_delta: bfloat16 [512, 16], P('seq'), may hold values from 0.5 to 1
- ema_beta: bfloat16 [512, 16], P('seq'), may hold values from -600 to 600
- ema_eta: bfloat16 [512, 16], P('seq'), may hold values from -1.5 to 1.5
- ema_omega: bfloat16 [512], P('seq'), may hold values from -4 to 4
- norm_gain: bfloat16 [512], P('seq'), may hold values from 0.5 to 1.5
- ffn_gain: bfloat16 [512], P('seq'), may hold values from 0.5 to 1.5
- query_scale: bfloat16 [128], P('seq'), may hold values from -8 to 8
- query_shift: bfloat16 [128], P('seq'), may hold values from -2 to 2
- key_scale: bfloat16 [128], P('seq'), may hold values from -8 to 8
Outputs:
- layer_out: bfloat16 [2, 3, 2, 2048, 512], P('grp', None, None, 'seq')
- input_grad: bfloat16 [2, 3, 2, 2048, 512], P('grp', None, None, 'seq')
- value_grad: float32 [512, 1024], P('seq')
- shared_grad: float32 [512, 128], P('seq')
- reset_grad: float32 [512, 1024], P('seq')
- hidden_grad: float32 [1024, 512], P('seq')
- inner_grad: float32 [512, 1024], P('seq')
- outer_grad: float32 [1024, 512], P('seq')
- alpha_grad: float32 [512, 16], P('seq')
- delta_grad: float32 [512, 16], P('seq')
- beta_grad: float32 [512, 16], P('seq')
- eta_grad: float32 [512, 16], P('seq')
- omega_grad: float32 [512], P('seq')
- norm_gain_grad: float32 [512], P('seq')
- ffn_gain_grad: float32 [512], P('seq')
- query_scale_grad: float32 [128], P('seq')
- query_shift_grad: float32 [128], P('seq')
- key_scale_grad: float32 [128], P('seq')
All inputs are finite; a program needn't handle non-finite values.
Results may differ from a plain program's by a relative error of at most 0.04.
Values may be sent and summed in bfloat16 or wider, within the bound.
A program may use at most 320 MiB of HBM per device.

v0:
```python
import functools
import math

import jax
import jax.numpy as jnp
from jax import lax
from jax.experimental import pallas as pl
from jax.experimental.pallas import tpu as pltpu
from jax.sharding import PartitionSpec as P

CLEN = 512
NORM_EPS = 1e-05
MASKED_SCORE = -1e30
MESH = pl.DeviceIdType.MESH
SUB = 16
NJ = 16
TINY = 1e-20
F32 = jnp.float32
BF16 = jnp.bfloat16
VMEM = pl.BlockSpec(memory_space=pltpu.VMEM)
ANY = pl.BlockSpec(memory_space=pl.ANY)
SMEM = pl.BlockSpec(memory_space=pltpu.SMEM)


def shift_down(value, count):
    rows = lax.broadcasted_iota(jnp.int32, value.shape, 0)
    return jnp.where(rows >= count, pltpu.roll(value, count, 0), 0.0)


def shift_up(value, count):
    rows = lax.broadcasted_iota(jnp.int32, value.shape, 0)
    return jnp.where(rows < 8 - count, pltpu.roll(value, 8 - count, 0), 0.0)


def row_of(ref, row):
    return jnp.broadcast_to(ref[pl.ds(row, 1), :], (8, 128))


def ema_local_pass(rows, x_ref, decay, decay16, decay32, decay64, inner_ref, final_ref, backward):
    shift = shift_up if backward else shift_down

    def body(item, carry):
        row, lane = item // 4, item % 4
        base = lane * (rows * 128) + row * 128
        dec = [row_of(decay, lane * 16 + j) for j in range(NJ)]
        state = [jnp.zeros((8, 128), F32)] * NJ
        for step in range(SUB - 1, -1, -1) if backward else range(SUB):
            x = x_ref[pl.ds(base + step, 8, stride=SUB), :]
            if backward:
                state = [dec[j] * (state[j] + x) for j in range(NJ)]
            else:
                state = [dec[j] * state[j] + x for j in range(NJ)]
        for j in range(NJ):
            total = state[j]
            total = total + row_of(decay16, lane * 16 + j) * shift(total, 1)
            total = total + row_of(decay32, lane * 16 + j) * shift(total, 2)
            total = total + row_of(decay64, lane * 16 + j) * shift(total, 4)
            inner_ref[pl.ds((item * 16 + j) * 8, 8), :] = shift(total, 1)
            final_ref[pl.ds(row * 64 + lane * 16 + j, 1), :] = total[0:1] if backward else total[7:8]
        return carry

    lax.fori_loop(0, rows * 4, body, 0)


def ema_apply_pass(rows, x_ref, decay, mix, omega, power, inner_ref, start_ref, y_ref):
    def body(item, carry):
        row, lane = item // 4, item % 4
        base = lane * (rows * 128) + row * 128
        state = [
            inner_ref[pl.ds((item * 16 + j) * 8, 8), :]
            + power[pl.ds((lane * 16 + j) * 8, 8), :] * row_of(start_ref, row * 64 + lane * 16 + j)
            for j in range(NJ)
        ]
        skip = row_of(omega, lane)
        for step in range(SUB):
            x = x_ref[pl.ds(base + step, 8, stride=SUB), :]
            sums = [skip * x, None]
            for j in range(NJ):
                state[j] = row_of(decay, lane * 16 + j) * state[j] + x
                term = row_of(mix, lane * 16 + j) * state[j]
                sums[j % 2] = term if sums[j % 2] is None else sums[j % 2] + term
            y_ref[pl.ds(base + step, 8, stride=SUB), :] = sums[0] + sums[1]
        return carry

    lax.fori_loop(0, rows * 4, body, 0)


def ema_back_pass(
    rows, x_rows, x_ref, g_ref, decay, mix, omega, power, inner_ref, start_ref, power_rev,
    back_inner_ref, back_start_ref, dx_ref, sum_in, sum_decay, sum_out, kept,
):
    half = 8

    def body(item, carry):
        row, lane = item // 4, item % 4
        base = lane * (rows * 128) + row * 128
        x_base = lane * (x_rows * 128) + row * 128
        skip = row_of(omega, lane)
        for part in range(NJ // half):
            js = range(part * half, part * half + half)
            dec = [row_of(decay, lane * 16 + j) for j in js]
            state = [
                inner_ref[pl.ds((item * 16 + j) * 8, 8), :]
                + power[pl.ds((lane * 16 + j) * 8, 8), :] * row_of(start_ref, row * 64 + lane * 16 + j)
                for j in js
            ]
            for step in range(SUB):
                x = x_ref[pl.ds(x_base + step, 8, stride=SUB), :]
                for i in range(half):
                    kept[step * half + i] = state[i]
                    state[i] = dec[i] * state[i] + x
            adj = [
                back_inner_ref[pl.ds((item * 16 + j) * 8, 8), :]
                + power_rev[pl.ds((lane * 16 + j) * 8, 8), :]
                * row_of(back_start_ref, row * 64 + lane * 16 + j)
                for j in js
            ]
            weight = [row_of(mix, lane * 16 + j) for j in js]
            edge = [-(adj[i] * state[i]) for i in range(half)]
            first, second = [None] * half, [None] * half
            for step in range(SUB - 1, -1, -1):
                x = x_ref[pl.ds(x_base + step, 8, stride=SUB), :]
                g = g_ref[pl.ds(base + step, 8, stride=SUB), :]
                sums = [skip * g if part == 0 else dx_ref[pl.ds(base + step, 8, stride=SUB), :], None]
                for i in range(half):
                    full = adj[i] + g
                    term = weight[i] * full
                    sums[i % 2] = term if sums[i % 2] is None else sums[i % 2] + term
                    with_x, with_s = full * x, full * kept[step * half + i]
                    first[i] = with_x if first[i] is None else first[i] + with_x
                    second[i] = with_s if second[i] is None else second[i] + with_s
                    adj[i] = dec[i] * full
                dx_ref[pl.ds(base + step, 8, stride=SUB), :] = sums[0] + sums[1]
            for i, j in enumerate(js):
                at = pl.ds(lane * 16 + j, 1)
                flow = edge[i] + adj[i] * kept[i]
                total = jnp.sum(first[i], axis=0, keepdims=True)
                sum_in[at, :] += total
                sum_decay[at, :] += jnp.sum(second[i], axis=0, keepdims=True)
                sum_out[at, :] += total + jnp.sum(flow, axis=0, keepdims=True)
        return carry

    lax.fori_loop(0, rows * 4, body, 0)


class Place:
    def __init__(self, n, groups):
        self.n, self.nq, self.groups = n, n // 4, groups
        self.g, self.s = lax.axis_index("grp"), lax.axis_index("seq")
        self.c, self.y, self.q, self.x = self.s % 2, (self.s // 2) % 2, self.s // 4, self.g % 2
        self.pos = self.s % 4
        self.core = (self.g, self.s + 1 - 2 * self.c)
        self.side = (self.g, self.s + 2 - 4 * self.y)
        self.cross = (self.g + 1 - 2 * self.x, self.s)
        self.is_last = self.s == n - 1

    def quad(self, k):
        return (self.q + k) % self.nq

    def at_quad(self, q):
        return (self.g, q * 4 + self.pos)

    def group_peers(self):
        return [(self.g, (self.s + k) % self.n) for k in range(1, self.n)]

    def cross_bit(self, bit):
        return (self.g + bit - 2 * bit * ((self.g // bit) % 2), self.s)

    def cross_bits(self):
        return [1 << b for b in range(self.groups.bit_length() - 1)]


def meet(peers):
    barrier = pltpu.get_barrier_semaphore()
    for peer in peers:
        pl.semaphore_signal(barrier, inc=1, device_id=peer, device_id_type=MESH)
    pl.semaphore_wait(barrier, len(peers))


def remote(src, dst, send, recv, device):
    return pltpu.make_async_remote_copy(
        src_ref=src, dst_ref=dst, send_sem=send, recv_sem=recv, device_id=device, device_id_type=MESH
    )


def gather_kernel(n, groups, s_in, a_in, b_in, x_in, s_out, a_out, b_out, x_out, ss, sr, zs, zr, ys, yr, xs, xr, cs, cr, ts, tr, ls):
    me = Place(n, groups)
    nq = me.nq
    meet(me.group_peers() + [me.cross])
    mats = ((a_in, a_out, a_in.shape[-1] // 2), (b_in, b_out, b_in.shape[-1] // 2))
    sent = []

    def send(*args):
        copy = remote(*args)
        copy.start()
        sent.append(copy)

    def got(ref, recv):
        remote(ref, ref, ls.at[0], recv, me.core).wait_recv()

    own = [pltpu.make_async_copy(s_in, s_out.at[me.s], ls.at[0])]
    own += [pltpu.make_async_copy(w_in, w_out.at[me.s], ls.at[1 + i]) for i, (w_in, w_out, _) in enumerate(mats)]
    for copy in own:
        copy.start()
    for k in range(1, n):
        send(s_in, s_out.at[me.s], ss.at[k - 1], sr.at[k - 1], (me.g, (me.s + k) % n))

    @pl.when(me.is_last)
    def _():
        for j in range(3):
            remote(x_in.at[j], x_out.at[j], ts.at[j], tr.at[0], (me.g, 4 * (nq - 1) + j)).start()
        pltpu.make_async_copy(x_in.at[3], x_out.at[3], ls.at[3]).start()

    def half(ref, width, which):
        return ref.at[:, pl.ds(pl.multiple_of(which * width, 128), width)]

    for k in range(1, nq):
        for i, (w_in, w_out, width) in enumerate(mats):
            send(half(w_in, width, me.x), half(w_out.at[me.s], width, me.x), zs.at[k - 1, i], zr.at[k - 1, i], me.at_quad(me.quad(k)))
    for i, (w_in, w_out, width) in enumerate(mats):
        send(w_in, w_out.at[me.s], ys.at[0, i], yr.at[0, i], me.side)
        send(w_in, w_out.at[me.s], cs.at[0, i], cr.at[0, i], me.core)

    @pl.when(me.q == nq - 1)
    def _():
        @pl.when(me.is_last)
        def _():
            pltpu.make_async_copy(x_in.at[3], x_out.at[3], ls.at[3]).wait()

        @pl.when(jnp.logical_not(me.is_last))
        def _():
            got(x_out.at[me.pos], tr.at[0])

        for k in range(1, nq):
            remote(x_out.at[me.pos], x_out.at[me.pos], ts.at[2 + k], tr.at[1], me.at_quad(me.quad(k))).start()

    other = 1 - me.x
    for k in range(1, nq):
        shard = me.quad(nq - k) * 4 + me.pos
        for i, (w_in, w_out, width) in enumerate(mats):
            piece = half(w_out.at[shard], width, me.x)
            got(piece, zr.at[k - 1, i])
            send(piece, piece, ys.at[k, i], yr.at[k, i], me.side)
            send(piece, piece, xs.at[k - 1, i], xr.at[k - 1, i], me.cross)
            send(piece, piece, cs.at[k, i], cr.at[k, i], me.core)

    @pl.when(me.q != nq - 1)
    def _():
        got(x_out.at[me.pos], tr.at[1])

    mine = x_out.at[me.pos]
    send(mine, mine, ts.at[nq + 2], tr.at[2], me.side)
    send(mine, mine, ts.at[nq + 3], tr.at[3], me.core)

    side_pos = me.pos + 2 - 4 * me.y
    for k in range(nq):
        shard = me.quad(nq - k) * 4 + side_pos
        for i, (w_in, w_out, width) in enumerate(mats):
            piece = w_out.at[shard] if k == 0 else half(w_out.at[shard], width, me.x)
            got(piece, yr.at[k, i])
            if k:
                send(piece, piece, xs.at[nq - 2 + k, i], xr.at[nq - 2 + k, i], me.cross)
            send(piece, piece, cs.at[nq + k, i], cr.at[nq + k, i], me.core)
    theirs = x_out.at[side_pos]
    got(theirs, tr.at[2])
    send(theirs, theirs, ts.at[nq + 4], tr.at[4], me.core)
    for group, pos in ((0, me.pos), (1, side_pos)):
        for k in range(1, nq):
            shard = me.quad(nq - k) * 4 + pos
            at = group * (nq - 1) + k - 1
            for i, (w_in, w_out, width) in enumerate(mats):
                piece = half(w_out.at[shard], width, other)
                got(piece, xr.at[at, i])
                send(piece, piece, cs.at[2 * nq + at, i], cr.at[2 * nq + at, i], me.core)
    flip = 1 - 2 * me.c
    for group, pos in ((0, me.pos + flip), (1, side_pos + flip)):
        for k in range(nq):
            shard = me.quad(nq - k) * 4 + pos
            for i, (w_in, w_out, width) in enumerate(mats):
                if k == 0:
                    got(w_out.at[shard], cr.at[group * nq, i])
                else:
                    got(half(w_out.at[shard], width, me.x), cr.at[group * nq + k, i])
                    at = 2 * nq + group * (nq - 1) + k - 1
                    got(half(w_out.at[shard], width, other), cr.at[at, i])
    got(x_out.at[me.pos + flip], tr.at[3])
    got(x_out.at[side_pos + flip], tr.at[4])
    for k in range(1, n):
        got(s_out.at[(me.s + n - k) % n], sr.at[k - 1])
    for copy in own:
        copy.wait()
    for copy in sent:
        copy.wait_send()

    @pl.when(me.is_last)
    def _():
        for j in range(3):
            remote(x_in.at[j], x_out.at[j], ts.at[j], tr.at[0], (me.g, 4 * (nq - 1) + j)).wait_send()

    @pl.when(me.q == nq - 1)
    def _():
        for k in range(1, nq):
            remote(x_out.at[me.pos], x_out.at[me.pos], ts.at[2 + k], tr.at[1], me.at_quad(me.quad(k))).wait_send()


def gather_call(n, groups, small, mat_a, mat_b, tail):
    nq = n // 4
    sems = [(n - 1,), (n - 1,), (nq - 1, 2), (nq - 1, 2), (nq, 2), (nq, 2), (2 * nq - 2, 2), (2 * nq - 2, 2), (4 * nq - 2, 2), (4 * nq - 2, 2), (nq + 5,), (5,), (4,)]
    return pl.pallas_call(
        functools.partial(gather_kernel, n, groups),
        out_shape=[
            jax.ShapeDtypeStruct((n,) + small.shape, BF16),
            jax.ShapeDtypeStruct((n,) + mat_a.shape, BF16),
            jax.ShapeDtypeStruct((n,) + mat_b.shape, BF16),
            jax.ShapeDtypeStruct(tail.shape, BF16),
        ],
        in_specs=[ANY] * 4,
        out_specs=[ANY] * 4,
        scratch_shapes=[pltpu.SemaphoreType.DMA(shape) for shape in sems],
        compiler_params=pltpu.CompilerParams(collective_id=0, has_side_effects=True),
        name="gather_weights",
    )(small, mat_a, mat_b, tail)


def pick(index, values):
    out = values[0]
    for k in range(1, len(values)):
        out = jnp.where(index == k, values[k], out)
    return out


def forward_exchange(n, groups, f_ref, ab_ref, d_ref, sel_ref, s_ref, m0, r0, m1, r1, m2, r2, ss, rs, zs, zr, ps, pr):
    me = Place(n, groups)
    nq = me.nq
    meet(me.group_peers())
    one, two, three, four = d_ref[0], d_ref[1], d_ref[2], d_ref[3]
    m0[...] = f_ref[0:3].astype(BF16)
    copy = remote(m0, r0, ss.at[0], rs.at[0], me.core)
    copy.start()
    copy.wait()
    upper_core, upper_side = me.c == 1, me.y == 1
    mine = f_ref[0:3]
    other = r0[...].astype(F32)
    lower = jnp.where(upper_core, other, mine)
    upper = jnp.where(upper_core, mine, other)
    pair = one * lower + upper
    before = jnp.where(upper_core, other, 0.0)
    m1[0] = pair.astype(BF16)
    m1[1, :, 0] = lower[:, 0].astype(BF16)
    copy = remote(m1, r1, ss.at[1], rs.at[1], me.side)
    m1[1, :, 1] = jnp.zeros_like(m1[1, :, 1])
    copy.start()
    copy.wait()
    far = r1[0].astype(F32)
    low_pair = jnp.where(upper_side, far, pair)
    high_pair = jnp.where(upper_side, pair, far)
    total = two * low_pair + high_pair
    before = jnp.where(upper_side, jnp.where(upper_core, one * far, far), 0.0) + before
    third = jnp.where(upper_side, lower[:, 0], r1[1, :, 0].astype(F32))
    last_in = one * low_pair[:, 0] + third
    m2[0] = total[:, 0].astype(BF16)
    m2[1] = last_in.astype(BF16)
    sends = []
    for k in range(1, nq):
        copy = remote(m2.at[0], r2.at[me.q], zs.at[k - 1], zr.at[k - 1], me.at_quad(me.quad(k)))
        copy.start()
        sends.append(copy)

    @pl.when(me.q == nq - 1)
    def _():
        for k in range(1, nq):
            remote(m2.at[1], r2.at[nq], ps.at[k - 1], pr.at[0], me.at_quad(me.quad(k))).start()
        r2[nq] = m2[1]

    r2[me.q] = m2[0]
    for k in range(1, nq):
        src = r2.at[me.quad(nq - k)]
        remote(src, src, zs.at[k - 1], zr.at[k - 1], me.core).wait_recv()

    @pl.when(me.q != nq - 1)
    def _():
        remote(r2.at[nq], r2.at[nq], ps.at[0], pr.at[0], me.core).wait_recv()

    run = jnp.zeros((3, 64, 128), F32)
    carry, tail_in = run, run
    for k in range(nq):
        carry = jnp.where(me.q == k, run, carry)
        if k == nq - 1:
            tail_in = three * run + r2[nq].astype(F32)
        run = four * run + r2[k].astype(F32)
    low = (ab_ref[...] * run).astype(BF16).astype(F32)
    safe = jnp.abs(ab_ref[...]) >= TINY
    begin = jnp.where(safe, low / jnp.where(safe, ab_ref[...], 1.0), run)
    lead = pick(me.pos, [jnp.ones_like(one), one, two, three])
    for p in range(3):
        start = sel_ref[p * 3] * begin[0] + sel_ref[p * 3 + 1] * begin[1] + sel_ref[p * 3 + 2] * begin[2]
        s_ref[2 * p] = lead * carry[p] + before[p, 0]
        s_ref[2 * p + 1] = lead * start + before[p, 1]
        s_ref[6 + p] = tail_in[p]
    for copy in sends:
        copy.wait_send()

    @pl.when(me.q == nq - 1)
    def _():
        for k in range(1, nq):
            remote(m2.at[1], r2.at[nq], ps.at[k - 1], pr.at[0], me.at_quad(me.quad(k))).wait_send()


def forward_exchange_call(n, groups, finals, ab, decays, sel):
    nq = n // 4
    dma = pltpu.SemaphoreType.DMA
    return pl.pallas_call(
        functools.partial(forward_exchange, n, groups),
        out_shape=jax.ShapeDtypeStruct((9, 64, 128), F32),
        in_specs=[VMEM, VMEM, VMEM, SMEM],
        out_specs=VMEM,
        scratch_shapes=[
            pltpu.VMEM((3, 2, 64, 128), BF16), pltpu.VMEM((3, 2, 64, 128), BF16),
            pltpu.VMEM((2, 3, 2, 64, 128), BF16), pltpu.VMEM((2, 3, 2, 64, 128), BF16),
            pltpu.VMEM((2, 3, 64, 128), BF16), pltpu.VMEM((nq + 1, 3, 64, 128), BF16),
            dma((2,)), dma((2,)), dma((nq - 1,)), dma((nq - 1,)), dma((nq - 1,)), dma((1,)),
        ],
        compiler_params=pltpu.CompilerParams(collective_id=1, has_side_effects=True, vmem_limit_bytes=40 << 20),
        name="forward_exchange",
    )(finals, ab, decays, sel)


def backward_exchange(n, groups, f_ref, d_ref, sel_ref, s_ref, m0, r0, m1, r1, m2, r2, ss, rs, zs, zr):
    me = Place(n, groups)
    nq = me.nq
    meet(me.group_peers())
    one, two, three, four = d_ref[0], d_ref[1], d_ref[2], d_ref[3]
    m0[...] = f_ref[...].astype(BF16)
    copy = remote(m0, r0, ss.at[0], rs.at[0], me.core)
    copy.start()
    copy.wait()
    upper_core, upper_side = me.c == 1, me.y == 1
    mine = f_ref[...]
    other = r0[...].astype(F32)
    lower = jnp.where(upper_core, other, mine)
    upper = jnp.where(upper_core, mine, other)
    pair = lower + one * upper
    after = jnp.where(upper_core, 0.0, other)
    m1[...] = pair.astype(BF16)
    copy = remote(m1, r1, ss.at[1], rs.at[1], me.side)
    copy.start()
    copy.wait()
    far = r1[...].astype(F32)
    low_pair = jnp.where(upper_side, far, pair)
    high_pair = jnp.where(upper_side, pair, far)
    total = low_pair + two * high_pair
    after = jnp.where(upper_side, 0.0, jnp.where(upper_core, far, one * far)) + after
    m2[0] = total[:, 0].astype(BF16)
    for m in range(3):
        m2[1, m] = (sel_ref[m] * total[0, 1] + sel_ref[3 + m] * total[1, 1] + sel_ref[6 + m] * total[2, 1]).astype(BF16)
    sends = []
    for k in range(1, nq):
        copy = remote(m2, r2.at[me.q], zs.at[k - 1], zr.at[k - 1], me.at_quad(me.quad(k)))
        copy.start()
        sends.append(copy)
    r2[me.q] = m2[...]
    for k in range(1, nq):
        src = r2.at[me.quad(nq - k)]
        remote(src, src, zs.at[k - 1], zr.at[k - 1], me.core).wait_recv()
    run = r2[0, 1].astype(F32)
    for k in range(1, nq):
        run = run + r2[k, 1].astype(F32)
    carry = run
    for k in range(nq - 1, -1, -1):
        carry = jnp.where(me.q == k, run, carry)
        run = four * run + r2[k, 0].astype(F32)
    lead = pick(me.pos, [three, two, one, jnp.ones_like(one)])
    for p in range(3):
        s_ref[2 * p] = lead * carry[p] + after[p, 0]
        s_ref[2 * p + 1] = after[p, 1]
    for copy in sends:
        copy.wait_send()


def backward_exchange_call(n, groups, flows, decays, sel):
    nq = n // 4
    dma = pltpu.SemaphoreType.DMA
    return pl.pallas_call(
        functools.partial(backward_exchange, n, groups),
        out_shape=jax.ShapeDtypeStruct((6, 64, 128), F32),
        in_specs=[VMEM, VMEM, SMEM],
        out_specs=VMEM,
        scratch_shapes=[
            pltpu.VMEM((3, 2, 64, 128), BF16), pltpu.VMEM((3, 2, 64, 128), BF16),
            pltpu.VMEM((3, 2, 64, 128), BF16), pltpu.VMEM((3, 2, 64, 128), BF16),
            pltpu.VMEM((2, 3, 64, 128), BF16), pltpu.VMEM((nq, 2, 3, 64, 128), BF16),
            dma((2,)), dma((2,)), dma((nq - 1,)), dma((nq - 1,)),
        ],
        compiler_params=pltpu.CompilerParams(collective_id=2, has_side_effects=True, vmem_limit_bytes=40 << 20),
        name="backward_exchange",
    )(flows, decays, sel)


def tail_flow(me, t, r1, w1, r2, w2, r3, out, send, recv):
    nq = me.nq
    last = me.q == nq - 1
    out[...] = jnp.zeros_like(out)
    copy1 = remote(t.at[:, 1 - me.c], r1, send.at[0], recv.at[0], me.core)
    copy1.start()
    yield
    copy1.wait()
    for i in range(2):
        w1[i] = (t[i, me.c].astype(F32) + r1[i].astype(F32)).astype(BF16)
    copy2 = remote(w1.at[1 - me.y], r2, send.at[1], recv.at[1], me.side)
    copy2.start()
    yield
    copy2.wait()
    w2[...] = (w1[me.y].astype(F32) + r2[...].astype(F32)).astype(BF16)
    top = (me.g, (nq - 1) * 4 + me.pos)
    end = (me.g, nq * 4 - 1)
    for k in range(nq - 1):
        @pl.when(me.q == k)
        def _():
            remote(w2, r3.at[k], send.at[2], recv.at[2 + k], top).start()
    yield

    @pl.when(last)
    def _():
        total = w2[...].astype(F32)
        for k in range(nq - 1):
            remote(r3.at[k], r3.at[k], send.at[2], recv.at[2 + k], me.core).wait_recv()
            total = total + r3[k].astype(F32)
        w2[...] = total.astype(BF16)

        @pl.when(jnp.logical_not(me.is_last))
        def _():
            for j in range(3):
                @pl.when(me.pos == j)
                def _():
                    remote(w2, out.at[j // 2, j % 2], send.at[2], recv.at[nq + 1 + j], end).start()

        @pl.when(me.is_last)
        def _():
            out[1, 1] = w2[...]
    yield

    @pl.when(me.is_last)
    def _():
        for j in range(3):
            dst = out.at[j // 2, j % 2]
            remote(dst, dst, send.at[2], recv.at[nq + 1 + j], me.core).wait_recv()

    @pl.when(jnp.logical_not(me.is_last))
    def _():
        remote(w2, w2, send.at[2], recv.at[2], me.core).wait_send()


def tail_scratch(nq, rows, width):
    return [
        pltpu.VMEM((2, rows, width), BF16), pltpu.VMEM((2, rows, width), BF16),
        pltpu.VMEM((rows, width), BF16), pltpu.VMEM((rows, width), BF16),
        pltpu.VMEM((nq - 1, rows, width), BF16),
    ]


def keys_kernel(n, groups, t, out, r1, w1, r2, w2, r3, send, recv):
    me = Place(n, groups)
    meet(me.group_peers())
    for _ in tail_flow(me, t, r1, w1, r2, w2, r3, out, send, recv):
        pass


def keys_call(n, groups, t):
    nq = n // 4
    dma = pltpu.SemaphoreType.DMA
    return pl.pallas_call(
        functools.partial(keys_kernel, n, groups),
        out_shape=jax.ShapeDtypeStruct(t.shape, BF16),
        in_specs=[VMEM],
        out_specs=VMEM,
        scratch_shapes=tail_scratch(nq, t.shape[2], t.shape[3]) + [dma((3,)), dma((nq + 4,))],
        compiler_params=pltpu.CompilerParams(collective_id=3, has_side_effects=True),
        name="tail_keys",
    )(t)


def sum_flow(me, cross_first, grads, r1, w1, r2, w2, r3, w3, r4, rx, out, send, recv):
    nq = me.nq
    rows, width = out.shape
    wide = width // 2
    ours = pl.ds(pl.multiple_of(me.x * wide, 128), wide)
    others = pl.ds(pl.multiple_of((1 - me.x) * wide, 128), wide)
    copy1 = remote(grads.at[:, :, 1 - me.c], r1, send.at[0], recv.at[0], me.core)
    copy1.start()
    yield
    copy1.wait()

    def add1(i, carry):
        w1[i // 2, i % 2] = (grads[i // 2, i % 2, me.c].astype(F32) + r1[i // 2, i % 2].astype(F32)).astype(BF16)
        return carry

    lax.fori_loop(0, 2 * nq, add1, 0)
    if cross_first:
        copy2 = remote(w1.at[:, :, :, others], r2, send.at[1], recv.at[1], me.cross)
    else:
        copy2 = remote(w1.at[:, 1 - me.y], r2, send.at[1], recv.at[1], me.side)
    copy2.start()
    yield
    copy2.wait()
    if cross_first:
        def add2(i, carry):
            w2[i // 2, i % 2] = (w1[i // 2, i % 2, :, ours].astype(F32) + r2[i // 2, i % 2].astype(F32)).astype(BF16)
            return carry

        lax.fori_loop(0, 2 * nq, add2, 0)
        copy3 = remote(w2.at[:, 1 - me.y], r3, send.at[2], recv.at[2], me.side)
    else:
        def add2(i, carry):
            w2[i] = (w1[i, me.y].astype(F32) + r2[i].astype(F32)).astype(BF16)
            return carry

        lax.fori_loop(0, nq, add2, 0)
        copy3 = remote(w2.at[:, :, others], r3, send.at[2], recv.at[2], me.cross)
    copy3.start()
    yield
    copy3.wait()

    def add3(i, carry):
        kept = w2[i, me.y] if cross_first else w2[i, :, ours]
        w3[i] = (kept.astype(F32) + r3[i].astype(F32)).astype(BF16)
        return carry

    lax.fori_loop(0, nq, add3, 0)
    copies = []
    for k in range(1, nq):
        copy = remote(w3.at[me.quad(k)], r4.at[k - 1], send.at[2 + k], recv.at[2 + k], me.at_quad(me.quad(k)))
        copy.start()
        copies.append(copy)
    yield
    total = w3[me.q].astype(F32)
    for k in range(1, nq):
        copies[k - 1].wait()
        total = total + r4[k - 1].astype(F32)
    out[:, ours] = total.astype(BF16)
    copy5 = remote(out.at[:, ours], out.at[:, ours], send.at[nq + 2], recv.at[nq + 2], me.cross)
    copy5.start()
    yield
    remote(out.at[:, others], out.at[:, others], send.at[nq + 2], recv.at[nq + 2], me.cross).wait_recv()
    copy5.wait_send()
    for at, bit in enumerate(me.cross_bits()[1:]):
        copy = remote(out, rx.at[at], send.at[nq + 3 + at], recv.at[nq + 3 + at], me.cross_bit(bit))
        copy.start()
        copy.wait()
        out[...] = (out[...].astype(F32) + rx[at].astype(F32)).astype(BF16)


def sum_scratch(nq, groups, cross_first, rows, width):
    extra = max(groups.bit_length() - 2, 1)
    half = width // 2
    full = [pltpu.VMEM((nq, 2, rows, width), BF16)] * 2
    if cross_first:
        mid = [pltpu.VMEM((nq, 2, rows, half), BF16)] * 2
    else:
        mid = [pltpu.VMEM((nq, rows, width), BF16)] * 2
    return full + mid + [
        pltpu.VMEM((nq, rows, half), BF16), pltpu.VMEM((nq, rows, half), BF16),
        pltpu.VMEM((nq - 1, rows, half), BF16), pltpu.VMEM((extra, rows, width), BF16),
    ]


def drive(flows):
    live, waiting = [], list(flows)
    while live or waiting:
        if waiting:
            live.append(waiting.pop(0))
        for flow in list(live):
            try:
                next(flow)
            except StopIteration:
                live.remove(flow)


def sums_kernel(n, groups, orders, *refs):
    me = Place(n, groups)
    count = len(orders)
    grads, t = refs[:count], refs[count]
    outs, t_out = refs[count + 1 : 2 * count + 1], refs[2 * count + 1]
    rest = list(refs[2 * count + 2 :])
    send, recv, tsend, trecv = rest[-4:]
    meet(me.group_peers() + [me.cross_bit(bit) for bit in me.cross_bits()])
    flows = []
    for i, order in enumerate(orders):
        scratch = rest[8 * i : 8 * i + 8]
        flows.append(sum_flow(me, order, grads[i], *scratch, outs[i], send.at[i], recv.at[i]))
    flows.append(tail_flow(me, t, *rest[8 * count : 8 * count + 5], t_out, tsend, trecv))
    drive(flows)


def sums_call(n, groups, grads, tail):
    nq = n // 4
    dma = pltpu.SemaphoreType.DMA
    orders = tuple(i % 2 == 0 for i in range(len(grads)))
    scratch = []
    for order, grad in zip(orders, grads):
        scratch += sum_scratch(nq, groups, order, grad.shape[-2], grad.shape[-1])
    scratch += tail_scratch(nq, tail.shape[2], tail.shape[3])
    sems = nq + 3 + max(groups.bit_length() - 2, 1)
    scratch += [dma((len(grads), sems)), dma((len(grads), sems)), dma((3,)), dma((nq + 4,))]
    return pl.pallas_call(
        functools.partial(sums_kernel, n, groups, orders),
        out_shape=[jax.ShapeDtypeStruct(grad.shape[-2:], BF16) for grad in grads] + [jax.ShapeDtypeStruct(tail.shape, BF16)],
        in_specs=[VMEM] * (len(grads) + 1),
        out_specs=[VMEM] * (len(grads) + 1),
        scratch_shapes=scratch,
        compiler_params=pltpu.CompilerParams(collective_id=4, has_side_effects=True, vmem_limit_bytes=56 << 20),
        name="sum_weights",
    )(*grads, tail)


def ema_call(kernel, name, outs, ins, scratch=()):
    return pl.pallas_call(
        kernel,
        out_shape=[jax.ShapeDtypeStruct(shape, F32) for shape in outs],
        in_specs=[VMEM] * len(ins),
        out_specs=[VMEM] * len(outs),
        scratch_shapes=scratch,
        compiler_params=pltpu.CompilerParams(vmem_limit_bytes=56 << 20),
        name=name,
    )(*ins)


def local_pass_call(rows, backward, x, dec):
    def kernel(x_ref, d_ref, inner_ref, final_ref):
        ema_local_pass(rows, x_ref, d_ref.at[0], d_ref.at[1], d_ref.at[2], d_ref.at[3], inner_ref, final_ref, backward)

    return ema_call(kernel, "ema_local", [(rows * 512, 128), (rows * 64, 128)], (x, dec))


def apply_pass_call(rows, x, dec, mix, omega, power, inner, start):
    def kernel(x_ref, d_ref, mix_ref, omega_ref, power_ref, inner_ref, start_ref, y_ref):
        ema_apply_pass(rows, x_ref, d_ref.at[0], mix_ref, omega_ref, power_ref, inner_ref, start_ref, y_ref)

    return ema_call(kernel, "ema_apply", [(rows * 512, 128)], (x, dec, mix, omega, power, inner, start))[0]


def back_pass_call(rows, x_rows, x, g, dec, mix, omega, power, inner, start, power_rev, back_inner, back_start):
    def kernel(x_ref, g_ref, d_ref, mix_ref, omega_ref, power_ref, inner_ref, start_ref, rev_ref, bi_ref, bs_ref, dx_ref, a_ref, b_ref, c_ref, kept):
        for ref in (a_ref, b_ref, c_ref):
            ref[...] = jnp.zeros_like(ref)
        ema_back_pass(
            rows, x_rows, x_ref, g_ref, d_ref.at[0], mix_ref, omega_ref, power_ref, inner_ref, start_ref,
            rev_ref, bi_ref, bs_ref, dx_ref, a_ref, b_ref, c_ref, kept,
        )

    return ema_call(
        kernel, "ema_back", [(rows * 512, 128), (64, 128), (64, 128), (64, 128)],
        (x, g, dec, mix, omega, power, inner, start, power_rev, back_inner, back_start),
        [pltpu.VMEM((128, 8, 128), F32)],
    )


def silu_grad(pre_act):
    sigmoid_val = jax.nn.sigmoid(pre_act)
    return sigmoid_val * (1.0 + pre_act * (1.0 - sigmoid_val))


def norm_rows(row_data):
    centered = row_data - jnp.mean(row_data, axis=-1, keepdims=True)
    scale_inv = lax.rsqrt(jnp.mean(centered * centered, axis=-1, keepdims=True) + NORM_EPS)
    return (centered * scale_inv, scale_inv)


def norm_back(grad_rows, plain, scale_inv, gain_vec):
    grad_norm = grad_rows * gain_vec
    inner_term = (
        grad_norm
        - jnp.mean(grad_norm, axis=-1, keepdims=True)
        - plain * jnp.mean(grad_norm * plain, axis=-1, keepdims=True)
    )
    return inner_term * scale_inv


def nt(lhs, rhs):
    return lax.dot_general(lhs, rhs, (((1,), (1,)), ((), ())), preferred_element_type=F32)


def tn(lhs, rhs):
    return lax.dot_general(lhs, rhs, (((0,), (0,)), ((), ())), preferred_element_type=F32)


def nn(lhs, rhs):
    return lax.dot_general(lhs, rhs, (((1,), (0,)), ((), ())), preferred_element_type=F32)


def silu_pair(pre):
    sig = jax.nn.sigmoid(pre)
    return pre * sig, sig * (1.0 + pre * (1.0 - sig))


CHUNK = 256


def dense_kernel(
    n, tok, tail, ema, cot, mats_a, mats_b, w_shared, vec_wide, vec_head, target,
    result, g_middle, g_act, g_base, slope_s, shared_out, g_units, o_outer, o_inner, o_hidden, o_reset, o_value,
    tail_keys, sum_wide, sum_head,
    w_value, w_reset, w_inner, w_hidden, w_outer, values, slope_v, t_values, t_slope, t_keys, t_dv, t_dk,
    k_units, k_activ, k_gated, k_mid, k_inner, k_branch, k_gin, k_greset, k_gvalue, reset_pre, mixed, slope_i, sem,
):
    sets = t_keys.shape[0]
    length = t_keys.shape[1]
    own = tok.shape[0]
    total = own + tail.shape[0]
    width = tok.shape[1]
    chan = w_value.shape[1]
    rows_b = w_hidden.shape[1]
    hv = w_value.shape[2]
    parts = hv // CHUNK
    scale = 1.0 / math.sqrt(128.0)
    copies = [
        pltpu.make_async_copy(mats_a.at[:, 0:chan], w_value, sem.at[0]),
        pltpu.make_async_copy(mats_a.at[:, chan : 2 * chan], w_reset, sem.at[1]),
        pltpu.make_async_copy(mats_b.at[:, 0:rows_b], w_hidden, sem.at[2]),
        pltpu.make_async_copy(mats_a.at[:, 2 * chan : 3 * chan], w_inner, sem.at[3]),
        pltpu.make_async_copy(mats_b.at[:, rows_b : 2 * rows_b], w_outer, sem.at[4]),
    ]
    for copy in copies:
        copy.start()
    gain_one, gain_two = vec_wide[0:1], vec_wide[1:2]
    q_mul, q_add, k_mul = vec_head[0:1], vec_head[1:2], vec_head[2:3]
    t_dv[...] = jnp.zeros_like(t_dv)
    t_dk[...] = jnp.zeros_like(t_dk)
    sum_wide[...] = jnp.zeros_like(sum_wide)
    sum_head[...] = jnp.zeros_like(sum_head)

    def columns(ref, at):
        block = ref[:, :, at * CHUNK : (at + 1) * CHUNK]
        return block.reshape(block.shape[0] * block.shape[1], CHUNK)

    def rows(ref, at):
        per = CHUNK // rows_b
        return ref[at * per : (at + 1) * per].reshape(CHUNK, ref.shape[2])

    def ema_rows(start, count):
        return jnp.concatenate([ema[pl.ds(lane * total + start, count), :] for lane in range(4)], axis=1)

    copies[0].wait()

    def tail_step(m, carry):
        at = pl.multiple_of(m * length, length)
        here = pl.ds(at, length)
        plain, _ = norm_rows(tail[here, :].astype(F32))
        units = (plain * gain_one).astype(BF16)
        k_units[pl.ds(own + at, length), :] = units
        for part in range(parts):
            value, slope = silu_pair(nn(units, columns(w_value, part)))
            t_values[m, :, part * CHUNK : (part + 1) * CHUNK] = value.astype(BF16)
            t_slope[m, :, part * CHUNK : (part + 1) * CHUNK] = slope.astype(BF16)
        pre = ema_rows(own + at, length)
        activ = (pre * jax.nn.sigmoid(pre)).astype(BF16)
        shared = nn(activ, w_shared[...])
        t_keys[m] = (shared * jax.nn.sigmoid(shared) * k_mul).astype(BF16)
        return carry

    lax.fori_loop(0, sets, tail_step, 0)
    for copy in copies[1:]:
        copy.wait()
    causal = lax.broadcasted_iota(jnp.int32, (length, length), 0) >= lax.broadcasted_iota(jnp.int32, (length, length), 1)

    def set_step(p, carry):
        here = pl.ds(pl.multiple_of(p * 2 * length, 2 * length), 2 * length)
        m = target[p]
        x = tok[here, :].astype(F32)
        plain, _ = norm_rows(x)
        units = (plain * gain_one).astype(BF16)
        k_units[here, :] = units
        for part in range(parts):
            cut = slice(part * CHUNK, (part + 1) * CHUNK)
            value, slope = silu_pair(nn(units, columns(w_value, part)))
            values[:, cut] = value.astype(BF16)
            slope_v[:, cut] = slope.astype(BF16)
        pre = ema_rows(p * 2 * length, 2 * length)
        activ = (pre * jax.nn.sigmoid(pre)).astype(BF16)
        k_activ[here, :] = activ
        shared, slope = silu_pair(nn(activ, w_shared[...]))
        slope_s[here, :] = slope
        shared_out[here, :] = shared
        queries = (shared * q_mul + q_add).astype(BF16)
        keys = (shared * k_mul).astype(BF16)
        for part in range(parts):
            reset_pre[:, part * CHUNK : (part + 1) * CHUNK] = nn(activ, columns(w_reset, part))
        p_q, c_q, p_k, c_k = queries[:length], queries[length:], keys[:length], keys[length:]
        e_k = t_keys[m]

        def weights(scores):
            expo = jnp.exp(scores - jnp.max(scores, axis=-1, keepdims=True))
            return expo * (1.0 / jnp.sum(expo, axis=-1, keepdims=True))

        p_probs = weights(jnp.where(causal, nt(p_q, p_k) * scale, MASKED_SCORE))
        c_probs = weights(
            jnp.concatenate((nt(c_q, e_k) * scale, jnp.where(causal, nt(c_q, c_k) * scale, MASKED_SCORE)), axis=1)
        )
        p_low, c_low = p_probs.astype(BF16), c_probs.astype(BF16)
        for part in range(parts):
            cut = slice(part * CHUNK, (part + 1) * CHUNK)
            mix_p = nn(p_low, values[:length, cut])
            mix_c = nn(c_low, jnp.concatenate((t_values[m, :, cut], values[length:, cut]), axis=0))
            mix = jnp.concatenate((mix_p, mix_c), axis=0)
            mixed[:, cut] = mix
            gate = reset_pre[:, cut]
            k_gated[here, cut] = (gate * jax.nn.sigmoid(gate) * mix).astype(BF16)
        middle = x + nn(k_gated[here, :], w_hidden[...].reshape(-1, width))
        plain_mid, inv_mid = norm_rows(middle)
        mid_low = (plain_mid * gain_two).astype(BF16)
        k_mid[here, :] = mid_low
        for part in range(parts):
            cut = slice(part * CHUNK, (part + 1) * CHUNK)
            inner, slope = silu_pair(nn(mid_low, columns(w_inner, part)))
            k_inner[here, cut] = inner.astype(BF16)
            slope_i[:, cut] = slope
        result[here, :] = (middle + nn(k_inner[here, :], w_outer[...].reshape(-1, width))).astype(BF16)
        top = cot[here, :]
        for part in range(parts):
            cut = slice(part * CHUNK, (part + 1) * CHUNK)
            k_gin[here, cut] = (nt(top, rows(w_outer, part)) * slope_i[:, cut]).astype(BF16)
        back = nt(k_gin[here, :], w_inner[...].reshape(width, -1))
        sum_wide[0:1] += jnp.sum(back * plain_mid, axis=0, keepdims=True)
        g_mid = top.astype(F32) + norm_back(back, plain_mid, inv_mid, gain_two)
        g_middle[here, :] = g_mid
        branch = g_mid.astype(BF16)
        k_branch[here, :] = branch
        dp_p = jnp.zeros((length, length), F32)
        dp_c = jnp.zeros((length, 2 * length), F32)
        for part in range(parts):
            cut = slice(part * CHUNK, (part + 1) * CHUNK)
            gated_back = nt(branch, rows(w_hidden, part))
            gate, slope = silu_pair(reset_pre[:, cut])
            g_mix = (gated_back * gate).astype(BF16)
            k_greset[here, cut] = (gated_back * mixed[:, cut] * slope).astype(BF16)
            dp_p += nt(g_mix[:length], values[:length, cut])
            dp_c += nt(g_mix[length:], jnp.concatenate((t_values[m, :, cut], values[length:, cut]), axis=0))
            dv_p = tn(p_low, g_mix[:length])
            dv_c = tn(c_low, g_mix[length:])
            t_dv[m, :, cut] += dv_c[:length]
            dv = jnp.concatenate((dv_p, dv_c[length:]), axis=0)
            k_gvalue[here, cut] = (dv * slope_v[:, cut].astype(F32)).astype(BF16)
        g_act[here, :] = nt(k_greset[here, :], w_reset[...].reshape(width, -1))

        def score_back(probs, grads):
            return (probs * (grads - jnp.sum(grads * probs, axis=-1, keepdims=True))).astype(BF16)

        p_ds, c_ds = score_back(p_probs, dp_p), score_back(c_probs, dp_c)
        d_q = jnp.concatenate((nn(p_ds, p_k), nn(c_ds, jnp.concatenate((e_k, c_k), axis=0))), axis=0) * scale
        dk_c = tn(c_ds, c_q) * scale
        t_dk[m] += dk_c[:length]
        d_k = jnp.concatenate((tn(p_ds, p_q) * scale, dk_c[length:]), axis=0)
        sum_head[0:1] += jnp.sum(d_q * shared, axis=0, keepdims=True)
        sum_head[1:2] += jnp.sum(d_q, axis=0, keepdims=True)
        sum_head[2:3] += jnp.sum(d_k * shared, axis=0, keepdims=True)
        g_base[here, :] = d_q * q_mul + d_k * k_mul
        return carry

    lax.fori_loop(0, sets, set_step, 0)
    tail_keys[...] = t_dk[...].astype(BF16)

    def tail_back(m, carry):
        at = pl.multiple_of(own + m * length, length)
        k_gvalue[pl.ds(at, length), :] = (t_dv[m] * t_slope[m].astype(F32)).astype(BF16)
        return carry

    lax.fori_loop(0, sets, tail_back, 0)

    def units_step(i, carry):
        here = pl.ds(pl.multiple_of(i * CHUNK, CHUNK), CHUNK)
        g_units[here, :] = nt(k_gvalue[here, :], w_value[...].reshape(width, -1))
        return carry

    lax.fori_loop(0, total // CHUNK, units_step, 0) if total % CHUNK == 0 else None
    if total % CHUNK:
        here = slice(total // CHUNK * CHUNK, total)
        lax.fori_loop(0, total // CHUNK, units_step, 0)
        g_units[here, :] = nt(k_gvalue[here, :], w_value[...].reshape(width, -1))

    def weight_grad(lhs, rhs, out, count):
        per = CHUNK // out.shape[1]

        def step(i, carry):
            block = tn(lhs[0:count, pl.ds(pl.multiple_of(i * CHUNK, CHUNK), CHUNK)], rhs[0:count, :])
            out[pl.ds(i * per, per)] = block.astype(BF16).reshape(per, out.shape[1], out.shape[2])
            return carry

        lax.fori_loop(0, lhs.shape[1] // CHUNK, step, 0)

    weight_grad(k_inner, cot, o_outer, own)
    weight_grad(k_mid, k_gin, o_inner, own)
    weight_grad(k_gated, k_branch, o_hidden, own)
    weight_grad(k_activ, k_greset, o_reset, own)
    weight_grad(k_units, k_gvalue, o_value, total)


def dense_call(n, tok, tail, ema, cot, mats_a, mats_b, w_shared, vec_wide, vec_head, target):
    own, width = tok.shape
    rows_t = tail.shape[0]
    total = own + rows_t
    sets = target.shape[0]
    length = rows_t // sets
    hv = mats_a.shape[2]
    chan = mats_a.shape[1] // 3
    rows_b = mats_b.shape[1] // 2
    shape = jax.ShapeDtypeStruct
    vm = pltpu.VMEM
    outs = [
        shape((own, width), BF16), shape((own, width), F32), shape((own, width), F32), shape((own, 128), F32),
        shape((own, 128), F32), shape((own, 128), F32), shape((total, width), F32),
        shape((n, rows_b, width), BF16), shape((n, chan, hv), BF16), shape((n, rows_b, width), BF16),
        shape((n, chan, hv), BF16), shape((n, chan, hv), BF16),
        shape((sets, length, 128), BF16), shape((8, width), F32), shape((8, 128), F32),
    ]
    scratch = [
        vm((n, chan, hv), BF16), vm((n, chan, hv), BF16), vm((n, chan, hv), BF16),
        vm((n, rows_b, width), BF16), vm((n, rows_b, width), BF16),
        vm((2 * length, hv), BF16), vm((2 * length, hv), BF16),
        vm((sets, length, hv), BF16), vm((sets, length, hv), BF16), vm((sets, length, 128), BF16),
        vm((sets, length, hv), F32), vm((sets, length, 128), F32),
        vm((total, width), BF16), vm((own, width), BF16), vm((own, hv), BF16), vm((own, width), BF16),
        vm((own, hv), BF16), vm((own, width), BF16), vm((own, hv), BF16), vm((own, hv), BF16), vm((total, hv), BF16),
        vm((2 * length, hv), F32), vm((2 * length, hv), F32), vm((2 * length, hv), F32),
        pltpu.SemaphoreType.DMA((5,)),
    ]
    return pl.pallas_call(
        functools.partial(dense_kernel, n),
        out_shape=outs,
        in_specs=[VMEM] * 4 + [ANY] * 2 + [VMEM] * 3 + [SMEM],
        out_specs=[VMEM] * len(outs),
        scratch_shapes=scratch,
        compiler_params=pltpu.CompilerParams(vmem_limit_bytes=60 << 20),
        name="dense",
    )(tok, tail, ema, cot, mats_a, mats_b, w_shared, vec_wide, vec_head, target)


def lanes_first(rows):
    return rows.reshape(-1, 4, 128).transpose(1, 0, 2).reshape(-1, 128)


def rows_first(lanes):
    return lanes.reshape(4, -1, 128).transpose(1, 0, 2).reshape(-1, 512)


def dot(lhs, rhs, dims):
    return lax.dot_general(lhs, rhs, ((dims[:1], dims[1:]), ((), ())), preferred_element_type=F32)


def local(
    hidden_in, cotangent, cont_prompt, value_proj, shared_proj, reset_proj, hidden_proj, inner_proj,
    outer_proj, ema_alpha, ema_delta, ema_beta, ema_eta, ema_omega, norm_gain, ffn_gain, query_scale,
    query_shift, key_scale,
):
    n, groups = lax.axis_size("seq"), lax.axis_size("grp")
    nq = n // 4
    seq_index = lax.axis_index("seq")
    sets, kinds, length, width = hidden_in.shape[1:]
    chan = width // n
    heads = query_scale.shape[0]
    tokens_low = hidden_in[0]
    vectors = jnp.stack((query_scale, query_shift, key_scale), axis=1)
    small = jnp.concatenate(
        (
            ema_alpha, ema_delta, ema_beta, ema_eta, ema_omega[:, None], norm_gain[:, None], ffn_gain[:, None],
            jnp.pad(vectors, ((0, chan - heads), (0, 0))), jnp.zeros((chan, 58), BF16),
        ),
        axis=1,
    )
    small = jnp.concatenate((small, shared_proj), axis=0)
    mat_a = jnp.concatenate((value_proj, reset_proj, inner_proj), axis=0)
    mat_b = jnp.concatenate((hidden_proj, outer_proj), axis=0)
    rows_b = hidden_proj.shape[0]
    all_small, all_a, all_b, tail_low = gather_call(
        n, groups, small, mat_a, mat_b, tokens_low[:, 0].reshape(4, sets * length // 4, width)
    )
    mat_shared = all_small[:, chan:].reshape(width, 128)
    flat = all_small[:, :chan].astype(F32)
    table = flat.reshape(width, 128).T
    vecs = flat[:, :heads, 67:70].reshape(-1, 3)
    query_mul, query_add, key_mul = vecs[:, 0], vecs[:, 1], vecs[:, 2]

    def by_lane(part):
        return part.reshape(16, 4, 128).transpose(1, 0, 2).reshape(64, 128)

    alpha, delta, beta, eta = (by_lane(table[16 * i : 16 * i + 16]) for i in range(4))
    omega, gain_one, gain_two = table[64], table[65], table[66]
    omega_lanes = omega.reshape(4, 128)
    decay = 1.0 - alpha * delta
    decay2 = decay * decay
    decay4 = decay2 * decay2
    decay8 = decay4 * decay4
    decay16 = decay8 * decay8
    decay32 = decay16 * decay16
    decay64 = decay32 * decay32
    decay128 = decay64 * decay64
    decay256 = decay128 * decay128
    dec = jnp.stack((decay, decay16, decay32, decay64))
    far = jnp.stack((decay128, decay256, decay256 * decay128, decay256 * decay256))
    steps = [jnp.ones_like(decay), decay16, decay32, decay32 * decay16, decay64, decay64 * decay16, decay64 * decay32, decay64 * decay32 * decay16]
    power = jnp.stack(steps, axis=1).reshape(512, 128)
    power_rev = jnp.stack(steps[::-1], axis=1).reshape(512, 128)
    ab = alpha * beta
    mix = ab * eta
    targets = lax.dynamic_slice_in_dim(
        cont_prompt[0].reshape(sets, nq), seq_index // 4, 1, 1
    )[:, 0]
    select = (targets[:, None] == jnp.arange(sets, dtype=jnp.int32)[None, :]).astype(F32)
    sel = select.reshape(-1)
    own_rows = sets * kinds * length
    rows_low = jnp.concatenate((tokens_low.reshape(own_rows, width), tail_low.reshape(-1, width)), axis=0)
    tokens = rows_low.astype(F32)
    plain_in, inv_in = norm_rows(tokens)
    normed = plain_in * gain_one
    x_lanes = lanes_first(normed)
    inner, finals = local_pass_call(9, False, x_lanes, dec)
    starts = forward_exchange_call(n, groups, finals[: 6 * 64].reshape(3, 2, 64, 128), ab, far, sel)
    starts = starts.reshape(9 * 64, 128)
    ema_lanes = apply_pass_call(9, x_lanes, dec, mix, omega_lanes, power, inner, starts)
    grad_outer = cotangent[0].reshape(own_rows, width)
    vec_wide = jnp.pad(jnp.stack((gain_one, gain_two)), ((0, 6), (0, 0)))
    vec_head = jnp.pad(jnp.stack((query_mul, query_add, key_mul)), ((0, 5), (0, 0)))
    (
        result, grad_middle, grad_act, grad_base, slope_shared, shared, grad_units, sum_outer, sum_inner, sum_hidden,
        sum_reset, sum_value, sent_keys, sum_wide, sum_head,
    ) = dense_call(
        n, rows_low[:own_rows], rows_low[own_rows:], ema_lanes, grad_outer, all_a, all_b, mat_shared, vec_wide, vec_head, targets
    )
    sum_gain_two = sum_wide[0]
    tail_keys = keys_call(n, groups, sent_keys.reshape(2, 2, sets * length // 4, 128))
    tail_keys = tail_keys.reshape(sets, length, 128).astype(F32)
    zeros = jnp.zeros_like(tail_keys)
    tail_rows = jnp.stack((tail_keys, zeros), axis=1).reshape(own_rows, 128)
    sum_query_mul, sum_query_add = sum_head[0], sum_head[1]
    sum_key_mul = sum_head[2] + jnp.sum(tail_rows * shared, axis=0)
    grad_shared_pre = ((grad_base + tail_rows * key_mul) * slope_shared).astype(BF16)
    ema_own = rows_first(ema_lanes.reshape(4, -1, 128)[:, :own_rows].reshape(-1, 128))
    activ = jax.nn.silu(ema_own).astype(BF16)
    sum_shared = dot(activ, grad_shared_pre, (0, 0))
    grad_act = grad_act + dot(grad_shared_pre, mat_shared, (1, 1))
    grad_ema = grad_act * silu_grad(ema_own)
    g_lanes = lanes_first(grad_ema)
    back_inner, back_flow = local_pass_call(6, True, g_lanes, dec)
    back_start = backward_exchange_call(n, groups, back_flow.reshape(3, 2, 64, 128), far, sel)
    dx_lanes, acc_in, acc_decay, acc_out = back_pass_call(
        6, 9, x_lanes, g_lanes, dec, mix, omega_lanes, power, inner, starts, power_rev, back_inner,
        back_start.reshape(6 * 64, 128),
    )
    grad_units = jnp.concatenate((grad_units[:own_rows] + rows_first(dx_lanes), grad_units[own_rows:]), axis=0)
    sum_gain_one = jnp.sum(grad_units * plain_in, axis=0)
    grad_in = norm_back(grad_units, plain_in, inv_in, gain_one)
    m_sum, q_sum = eta * acc_in, eta * ab * acc_decay
    sum_alpha = beta * m_sum - delta * q_sum
    sum_delta = -alpha * q_sum
    sum_beta = alpha * m_sum
    sum_eta = ab * acc_out
    sum_omega = jnp.sum(grad_ema * normed[:own_rows], axis=0)

    def by_channel(part):
        return part.reshape(4, 16, 128).transpose(1, 0, 2).reshape(16, 512)

    top = jnp.concatenate(
        [by_channel(part) for part in (sum_alpha, sum_delta, sum_beta, sum_eta)]
        + [sum_omega[None], sum_gain_one[None], sum_gain_two[None], jnp.zeros((61, width), F32)],
        axis=0,
    ).T.reshape(n, chan, 128)
    triple = jnp.stack((sum_query_mul, sum_query_add, sum_key_mul), axis=1).reshape(n, heads, 3)
    top = top + jnp.pad(triple, ((0, 0), (0, chan - heads), (67, 58)))
    small_grad = jnp.concatenate((top, sum_shared.reshape(n, chan, 128)), axis=1)
    small_grad = jnp.concatenate((small_grad, jnp.zeros_like(small_grad)), axis=2)

    def shards(grad):
        return grad.reshape(nq, 2, 2, -1, grad.shape[-1])

    grads = [shards(part) for part in (sum_outer, sum_inner, sum_hidden, sum_reset, sum_value)]
    grads.append(small_grad.astype(BF16).reshape(nq, 2, 2, 2 * chan, 256))
    tail_grad = grad_in[own_rows:].astype(BF16).reshape(2, 2, sets * length // 4, width)
    *sums, tail_sum = sums_call(n, groups, grads, tail_grad)
    d_outer, d_inner, d_hidden, d_reset, d_value, d_small = [part.astype(F32) for part in sums]
    add_tail = tail_sum.reshape(sets, length, width).astype(F32)
    input_grad = (grad_middle + grad_in[:own_rows]).reshape(sets, 2, length, width)
    input_grad = jnp.stack((input_grad[:, 0] + add_tail, input_grad[:, 1]), axis=1).astype(BF16)
    return (
        result.reshape(hidden_in.shape), input_grad[None], d_value, d_small[chan:, :128], d_reset, d_hidden, d_inner, d_outer,
        d_small[:chan, 0:16], d_small[:chan, 16:32], d_small[:chan, 32:48], d_small[:chan, 48:64],
        d_small[:chan, 64], d_small[:chan, 65], d_small[:chan, 66],
        d_small[:heads, 67], d_small[:heads, 68], d_small[:heads, 69],
    )


def solution(mesh):
    mat, vec = P("seq", None), P("seq")
    tok = P("grp", None, None, "seq", None)
    in_specs = (tok, tok, P("grp", None)) + (mat,) * 10 + (vec,) * 6
    out_specs = (tok, tok) + (mat,) * 10 + (vec,) * 6
    return jax.shard_map(local, mesh=mesh, in_specs=in_specs, out_specs=out_specs, check_vma=False)
```

profile of v0, /device:TPU:0, one launch (start us, length us, event | category | flops | bytes accessed | tf_op | source)
XLA Modules:
  0.0 325.2 jit_solution(16569355263512089516)
XLA Ops:
  1.2 1.3 reduce.29
  2.9 1.8 slice.152
  4.7 1.7 pad_maximum_fusion.3.a_in
  6.4 1.5 pad_maximum_fusion.4.b_in
  15.7 1.3 pad_maximum_fusion.7.s_in
  17.0 49.2 %gather_weights.1 = (bf16[16,64,128]{2,1,0:T(8,128)(2,1)}, bf16[16,96,1024]{2,1,0:T(8,128)(2,1)}, bf16[16,128,512]{2,1,0:T(8,128)(2,1)}, bf16[4,96,512]{2,1,0:T(8,128)(2,1)}) custom-call(bf16[64,128]{1,0:T(8,128)(2,1)} %pad_maximum_fusion.7.s_in, bf16[96,1024]{1,0:T(8,128)(2,1)} %pad_maximum_fusion.3.a_in, bf16[128,512]{1,0:T(8,128)(2,1)} %pad_maximum_fusion.4.b_in, ...), custom_call_target="tpu_custom_call" | custom-call | tf_op jit(solution)/shard_map/gather_weights/pallas_call | solution.py:309
  66.2 1.7 fusion.43
  70.8 1.8 multiply_multiply_fusion
  72.6 7.9 %ema_local.2 = (f32[4608,128]{1,0:T(8,128)}, f32[576,128]{1,0:T(8,128)}) custom-call(f32[4608,128]{1,0:T(8,128)} %bitcast.226, f32[4,64,128]{2,1,0:T(8,128)} %get-tuple-element.265.d_ref), custom_call_target="tpu_custom_call" | custom-call | tf_op jit(solution)/shard_map/ema_local/pallas_call | solution.py:716
  80.5 0.9 slice.123
  82.1 18.6 %forward_exchange.1 = f32[9,64,128]{2,1,0:T(8,128)S(1)} custom-call(f32[3,2,64,128]{3,2,1,0:T(8,128)S(1)} %bitcast.223, f32[64,128]{1,0:T(8,128)S(1)} %get-tuple-element.227.ab_ref, f32[4,64,128]{2,1,0:T(8,128)S(1)} %get-tuple-element.266.d_ref, f32[9]{0:T(128)S(1)} %reshape.564.sel_ref), custom_call_target="tpu_custom_call" | custom-call | tf_op jit(solution)/shard_map/forward_exchange/pallas_call | solution.py:412
  102.5 10.0 %ema_apply.1.ema = f32[4608,128]{1,0:T(8,128)} custom-call(f32[4608,128]{1,0:T(8,128)} %bitcast.227, f32[4,64,128]{2,1,0:T(8,128)} %get-tuple-element.265.d_ref, f32[64,128]{1,0:T(8,128)} %get-tuple-element.226.mix_ref, f32[4,128]{1,0:T(4,128)} %bitcast.301, f32[512,128]{1,0:T(8,128)} %bitcast.260, f32[4608,128]{1,0:T(8,128)} %get-tuple-element.54.inner_ref, ...), custom_call_target="tpu_custom_call" | custom-call | tf_op jit(solution)/shard_map/ema_apply/pallas_call | solution.py:716
  114.2 35.0 %dense.1 = (bf16[768,512]{1,0:T(8,128)(2,1)}, f32[768,512]{1,0:T(8,128)}, f32[768,512]{1,0:T(8,128)}, f32[768,128]{1,0:T(8,128)}, f32[768,128]{1,0:T(8,128)}, /*...) custom-call(bf16[768,512]{1,0:T(8,128)(2,1)} %bitcast.230, ...), custom_call_target="tpu_custom_call" | custom-call | tf_op jit(solution)/shard_map/dense/pallas_call | solution.py:1025
  149.2 9.3 %tail_keys.1 = bf16[2,2,96,128]{3,2,1,0:T(8,128)(2,1)} custom-call(bf16[2,2,96,128]{3,2,1,0:T(8,128)(2,1)} %bitcast.296), custom_call_target="tpu_custom_call" | custom-call | tf_op jit(solution)/shard_map/tail_keys/pallas_call | solution.py:571
  159.4 1.4 fusion.26
  162.1 1.0 copy.370
  164.2 1.3 copy_bitcast_fusion
  165.5 5.8 %ema_local.3 = (f32[3072,128]{1,0:T(8,128)}, f32[384,128]{1,0:T(8,128)}) custom-call(f32[3072,128]{1,0:T(8,128)} %bitcast.236, f32[4,64,128]{2,1,0:T(8,128)} %get-tuple-element.265.d_ref), custom_call_target="tpu_custom_call" | custom-call | tf_op jit(solution)/shard_map/ema_local/pallas_call | solution.py:716
  172.2 20.1 %backward_exchange.1 = f32[6,64,128]{2,1,0:T(8,128)S(1)} custom-call(f32[3,2,64,128]{3,2,1,0:T(8,128)S(1)} %bitcast.225, f32[4,64,128]{2,1,0:T(8,128)S(1)} %get-tuple-element.266.d_ref, f32[9]{0:T(128)S(1)} %reshape.564.sel_ref), custom_call_target="tpu_custom_call" | custom-call | tf_op jit(solution)/shard_map/backward_exchange/pallas_call | solution.py:483
  193.9 16.8 %ema_back.1 = (f32[3072,128]{1,0:T(8,128)}, f32[64,128]{1,0:T(8,128)}, f32[64,128]{1,0:T(8,128)}, f32[64,128]{1,0:T(8,128)}) custom-call(f32[4608,128]{1,0:T(8,128)} %bitcast.228, f32[3072,128]{1,0:T(8,128)} %bitcast.237, f32[4,64,128]{2,1,0:T(8,128)} %get-tuple-element.265.d_ref, f32[64,128]{1,0:T(8,128)} %get-tuple-element.226.mix_ref, ...), custom_call_target="tpu_custom_call" | custom-call | tf_op jit(solution)/shard_map/ema_back/pallas_call | solution.py:716
  210.7 1.7 bitcast_add_fusion
  212.5 1.2 multiply_reduce_fusion
  221.1 1.9 concatenate.53
  223.1 2.9 copy.354
  226.2 2.8 fusion.4
  229.0 2.5 copy.356
  231.6 2.8 fusion.19
  234.3 2.3 copy.355
  236.7 1.6 convolution_convert_fusion
  239.1 2.2 subtract_multiply_fusion
  242.1 72.8 %sum_weights.1 = (bf16[64,512]{1,0:T(8,128)(2,1)}, bf16[32,1024]{1,0:T(8,128)(2,1)}, bf16[64,512]{1,0:T(8,128)(2,1)}, bf16[32,1024]{1,0:T(8,128)(2,1)}, bf16[32,...) custom-call(bf16[4,2,2,64,512]{4,3,2,1,0:T(8,128)(2,1)} %bitcast.273, ...), custom_call_target="tpu_custom_call" | custom-call | tf_op jit(solution)/shard_map/sum_weights/pallas_call | solution.py:704
  316.1 0.9 pad_maximum_fusion.2
  (165 shorter events, 40.0 us)
Async XLA Ops:
  2.8 65.4 %copy-start.26 = (s32[3]{0:T(128)}, s32[3]{0:T(128)S(1)}, u32[]{:S(2)}) copy-start(s32[3]{0:T(128)S(1)} %dynamic-slice_reduce_fusion.target) | copy-start | bytes 40
  4.7 64.1 %copy-start.3 = (bf16[1,3,2,128,512]{4,3,2,1,0:T(8,128)(2,1)S(1)}, bf16[1,3,2,128,512]{4,3,2,1,0:T(8,128)(2,1)}, u32[]{:S(2)}) copy-start(bf16[1,3,2,128,512]{4,3,2,1,0:T(8,128)(2,1)} %param.19) | copy-start | bytes 2359300
  66.2 2.6 copy-start.6
  100.7 0.7 copy-start
  149.1 12.8 %copy-start.5 = (f32[4608,128]{1,0:T(8,128)S(1)}, f32[4608,128]{1,0:T(8,128)}, u32[]{:S(2)}) copy-start(f32[4608,128]{1,0:T(8,128)} %ema_apply.1.ema) | copy-start | bytes 7077892
  160.8 2.3 copy-start.13
  162.1 1.1 copy-start.15
  162.1 1.5 copy-start.27
  163.1 1.1 copy-start.10
  171.3 0.9 copy-start.2
  192.3 0.7 copy-start.1
  193.9 16.8 %copy-start.11 = (f32[1152,512]{1,0:T(8,128)S(1)}, f32[1152,512]{1,0:T(8,128)}, u32[]{:S(2)}) copy-start(f32[1152,512]{1,0:T(8,128)} %get-tuple-element.60) | copy-start | bytes 7077892
  210.6 1.8 copy-start.4
  210.7 1.8 copy-start.7
  212.4 1.3 copy-start.8
  213.7 0.8 copy-start.23
  213.7 0.8 copy-start.24
  213.7 0.8 copy-start.25
  231.6 5.1 %copy-start.14 = (bf16[768,128]{1,0:T(8,128)(2,1)S(1)}, bf16[768,128]{1,0:T(8,128)(2,1)}, u32[]{:S(2)}) copy-start(bf16[768,128]{1,0:T(8,128)(2,1)} %copy-done.13) | copy-start | bytes 589828
  236.6 2.5 copy-start.9
  242.1 72.8 %copy-start.12 = (f32[768,512]{1,0:T(8,128)S(1)}, f32[768,512]{1,0:T(8,128)}, u32[]{:S(2)}) copy-start(f32[768,512]{1,0:T(8,128)} %get-tuple-element.59) | copy-start | bytes 4718596
  314.9 1.0 copy-start.17
  315.2 1.8 copy-start.22
  315.2 2.5 copy-start.21
  315.9 2.5 copy-start.20
  315.9 3.2 copy-start.19
  315.9 3.8 %copy-start.18 = (bf16[64,512]{1,0:T(8,128)(2,1)S(1)}, bf16[64,512]{1,0:T(8,128)(2,1)}, u32[]{:S(2)}) copy-start(bf16[64,512]{1,0:T(8,128)(2,1)} %get-tuple-element.85) | copy-start | bytes 196612
  315.9 4.5 %copy-start.16 = (bf16[64,256]{1,0:T(8,128)(2,1)S(1)}, bf16[64,256]{1,0:T(8,128)(2,1)}, u32[]{:S(2)}) copy-start(bf16[64,256]{1,0:T(8,128)(2,1)} %get-tuple-element.81) | copy-start | bytes 98308
where the time goes:
time: 326 us; the launch traced here: 325 us
  Pallas kernels  245 us (75%)
  local copies, waits for them, and re-layouts  44.7 us (14%)
  other arithmetic  31.5 us (10%)
    pallas_call x1, Pallas kernels, sums_call(): pl.pallas_call(functools.partial(sums_kernel, n, groups, orders), out_sha...  72.8 us
    pallas_call x1, Pallas kernels, gather_call(): pl.pallas_call(functools.partial(gather_kernel, n, groups), out_shape=[ja...  49.2 us
    pallas_call x4, Pallas kernels, ema_call(): pl.pallas_call(kernel, out_shape=[jax.ShapeDtypeStruct(shape, F32) for sh...  40.5 us
    pallas_call x1, Pallas kernels, dense_call(): pl.pallas_call(functools.partial(dense_kernel, n), out_shape=outs, in_spe...  35 us
    pallas_call x1, Pallas kernels, backward_exchange_call(): pl.pallas_call(functools.partial(backward_exchange, n, groups), out_shape...  20.1 us
    pallas_call x1, Pallas kernels, forward_exchange_call(): pl.pallas_call(functools.partial(forward_exchange, n, groups), out_shape=...  18.6 us
    unnamed x70, local copies, waits for them, and re-layouts  11.1 us
    pallas_call x1, Pallas kernels, keys_call(): pl.pallas_call(functools.partial(keys_kernel, n, groups), out_shape=jax.S...  9.29 us

commit v1 on v0

--- a/solution.py
+++ b/solution.py
@@ -36,11 +36,14 @@
     return jnp.broadcast_to(ref[pl.ds(row, 1), :], (8, 128))
 
 
-def ema_local_pass(rows, x_ref, decay, decay16, decay32, decay64, inner_ref, final_ref, backward):
+def ema_local_pass(rows, pick_rows, x_ref, decay, decay16, decay32, decay64, inner_ref, final_ref, backward):
     shift = shift_up if backward else shift_down
 
-    def body(item, carry):
-        row, lane = item // 4, item % 4
+    first, stride, many = pick_rows
+
+    def body(turn, carry):
+        row, lane = first + stride * (turn // 4), turn % 4
+        item = row * 4 + lane
         base = lane * (rows * 128) + row * 128
         dec = [row_of(decay, lane * 16 + j) for j in range(NJ)]
         state = [jnp.zeros((8, 128), F32)] * NJ
@@ -59,7 +62,7 @@
             final_ref[pl.ds(row * 64 + lane * 16 + j, 1), :] = total[0:1] if backward else total[7:8]
         return carry
 
-    lax.fori_loop(0, rows * 4, body, 0)
+    lax.fori_loop(0, many * 4, body, 0)
 
 
 def ema_apply_pass(rows, x_ref, decay, mix, omega, power, inner_ref, start_ref, y_ref):
@@ -86,16 +89,16 @@
 
 
 def ema_back_pass(
-    rows, x_rows, x_ref, g_ref, decay, mix, omega, power, inner_ref, start_ref, power_rev,
+    rows, x_rows, row, x_ref, g_ref, decay, mix, omega, power, inner_ref, start_ref, power_rev,
     back_inner_ref, back_start_ref, dx_ref, sum_in, sum_decay, sum_out, kept,
 ):
     half = 8
 
-    def body(item, carry):
-        row, lane = item // 4, item % 4
+    def body(lane, carry):
+        item = row * 4 + lane
         base = lane * (rows * 128) + row * 128
         x_base = lane * (x_rows * 128) + row * 128
-        skip = row_of(omega, lane)
+        skip = row_of(omega, 4 + lane)
         for part in range(NJ // half):
             js = range(part * half, part * half + half)
             dec = [row_of(decay, lane * 16 + j) for j in js]
@@ -140,7 +143,7 @@
                 sum_out[at, :] += total + jnp.sum(flow, axis=0, keepdims=True)
         return carry
 
-    lax.fori_loop(0, rows * 4, body, 0)
+    lax.fori_loop(0, 4, body, 0)
 
 
 class Place:
@@ -425,77 +428,6 @@
     )(finals, ab, decays, sel)
 
 
-def backward_exchange(n, groups, f_ref, d_ref, sel_ref, s_ref, m0, r0, m1, r1, m2, r2, ss, rs, zs, zr):
-    me = Place(n, groups)
-    nq = me.nq
-    meet(me.group_peers())
-    one, two, three, four = d_ref[0], d_ref[1], d_ref[2], d_ref[3]
-    m0[...] = f_ref[...].astype(BF16)
-    copy = remote(m0, r0, ss.at[0], rs.at[0], me.core)
-    copy.start()
-    copy.wait()
-    upper_core, upper_side = me.c == 1, me.y == 1
-    mine = f_ref[...]
-    other = r0[...].astype(F32)
-    lower = jnp.where(upper_core, other, mine)
-    upper = jnp.where(upper_core, mine, other)
-    pair = lower + one * upper
-    after = jnp.where(upper_core, 0.0, other)
-    m1[...] = pair.astype(BF16)
-    copy = remote(m1, r1, ss.at[1], rs.at[1], me.side)
-    copy.start()
-    copy.wait()
-    far = r1[...].astype(F32)
-    low_pair = jnp.where(upper_side, far, pair)
-    high_pair = jnp.where(upper_side, pair, far)
-    total = low_pair + two * high_pair
-    after = jnp.where(upper_side, 0.0, jnp.where(upper_core, far, one * far)) + after
-    m2[0] = total[:, 0].astype(BF16)
-    for m in range(3):
-        m2[1, m] = (sel_ref[m] * total[0, 1] + sel_ref[3 + m] * total[1, 1] + sel_ref[6 + m] * total[2, 1]).astype(BF16)
-    sends = []
-    for k in range(1, nq):
-        copy = remote(m2, r2.at[me.q], zs.at[k - 1], zr.at[k - 1], me.at_quad(me.quad(k)))
-        copy.start()
-        sends.append(copy)
-    r2[me.q] = m2[...]
-    for k in range(1, nq):
-        src = r2.at[me.quad(nq - k)]
-        remote(src, src, zs.at[k - 1], zr.at[k - 1], me.core).wait_recv()
-    run = r2[0, 1].astype(F32)
-    for k in range(1, nq):
-        run = run + r2[k, 1].astype(F32)
-    carry = run
-    for k in range(nq - 1, -1, -1):
-        carry = jnp.where(me.q == k, run, carry)
-        run = four * run + r2[k, 0].astype(F32)
-    lead = pick(me.pos, [three, two, one, jnp.ones_like(one)])
-    for p in range(3):
-        s_ref[2 * p] = lead * carry[p] + after[p, 0]
-        s_ref[2 * p + 1] = after[p, 1]
-    for copy in sends:
-        copy.wait_send()
-
-
-def backward_exchange_call(n, groups, flows, decays, sel):
-    nq = n // 4
-    dma = pltpu.SemaphoreType.DMA
-    return pl.pallas_call(
-        functools.partial(backward_exchange, n, groups),
-        out_shape=jax.ShapeDtypeStruct((6, 64, 128), F32),
-        in_specs=[VMEM, VMEM, SMEM],
-        out_specs=VMEM,
-        scratch_shapes=[
-            pltpu.VMEM((3, 2, 64, 128), BF16), pltpu.VMEM((3, 2, 64, 128), BF16),
-            pltpu.VMEM((3, 2, 64, 128), BF16), pltpu.VMEM((3, 2, 64, 128), BF16),
-            pltpu.VMEM((2, 3, 64, 128), BF16), pltpu.VMEM((nq, 2, 3, 64, 128), BF16),
-            dma((2,)), dma((2,)), dma((nq - 1,)), dma((nq - 1,)),
-        ],
-        compiler_params=pltpu.CompilerParams(collective_id=2, has_side_effects=True, vmem_limit_bytes=40 << 20),
-        name="backward_exchange",
-    )(flows, decays, sel)
-
-
 def tail_flow(me, t, r1, w1, r2, w2, r3, out, send, recv):
     nq = me.nq
     last = me.q == nq - 1
@@ -558,160 +490,6 @@
     ]
 
 
-def keys_kernel(n, groups, t, out, r1, w1, r2, w2, r3, send, recv):
-    me = Place(n, groups)
-    meet(me.group_peers())
-    for _ in tail_flow(me, t, r1, w1, r2, w2, r3, out, send, recv):
-        pass
-
-
-def keys_call(n, groups, t):
-    nq = n // 4
-    dma = pltpu.SemaphoreType.DMA
-    return pl.pallas_call(
-        functools.partial(keys_kernel, n, groups),
-        out_shape=jax.ShapeDtypeStruct(t.shape, BF16),
-        in_specs=[VMEM],
-        out_specs=VMEM,
-        scratch_shapes=tail_scratch(nq, t.shape[2], t.shape[3]) + [dma((3,)), dma((nq + 4,))],
-        compiler_params=pltpu.CompilerParams(collective_id=3, has_side_effects=True),
-        name="tail_keys",
-    )(t)
-
-
-def sum_flow(me, cross_first, grads, r1, w1, r2, w2, r3, w3, r4, rx, out, send, recv):
-    nq = me.nq
-    rows, width = out.shape
-    wide = width // 2
-    ours = pl.ds(pl.multiple_of(me.x * wide, 128), wide)
-    others = pl.ds(pl.multiple_of((1 - me.x) * wide, 128), wide)
-    copy1 = remote(grads.at[:, :, 1 - me.c], r1, send.at[0], recv.at[0], me.core)
-    copy1.start()
-    yield
-    copy1.wait()
-
-    def add1(i, carry):
-        w1[i // 2, i % 2] = (grads[i // 2, i % 2, me.c].astype(F32) + r1[i // 2, i % 2].astype(F32)).astype(BF16)
-        return carry
-
-    lax.fori_loop(0, 2 * nq, add1, 0)
-    if cross_first:
-        copy2 = remote(w1.at[:, :, :, others], r2, send.at[1], recv.at[1], me.cross)
-    else:
-        copy2 = remote(w1.at[:, 1 - me.y], r2, send.at[1], recv.at[1], me.side)
-    copy2.start()
-    yield
-    copy2.wait()
-    if cross_first:
-        def add2(i, carry):
-            w2[i // 2, i % 2] = (w1[i // 2, i % 2, :, ours].astype(F32) + r2[i // 2, i % 2].astype(F32)).astype(BF16)
-            return carry
-
-        lax.fori_loop(0, 2 * nq, add2, 0)
-        copy3 = remote(w2.at[:, 1 - me.y], r3, send.at[2], recv.at[2], me.side)
-    else:
-        def add2(i, carry):
-            w2[i] = (w1[i, me.y].astype(F32) + r2[i].astype(F32)).astype(BF16)
-            return carry
-
-        lax.fori_loop(0, nq, add2, 0)
-        copy3 = remote(w2.at[:, :, others], r3, send.at[2], recv.at[2], me.cross)
-    copy3.start()
-    yield
-    copy3.wait()
-
-    def add3(i, carry):
-        kept = w2[i, me.y] if cross_first else w2[i, :, ours]
-        w3[i] = (kept.astype(F32) + r3[i].astype(F32)).astype(BF16)
-        return carry
-
-    lax.fori_loop(0, nq, add3, 0)
-    copies = []
-    for k in range(1, nq):
-        copy = remote(w3.at[me.quad(k)], r4.at[k - 1], send.at[2 + k], recv.at[2 + k], me.at_quad(me.quad(k)))
-        copy.start()
-        copies.append(copy)
-    yield
-    total = w3[me.q].astype(F32)
-    for k in range(1, nq):
-        copies[k - 1].wait()
-        total = total + r4[k - 1].astype(F32)
-    out[:, ours] = total.astype(BF16)
-    copy5 = remote(out.at[:, ours], out.at[:, ours], send.at[nq + 2], recv.at[nq + 2], me.cross)
-    copy5.start()
-    yield
-    remote(out.at[:, others], out.at[:, others], send.at[nq + 2], recv.at[nq + 2], me.cross).wait_recv()
-    copy5.wait_send()
-    for at, bit in enumerate(me.cross_bits()[1:]):
-        copy = remote(out, rx.at[at], send.at[nq + 3 + at], recv.at[nq + 3 + at], me.cross_bit(bit))
-        copy.start()
-        copy.wait()
-        out[...] = (out[...].astype(F32) + rx[at].astype(F32)).astype(BF16)
-
-
-def sum_scratch(nq, groups, cross_first, rows, width):
-    extra = max(groups.bit_length() - 2, 1)
-    half = width // 2
-    full = [pltpu.VMEM((nq, 2, rows, width), BF16)] * 2
-    if cross_first:
-        mid = [pltpu.VMEM((nq, 2, rows, half), BF16)] * 2
-    else:
-        mid = [pltpu.VMEM((nq, rows, width), BF16)] * 2
-    return full + mid + [
-        pltpu.VMEM((nq, rows, half), BF16), pltpu.VMEM((nq, rows, half), BF16),
-        pltpu.VMEM((nq - 1, rows, half), BF16), pltpu.VMEM((extra, rows, width), BF16),
-    ]
-
-
-def drive(flows):
-    live, waiting = [], list(flows)
-    while live or waiting:
-        if waiting:
-            live.append(waiting.pop(0))
-        for flow in list(live):
-            try:
-                next(flow)
-            except StopIteration:
-                live.remove(flow)
-
-
-def sums_kernel(n, groups, orders, *refs):
-    me = Place(n, groups)
-    count = len(orders)
-    grads, t = refs[:count], refs[count]
-    outs, t_out = refs[count + 1 : 2 * count + 1], refs[2 * count + 1]
-    rest = list(refs[2 * count + 2 :])
-    send, recv, tsend, trecv = rest[-4:]
-    meet(me.group_peers() + [me.cross_bit(bit) for bit in me.cross_bits()])
-    flows = []
-    for i, order in enumerate(orders):
-        scratch = rest[8 * i : 8 * i + 8]
-        flows.append(sum_flow(me, order, grads[i], *scratch, outs[i], send.at[i], recv.at[i]))
-    flows.append(tail_flow(me, t, *rest[8 * count : 8 * count + 5], t_out, tsend, trecv))
-    drive(flows)
-
-
-def sums_call(n, groups, grads, tail):
-    nq = n // 4
-    dma = pltpu.SemaphoreType.DMA
-    orders = tuple(i % 2 == 0 for i in range(len(grads)))
-    scratch = []
-    for order, grad in zip(orders, grads):
-        scratch += sum_scratch(nq, groups, order, grad.shape[-2], grad.shape[-1])
-    scratch += tail_scratch(nq, tail.shape[2], tail.shape[3])
-    sems = nq + 3 + max(groups.bit_length() - 2, 1)
-    scratch += [dma((len(grads), sems)), dma((len(grads), sems)), dma((3,)), dma((nq + 4,))]
-    return pl.pallas_call(
-        functools.partial(sums_kernel, n, groups, orders),
-        out_shape=[jax.ShapeDtypeStruct(grad.shape[-2:], BF16) for grad in grads] + [jax.ShapeDtypeStruct(tail.shape, BF16)],
-        in_specs=[VMEM] * (len(grads) + 1),
-        out_specs=[VMEM] * (len(grads) + 1),
-        scratch_shapes=scratch,
-        compiler_params=pltpu.CompilerParams(collective_id=4, has_side_effects=True, vmem_limit_bytes=56 << 20),
-        name="sum_weights",
-    )(*grads, tail)
-
-
 def ema_call(kernel, name, outs, ins, scratch=()):
     return pl.pallas_call(
         kernel,
@@ -726,7 +504,7 @@
 
 def local_pass_call(rows, backward, x, dec):
     def kernel(x_ref, d_ref, inner_ref, final_ref):
-        ema_local_pass(rows, x_ref, d_ref.at[0], d_ref.at[1], d_ref.at[2], d_ref.at[3], inner_ref, final_ref, backward)
+        ema_local_pass(rows, (0, 1, rows), x_ref, d_ref.at[0], d_ref.at[1], d_ref.at[2], d_ref.at[3], inner_ref, final_ref, backward)
 
     return ema_call(kernel, "ema_local", [(rows * 512, 128), (rows * 64, 128)], (x, dec))
 
@@ -736,22 +514,6 @@
         ema_apply_pass(rows, x_ref, d_ref.at[0], mix_ref, omega_ref, power_ref, inner_ref, start_ref, y_ref)
 
     return ema_call(kernel, "ema_apply", [(rows * 512, 128)], (x, dec, mix, omega, power, inner, start))[0]
-
-
-def back_pass_call(rows, x_rows, x, g, dec, mix, omega, power, inner, start, power_rev, back_inner, back_start):
-    def kernel(x_ref, g_ref, d_ref, mix_ref, omega_ref, power_ref, inner_ref, start_ref, rev_ref, bi_ref, bs_ref, dx_ref, a_ref, b_ref, c_ref, kept):
-        for ref in (a_ref, b_ref, c_ref):
-            ref[...] = jnp.zeros_like(ref)
-        ema_back_pass(
-            rows, x_rows, x_ref, g_ref, d_ref.at[0], mix_ref, omega_ref, power_ref, inner_ref, start_ref,
-            rev_ref, bi_ref, bs_ref, dx_ref, a_ref, b_ref, c_ref, kept,
-        )
-
-    return ema_call(
-        kernel, "ema_back", [(rows * 512, 128), (64, 128), (64, 128), (64, 128)],
-        (x, g, dec, mix, omega, power, inner, start, power_rev, back_inner, back_start),
-        [pltpu.VMEM((128, 8, 128), F32)],
-    )
 
 
 def silu_grad(pre_act):
@@ -1033,6 +795,443 @@
     )(tok, tail, ema, cot, mats_a, mats_b, w_shared, vec_wide, vec_head, target)
 
 
+def big_flow(me, cross_first, grads, r1, w1, r2, w2, r3, w3, r4, rx, out, send, recv, local_sem):
+    nq = me.nq
+    rows, width = out.shape
+    wide = width // 2
+    ours = pl.ds(pl.multiple_of(me.x * wide, 128), wide)
+    others = pl.ds(pl.multiple_of((1 - me.x) * wide, 128), wide)
+    copy1 = remote(grads.at[:, :, 1 - me.c], r1, send.at[0], recv.at[0], me.core)
+    copy1.start()
+    kept = pltpu.make_async_copy(grads.at[:, :, me.c], w1, local_sem)
+    kept.start()
+    yield
+    kept.wait()
+    copy1.wait()
+
+    def add1(i, carry):
+        w1[i // 2, i % 2] = (w1[i // 2, i % 2].astype(F32) + r1[i // 2, i % 2].astype(F32)).astype(BF16)
+        return carry
+
+    lax.fori_loop(0, 2 * nq, add1, 0)
+    if cross_first:
+        copy2 = remote(w1.at[:, :, :, others], r2, send.at[1], recv.at[1], me.cross)
+    else:
+        copy2 = remote(w1.at[:, 1 - me.y], r2, send.at[1], recv.at[1], me.side)
+    copy2.start()
+    yield
+    copy2.wait()
+    if cross_first:
+        def add2(i, carry):
+            w2[i // 2, i % 2] = (w1[i // 2, i % 2, :, ours].astype(F32) + r2[i // 2, i % 2].astype(F32)).astype(BF16)
+            return carry
+
+        lax.fori_loop(0, 2 * nq, add2, 0)
+        copy3 = remote(w2.at[:, 1 - me.y], r3, send.at[2], recv.at[2], me.side)
+    else:
+        def add2(i, carry):
+            w2[i] = (w1[i, me.y].astype(F32) + r2[i].astype(F32)).astype(BF16)
+            return carry
+
+        lax.fori_loop(0, nq, add2, 0)
+        copy3 = remote(w2.at[:, :, others], r3, send.at[2], recv.at[2], me.cross)
+    copy3.start()
+    yield
+    copy3.wait()
+
+    def add3(i, carry):
+        mine = w2[i, me.y] if cross_first else w2[i, :, ours]
+        w3[i] = (mine.astype(F32) + r3[i].astype(F32)).astype(BF16)
+        return carry
+
+    lax.fori_loop(0, nq, add3, 0)
+    copies = []
+    for k in range(1, nq):
+        copy = remote(w3.at[me.quad(k)], r4.at[k - 1], send.at[2 + k], recv.at[2 + k], me.at_quad(me.quad(k)))
+        copy.start()
+        copies.append(copy)
+    yield
+    total = w3[me.q].astype(F32)
+    for k in range(1, nq):
+        copies[k - 1].wait()
+        total = total + r4[k - 1].astype(F32)
+    out[:, ours] = total.astype(BF16)
+    copy5 = remote(out.at[:, ours], out.at[:, ours], send.at[nq + 2], recv.at[nq + 2], me.cross)
+    copy5.start()
+    yield
+    remote(out.at[:, others], out.at[:, others], send.at[nq + 2], recv.at[nq + 2], me.cross).wait_recv()
+    copy5.wait_send()
+    for at, bit in enumerate(me.cross_bits()[1:]):
+        copy = remote(out, rx.at[at], send.at[nq + 3 + at], recv.at[nq + 3 + at], me.cross_bit(bit))
+        copy.start()
+        copy.wait()
+        out[...] = (out[...].astype(F32) + rx[at].astype(F32)).astype(BF16)
+
+
+def big_scratch(nq, groups, cross_first, rows, width):
+    extra = max(groups.bit_length() - 2, 1)
+    half = width // 2
+    full = [pltpu.VMEM((nq, 2, rows, width), BF16)] * 2
+    if cross_first:
+        mid = [pltpu.VMEM((nq, 2, rows, half), BF16)] * 2
+    else:
+        mid = [pltpu.VMEM((nq, rows, width), BF16)] * 2
+    return full + mid + [
+        pltpu.VMEM((nq, rows, half), BF16), pltpu.VMEM((nq, rows, half), BF16),
+        pltpu.VMEM((nq - 1, rows, half), BF16), pltpu.VMEM((extra, rows, width), BF16),
+    ]
+
+
+def small_flow(me, grads, r1, w1, r2, w2, rx, out, send, recv):
+    many = 2 * me.nq
+    copy1 = remote(grads.at[:, 1 - me.c], r1, send.at[0], recv.at[0], me.core)
+    copy1.start()
+    yield
+    copy1.wait()
+
+    def add(i, carry):
+        w1[i] = (grads[i, me.c].astype(F32) + r1[i].astype(F32)).astype(BF16)
+        return carry
+
+    lax.fori_loop(0, many, add, 0)
+    mine = me.q * 2 + me.y
+    copies = []
+    for k in range(1, many):
+        to = (mine + k) % many
+        copy = remote(w1.at[to], r2.at[k - 1], send.at[k], recv.at[k], (me.g, to * 2 + me.c))
+        copy.start()
+        copies.append(copy)
+    yield
+    total = w1[mine].astype(F32)
+    for k in range(1, many):
+        copies[k - 1].wait()
+        total = total + r2[k - 1].astype(F32)
+    bits = me.cross_bits()
+    for at, bit in enumerate(bits):
+        w2[at] = total.astype(BF16)
+        copy = remote(w2.at[at], rx.at[at], send.at[many + at], recv.at[many + at], me.cross_bit(bit))
+        copy.start()
+        if at == 0:
+            yield
+        copy.wait()
+        total = total + rx[at].astype(F32)
+    out[...] = total.astype(BF16)
+
+
+def small_scratch(nq, groups, rows):
+    bits = groups.bit_length() - 1
+    return [
+        pltpu.VMEM((2 * nq, rows, 128), BF16), pltpu.VMEM((2 * nq, rows, 128), BF16),
+        pltpu.VMEM((2 * nq - 1, rows, 128), BF16), pltpu.VMEM((bits, rows, 128), BF16), pltpu.VMEM((bits, rows, 128), BF16),
+    ]
+
+
+def adjoint_flow(me, f_ref, tabs, sel_ref, s_ref, m0, r0, m1, r1, m2, r2, ss, rs, zs, zr):
+    nq = me.nq
+    one, two, three, four = tabs[4], tabs[5], tabs[6], tabs[7]
+    mine = f_ref[...].reshape(3, 2, 64, 128)
+    m0[...] = mine.astype(BF16)
+    copy = remote(m0, r0, ss.at[0], rs.at[0], me.core)
+    copy.start()
+    yield
+    copy.wait()
+    upper_core, upper_side = me.c == 1, me.y == 1
+    other = r0[...].astype(F32)
+    lower = jnp.where(upper_core, other, mine)
+    upper = jnp.where(upper_core, mine, other)
+    pair = lower + one * upper
+    after = jnp.where(upper_core, 0.0, other)
+    m1[...] = pair.astype(BF16)
+    copy = remote(m1, r1, ss.at[1], rs.at[1], me.side)
+    copy.start()
+    yield
+    copy.wait()
+    far = r1[...].astype(F32)
+    low_pair = jnp.where(upper_side, far, pair)
+    high_pair = jnp.where(upper_side, pair, far)
+    total = low_pair + two * high_pair
+    after = jnp.where(upper_side, 0.0, jnp.where(upper_core, far, one * far)) + after
+    m2[0] = total[:, 0].astype(BF16)
+    for m in range(3):
+        m2[1, m] = (sel_ref[m] * total[0, 1] + sel_ref[3 + m] * total[1, 1] + sel_ref[6 + m] * total[2, 1]).astype(BF16)
+    sends = []
+    for k in range(1, nq):
+        copy = remote(m2, r2.at[me.q], zs.at[k - 1], zr.at[k - 1], me.at_quad(me.quad(k)))
+        copy.start()
+        sends.append(copy)
+    r2[me.q] = m2[...]
+    yield
+    for k in range(1, nq):
+        src = r2.at[me.quad(nq - k)]
+        remote(src, src, zs.at[k - 1], zr.at[k - 1], me.core).wait_recv()
+    run = r2[0, 1].astype(F32)
+    for k in range(1, nq):
+        run = run + r2[k, 1].astype(F32)
+    carry = run
+    for k in range(nq - 1, -1, -1):
+        carry = jnp.where(me.q == k, run, carry)
+        run = four * run + r2[k, 0].astype(F32)
+    lead = pick(me.pos, [three, two, one, jnp.ones_like(one)])
+    for p in range(3):
+        s_ref[2 * p * 64 : (2 * p + 1) * 64] = lead * carry[p] + after[p, 0]
+        s_ref[(2 * p + 1) * 64 : (2 * p + 2) * 64] = after[p, 1]
+    for copy in sends:
+        copy.wait_send()
+
+
+class Steps:
+    def __init__(self, flows):
+        self.flows, self.live = flows, [True] * len(flows)
+
+    def __call__(self, *which):
+        for i in which:
+            if self.live[i]:
+                try:
+                    next(self.flows[i])
+                except StopIteration:
+                    self.live[i] = False
+
+    def finish(self):
+        while any(self.live):
+            self(*range(len(self.flows)))
+
+
+ORDERS = (True, False, True, False, True)
+N_BIG = 5
+
+
+def back_kernel(n, groups, *refs):
+    refs = list(refs)
+
+    def take(count):
+        got = refs[:count]
+        del refs[:count]
+        return got
+
+    base, slope_s, shared, t_keys, w_shared, tabs, power, power_rev, vec_wide, vec_head, starts, sum_wide, sum_head, sel = take(14)
+    h_act, h_ema, h_x, h_inner, h_units, h_middle, h_tokens = take(7)
+    grads = take(N_BIG)
+    (input_grad,) = take(1)
+    outs = take(N_BIG)
+    (out_small,) = take(1)
+    loads = take(7)
+    g_act, ema, x_lanes, inner, g_units, g_middle, tokens = loads
+    g_lanes, k_activ, k_gs, b_inner, b_flow, b_start, dx_lanes, acc_in, acc_decay, acc_out, kept, omega_acc, gain_acc = take(13)
+    t_sum, t_rows, t_grad, t_out, grad_in, g_small = take(6)
+    big = [take(8) for _ in range(N_BIG)]
+    small = take(5)
+    keys_s, tail_s = take(5), take(5)
+    exchange = take(6)
+    load_sem, big_send, big_recv, big_local, small_send, small_recv, k_send, k_recv, t_send, t_recv, ess, ers, ezs, ezr = take(14)
+
+    me = Place(n, groups)
+    own = base.shape[0]
+    total = tokens.shape[0]
+    width = tokens.shape[1]
+    length = 128
+    count = own // length
+    lanes = width // 128
+    chan = width // n
+    hbm = [h_act, h_ema, h_x, h_inner, h_units, h_middle, h_tokens]
+    arrive = [pltpu.make_async_copy(src, dst, load_sem.at[i]) for i, (src, dst) in enumerate(zip(hbm, loads))]
+    for copy in arrive:
+        copy.start()
+    meet(me.group_peers() + [me.cross_bit(bit) for bit in me.cross_bits()])
+    keys = tail_flow(me, t_keys, *keys_s, t_sum, k_send, k_recv)
+    next(keys)
+    steps = Steps(
+        [
+            big_flow(me, ORDERS[i], grads[i], *big[i], outs[i], big_send.at[i], big_recv.at[i], big_local.at[i])
+            for i in range(N_BIG)
+        ]
+    )
+    steps(*range(N_BIG))
+    k_mul = vec_head[2:3]
+    gain_one = vec_wide[0:1]
+    for ref in (omega_acc, gain_acc, acc_in, acc_decay, acc_out):
+        ref[...] = jnp.zeros_like(ref)
+    for i in range(3):
+        arrive[i].wait()
+
+    def grad_rows(row, with_tail):
+        at = pl.multiple_of(row * length, length)
+        here = pl.ds(at, length)
+        d_shared = base[here, :]
+        if with_tail:
+            extra = t_rows[pl.ds(pl.multiple_of(row // 2 * length, length), length), :]
+            d_shared = d_shared + extra * k_mul
+            gain_acc[1:2, 0:128] += jnp.sum(extra * shared[here, :], axis=0, keepdims=True)
+        gs = (d_shared * slope_s[here, :]).astype(BF16)
+        k_gs[here, :] = gs
+        for lane in range(lanes):
+            cut = slice(lane * 128, (lane + 1) * 128)
+            pre = ema[pl.ds(lane * total + at, length), :]
+            sig = jax.nn.sigmoid(pre)
+            k_activ[here, cut] = (pre * sig).astype(BF16)
+            back = g_act[here, cut] + nt(gs, w_shared[cut, :])
+            back = back * (sig * (1.0 + pre * (1.0 - sig)))
+            g_lanes[pl.ds(lane * own + at, length), :] = back
+            x = x_lanes[pl.ds(lane * total + at, length), :]
+            omega_acc[lane : lane + 1] += jnp.sum(back * x, axis=0, keepdims=True)
+
+    def local_pass(first):
+        ema_local_pass(
+            count, (first, 2, count // 2), g_lanes, tabs.at[0], tabs.at[1], tabs.at[2], tabs.at[3], b_inner, b_flow, True
+        )
+
+    def cont_rows(p, carry):
+        grad_rows(2 * p + 1, False)
+        return carry
+
+    def prompt_rows(p, carry):
+        grad_rows(2 * p, True)
+        return carry
+
+    def norm_rows_back(at, size, extra):
+        here = pl.ds(at, size)
+        plain, inv = norm_rows(tokens[here, :].astype(F32))
+        units = g_units[here, :]
+        if extra is not None:
+            units = units + extra
+        gain_acc[0:1] += jnp.sum(units * plain, axis=0, keepdims=True)
+        return norm_back(units, plain, inv, gain_one)
+
+    lax.fori_loop(0, count // 2, cont_rows, 0)
+    next(keys)
+    steps(0, 1)
+    local_pass(1)
+    next(keys)
+    steps(2, 3)
+    arrive[4].wait()
+    arrive[6].wait()
+    piece = (total - own) // 4
+    for part in range(4):
+        t_grad[part // 2, part % 2] = norm_rows_back(own + part * piece, piece, None).astype(BF16)
+    tail = tail_flow(me, t_grad, *tail_s, t_out, t_send, t_recv)
+    next(tail)
+    next(keys)
+    steps(4)
+    for _ in keys:
+        pass
+    for part in range(4):
+        t_rows[part * piece : (part + 1) * piece] = t_sum[part // 2, part % 2].astype(F32)
+    lax.fori_loop(0, count // 2, prompt_rows, 0)
+    local_pass(0)
+    adjoint = adjoint_flow(me, b_flow, tabs, sel, b_start, *exchange, ess, ers, ezs, ezr)
+    next(adjoint)
+    steps(0, 1)
+    next(adjoint)
+    next(tail)
+    steps(2)
+    next(adjoint)
+    next(tail)
+    steps(3)
+    for _ in adjoint:
+        pass
+    arrive[3].wait()
+    for row in range(count):
+        ema_back_pass(
+            count, total // length, row, x_lanes, g_lanes, tabs.at[0], tabs.at[8], vec_head, power, inner, starts,
+            power_rev, b_inner, b_start, dx_lanes, acc_in, acc_decay, acc_out, kept,
+        )
+        if row == 0:
+            steps(4)
+            next(tail)
+        elif row < count - 1:
+            steps(*range(N_BIG))
+    arrive[5].wait()
+
+    def own_rows(row, carry):
+        at = pl.multiple_of(row * length, length)
+        extra = jnp.concatenate([dx_lanes[pl.ds(lane * own + at, length), :] for lane in range(lanes)], axis=1)
+        grad_in[pl.ds(at, length), :] = g_middle[pl.ds(at, length), :] + norm_rows_back(at, length, extra)
+        return carry
+
+    lax.fori_loop(0, count, own_rows, 0)
+    alpha, beta, delta, eta, ab = (tabs[9 + i] for i in range(5))
+    m_sum, q_sum = eta * acc_in[...], eta * ab * acc_decay[...]
+    parts = (beta * m_sum - delta * q_sum, -alpha * q_sum, alpha * m_sum, ab * acc_out[...])
+    per = 128 // chan // 2
+    for lane in range(lanes):
+        cut = slice(lane * 128, (lane + 1) * 128)
+        block = [part[lane * 16 : lane * 16 + 16] for part in parts]
+        block += [omega_acc[lane : lane + 1], gain_acc[0:1, cut], sum_wide[0:1, cut], jnp.zeros((61, 128), F32)]
+        block = jnp.concatenate(block, axis=0).T.astype(BF16)
+        g_small[lane * per : (lane + 1) * per, :, 0:chan] = block.reshape(per, 2, chan, 128)
+    block = tn(k_activ[...], k_gs[...]).astype(BF16)
+    g_small[:, :, chan : 2 * chan] = block.reshape(n // 2, 2, chan, 128)
+    heads = jnp.concatenate((sum_head[0:2], sum_head[2:3] + gain_acc[1:2, 0:128], jnp.zeros((13, 128), F32)), axis=0)
+    heads = jnp.broadcast_to(heads.astype(BF16)[None, None], (n // 2, 2, 16, 128))
+    g_small[:, :, 2 * chan :] = heads
+    little = small_flow(me, g_small, *small, out_small, small_send, small_recv)
+    next(little)
+    for _ in tail:
+        pass
+    next(little)
+    steps(*range(N_BIG))
+
+    def cast_rows(row, carry):
+        here = pl.ds(pl.multiple_of(row * length, length), length)
+        input_grad[here, :] = grad_in[here, :].astype(BF16)
+        return carry
+
+    for part in range(4):
+        t_wide = t_out[part // 2, part % 2].astype(F32)
+        at = part * piece
+        while at < (part + 1) * piece:
+            m = at // length
+            stop = min((m + 1) * length, (part + 1) * piece)
+            here = slice(at + m * length, stop + m * length)
+            grad_in[here] = grad_in[here] + t_wide[at - part * piece : stop - part * piece]
+            at = stop
+    lax.fori_loop(0, count, cast_rows, 0)
+    next(little)
+    steps(*range(N_BIG))
+    for _ in little:
+        pass
+    steps.finish()
+
+
+def back_call(n, groups, ins, hbm, grads):
+    nq = n // 4
+    dma = pltpu.SemaphoreType.DMA
+    vm = pltpu.VMEM
+    shape = jax.ShapeDtypeStruct
+    own, total, width = ins[0].shape[0], hbm[6].shape[0], hbm[6].shape[1]
+    chan = width // n
+    small_rows = 2 * chan + 16
+    piece = (total - own) // 4
+    outs = [shape((own, width), BF16)] + [shape(grad.shape[-2:], BF16) for grad in grads] + [shape((small_rows, 128), BF16)]
+    scratch = [vm(part.shape, part.dtype) for part in hbm]
+    scratch += [
+        vm((own * 4, 128), F32), vm((own, width), BF16), vm((own, 128), BF16), vm((own * 4, 128), F32),
+        vm((own // 2, 128), F32), vm((own // 2, 128), F32), vm((own * 4, 128), F32), vm((64, 128), F32), vm((64, 128), F32),
+        vm((64, 128), F32), vm((128, 8, 128), F32), vm((8, 128), F32), vm((8, width), F32),
+        vm((2, 2, piece, 128), BF16), vm((4 * piece, 128), F32), vm((2, 2, piece, width), BF16), vm((2, 2, piece, width), BF16),
+        vm((own, width), F32), vm((n // 2, 2, small_rows, 128), BF16),
+    ]
+    for i, grad in enumerate(grads):
+        scratch += big_scratch(nq, groups, ORDERS[i], grad.shape[-2], grad.shape[-1])
+    scratch += small_scratch(nq, groups, small_rows)
+    scratch += tail_scratch(nq, piece, 128) + tail_scratch(nq, piece, width)
+    scratch += [vm((3, 2, 64, 128), BF16)] * 4 + [vm((2, 3, 64, 128), BF16), vm((nq, 2, 3, 64, 128), BF16)]
+    sems = nq + 3 + max(groups.bit_length() - 2, 1)
+    small_sems = 2 * nq + groups.bit_length() - 1
+    scratch += [
+        dma((7,)), dma((N_BIG, sems)), dma((N_BIG, sems)), dma((N_BIG,)), dma((small_sems,)), dma((small_sems,)),
+        dma((3,)), dma((nq + 4,)), dma((3,)), dma((nq + 4,)), dma((2,)), dma((2,)), dma((nq - 1,)), dma((nq - 1,)),
+    ]
+    return pl.pallas_call(
+        functools.partial(back_kernel, n, groups),
+        out_shape=outs,
+        in_specs=[VMEM] * 13 + [SMEM] + [ANY] * (7 + N_BIG),
+        out_specs=[VMEM] * len(outs),
+        scratch_shapes=scratch,
+        compiler_params=pltpu.CompilerParams(collective_id=2, has_side_effects=True, vmem_limit_bytes=60 << 20),
+        name="back",
+    )(*ins, *hbm, *grads)
+
+
 def lanes_first(rows):
     return rows.reshape(-1, 4, 128).transpose(1, 0, 2).reshape(-1, 128)
 
@@ -1117,72 +1316,32 @@
     ema_lanes = apply_pass_call(9, x_lanes, dec, mix, omega_lanes, power, inner, starts)
     grad_outer = cotangent[0].reshape(own_rows, width)
     vec_wide = jnp.pad(jnp.stack((gain_one, gain_two)), ((0, 6), (0, 0)))
-    vec_head = jnp.pad(jnp.stack((query_mul, query_add, key_mul)), ((0, 5), (0, 0)))
+    vec_head = jnp.concatenate((jnp.stack((query_mul, query_add, key_mul, key_mul)), omega_lanes), axis=0)
     (
         result, grad_middle, grad_act, grad_base, slope_shared, shared, grad_units, sum_outer, sum_inner, sum_hidden,
         sum_reset, sum_value, sent_keys, sum_wide, sum_head,
     ) = dense_call(
         n, rows_low[:own_rows], rows_low[own_rows:], ema_lanes, grad_outer, all_a, all_b, mat_shared, vec_wide, vec_head, targets
     )
-    sum_gain_two = sum_wide[0]
-    tail_keys = keys_call(n, groups, sent_keys.reshape(2, 2, sets * length // 4, 128))
-    tail_keys = tail_keys.reshape(sets, length, 128).astype(F32)
-    zeros = jnp.zeros_like(tail_keys)
-    tail_rows = jnp.stack((tail_keys, zeros), axis=1).reshape(own_rows, 128)
-    sum_query_mul, sum_query_add = sum_head[0], sum_head[1]
-    sum_key_mul = sum_head[2] + jnp.sum(tail_rows * shared, axis=0)
-    grad_shared_pre = ((grad_base + tail_rows * key_mul) * slope_shared).astype(BF16)
-    ema_own = rows_first(ema_lanes.reshape(4, -1, 128)[:, :own_rows].reshape(-1, 128))
-    activ = jax.nn.silu(ema_own).astype(BF16)
-    sum_shared = dot(activ, grad_shared_pre, (0, 0))
-    grad_act = grad_act + dot(grad_shared_pre, mat_shared, (1, 1))
-    grad_ema = grad_act * silu_grad(ema_own)
-    g_lanes = lanes_first(grad_ema)
-    back_inner, back_flow = local_pass_call(6, True, g_lanes, dec)
-    back_start = backward_exchange_call(n, groups, back_flow.reshape(3, 2, 64, 128), far, sel)
-    dx_lanes, acc_in, acc_decay, acc_out = back_pass_call(
-        6, 9, x_lanes, g_lanes, dec, mix, omega_lanes, power, inner, starts, power_rev, back_inner,
-        back_start.reshape(6 * 64, 128),
-    )
-    grad_units = jnp.concatenate((grad_units[:own_rows] + rows_first(dx_lanes), grad_units[own_rows:]), axis=0)
-    sum_gain_one = jnp.sum(grad_units * plain_in, axis=0)
-    grad_in = norm_back(grad_units, plain_in, inv_in, gain_one)
-    m_sum, q_sum = eta * acc_in, eta * ab * acc_decay
-    sum_alpha = beta * m_sum - delta * q_sum
-    sum_delta = -alpha * q_sum
-    sum_beta = alpha * m_sum
-    sum_eta = ab * acc_out
-    sum_omega = jnp.sum(grad_ema * normed[:own_rows], axis=0)
-
-    def by_channel(part):
-        return part.reshape(4, 16, 128).transpose(1, 0, 2).reshape(16, 512)
-
-    top = jnp.concatenate(
-        [by_channel(part) for part in (sum_alpha, sum_delta, sum_beta, sum_eta)]
-        + [sum_omega[None], sum_gain_one[None], sum_gain_two[None], jnp.zeros((61, width), F32)],
-        axis=0,
-    ).T.reshape(n, chan, 128)
-    triple = jnp.stack((sum_query_mul, sum_query_add, sum_key_mul), axis=1).reshape(n, heads, 3)
-    top = top + jnp.pad(triple, ((0, 0), (0, chan - heads), (67, 58)))
-    small_grad = jnp.concatenate((top, sum_shared.reshape(n, chan, 128)), axis=1)
-    small_grad = jnp.concatenate((small_grad, jnp.zeros_like(small_grad)), axis=2)
+    tabs = jnp.concatenate((dec, far, jnp.stack((mix, alpha, beta, delta, eta, ab))))
 
     def shards(grad):
         return grad.reshape(nq, 2, 2, -1, grad.shape[-1])
 
+    ins = (
+        grad_base, slope_shared, shared, sent_keys.reshape(2, 2, -1, 128), mat_shared, tabs, power, power_rev, vec_wide,
+        vec_head, starts, sum_wide, sum_head, sel,
+    )
+    hbm = (grad_act, ema_lanes, x_lanes, inner[: own_rows * 4], grad_units, grad_middle, rows_low)
     grads = [shards(part) for part in (sum_outer, sum_inner, sum_hidden, sum_reset, sum_value)]
-    grads.append(small_grad.astype(BF16).reshape(nq, 2, 2, 2 * chan, 256))
-    tail_grad = grad_in[own_rows:].astype(BF16).reshape(2, 2, sets * length // 4, width)
-    *sums, tail_sum = sums_call(n, groups, grads, tail_grad)
-    d_outer, d_inner, d_hidden, d_reset, d_value, d_small = [part.astype(F32) for part in sums]
-    add_tail = tail_sum.reshape(sets, length, width).astype(F32)
-    input_grad = (grad_middle + grad_in[:own_rows]).reshape(sets, 2, length, width)
-    input_grad = jnp.stack((input_grad[:, 0] + add_tail, input_grad[:, 1]), axis=1).astype(BF16)
+    input_grad, *sums, d_small = back_call(n, groups, ins, hbm, grads)
+    d_outer, d_inner, d_hidden, d_reset, d_value, d_small = [part.astype(F32) for part in (*sums, d_small)]
+    d_heads = lax.dynamic_slice(d_small, (2 * chan, seq_index * heads), (3, heads))
     return (
-        result.reshape(hidden_in.shape), input_grad[None], d_value, d_small[chan:, :128], d_reset, d_hidden, d_inner, d_outer,
-        d_small[:chan, 0:16], d_small[:chan, 16:32], d_small[:chan, 32:48], d_small[:chan, 48:64],
-        d_small[:chan, 64], d_small[:chan, 65], d_small[:chan, 66],
-        d_small[:heads, 67], d_small[:heads, 68], d_small[:heads, 69],
+        result.reshape(hidden_in.shape), input_grad.reshape(hidden_in.shape), d_value, d_small[chan : 2 * chan], d_reset,
+        d_hidden, d_inner, d_outer, d_small[:chan, 0:16], d_small[:chan, 16:32], d_small[:chan, 32:48],
+        d_small[:chan, 48:64], d_small[:chan, 64], d_small[:chan, 65], d_small[:chan, 66],
+        d_heads[0], d_heads[1], d_heads[2],
     )
 
 

time: 326 us -> 245 us (0.75)
  Pallas kernels: 245 us -> 196 us
  local copies, waits for them, and re-layouts: 44.7 us -> 26.3 us
  other arithmetic: 31.5 us -> 20.6 us
    pallas_call x3 -> x1, Pallas kernels: 102 us -> 74.9 us  [back_call(): pl.pallas_call(functools.partial(back_kernel, n, groups), out_shape=outs,...]
    pallas_call x4 -> x2, Pallas kernels: 40.5 us -> 18.1 us  [ema_call(): pl.pallas_call(kernel, out_shape=[jax.ShapeDtypeStruct(shape, F32) for sh...]
    reshape x11 -> x0, local copies, waits for them, and re-layouts: 7.59 us -> none  [the longest x8 3.44 us: by_channel(): return part.reshape(4, 16, 128).transpose(1, 0, 2).reshape(16, 512)]
    convert_element_type x6, other arithmetic: 3.33 us -> 8.25 us  [local(): part.astype(F32)]
    another operation x4 -> x1, other arithmetic: 4.53 us -> 0.01 us  [local(): jnp.stack((decay128, decay256, decay256 * decay128, decay256 * decay256))]
    unnamed x70 -> x41, local copies, waits for them, and re-layouts: 11.1 us -> 9.37 us
where the time goes in v1:
time: 245 us; the launch traced here: 244 us
  Pallas kernels  196 us (80%)
  local copies, waits for them, and re-layouts  26.3 us (11%)
  other arithmetic  20.6 us (8%)
    pallas_call x1, Pallas kernels, back_call(): pl.pallas_call(functools.partial(back_kernel, n, groups), out_shape=outs,...  74.9 us
    pallas_call x1, Pallas kernels, gather_call(): pl.pallas_call(functools.partial(gather_kernel, n, groups), out_shape=[ja...  49.2 us
    pallas_call x1, Pallas kernels, dense_call(): pl.pallas_call(functools.partial(dense_kernel, n), out_shape=outs, in_spe...  35.1 us
    pallas_call x1, Pallas kernels, forward_exchange_call(): pl.pallas_call(functools.partial(forward_exchange, n, groups), out_shape=...  18.6 us
    pallas_call x2, Pallas kernels, ema_call(): pl.pallas_call(kernel, out_shape=[jax.ShapeDtypeStruct(shape, F32) for sh...  18.1 us
    unnamed x41, local copies, waits for them, and re-layouts  9.37 us
    convert_element_type x6, other arithmetic, local(): part.astype(F32)  8.25 us

profile of v1, /device:TPU:0, one launch (start us, length us, event | category | flops | bytes accessed | tf_op | source)
XLA Modules:
  0.0 244.0 jit_solution(1283730273131131687)
XLA Ops:
  0.7 1.8 slice.106
  2.4 1.6 pad_maximum_fusion.1.a_in
  4.0 1.5 pad_maximum_fusion.2.b_in
  5.6 0.8 copy.63
  7.9 0.8 copy.66
  8.7 0.8 copy.67
  9.5 0.8 copy.68
  10.2 0.8 copy.69
  11.0 0.8 copy.70
  11.8 0.8 copy.71
  13.4 1.3 pad_maximum_fusion.5.s_in
  14.7 49.2 %gather_weights.1 = (bf16[16,64,128]{2,1,0:T(8,128)(2,1)}, bf16[16,96,1024]{2,1,0:T(8,128)(2,1)}, bf16[16,128,512]{2,1,0:T(8,128)(2,1)}, bf16[4,96,512]{2,1,0:T(8,128)(2,1)}) custom-call(bf16[64,128]{1,0:T(8,128)(2,1)} %pad_maximum_fusion.5.s_in, bf16[96,1024]{1,0:T(8,128)(2,1)} %pad_maximum_fusion.1.a_in, bf16[128,512]{1,0:T(8,128)(2,1)} %pad_maximum_fusion.2.b_in, ...), custom_call_target="tpu_custom_call" | custom-call | tf_op jit(solution)/shard_map/gather_weights/pallas_call | solution.py:312
  64.0 1.7 fusion.16
  68.8 1.9 multiply_multiply_fusion
  70.7 8.0 %ema_local.1 = (f32[4608,128]{1,0:T(8,128)}, f32[576,128]{1,0:T(8,128)}) custom-call(f32[4608,128]{1,0:T(8,128)} %bitcast.115, f32[4,64,128]{2,1,0:T(8,128)} %pad_maximum_fusion.3.d_ref), custom_call_target="tpu_custom_call" | custom-call | tf_op jit(solution)/shard_map/ema_local/pallas_call | solution.py:494
  78.8 0.9 slice.88
  81.4 18.6 %forward_exchange.1 = f32[9,64,128]{2,1,0:T(8,128)S(1)} custom-call(f32[3,2,64,128]{3,2,1,0:T(8,128)S(1)} %bitcast.113, f32[64,128]{1,0:T(8,128)S(1)} %bitcast.114, f32[4,64,128]{2,1,0:T(8,128)S(1)} %pad_maximum_fusion.4.d_ref, f32[9]{0:T(128)S(1)} %reshape.423.sel_ref.refs_13_), custom_call_target="tpu_custom_call" | custom-call | tf_op jit(solution)/shard_map/forward_exchange/pallas_call | solution.py:415
  100.9 0.9 copy.110
  102.4 10.0 %ema_apply.1.ema.refs_15_ = f32[4608,128]{1,0:T(8,128)} custom-call(f32[4608,128]{1,0:T(8,128)} %bitcast.116, f32[4,64,128]{2,1,0:T(8,128)} %pad_maximum_fusion.3.d_ref, f32[64,128]{1,0:T(8,128)} %bitcast_multiply_fusion.1.mix_ref, f32[4,128]{1,0:T(4,128)} %bitcast.164, f32[512,128]{1,0:T(8,128)} %bitcast.139, f32[4608,128]{1,0:T(8,128)} %get-tuple-element.48.inner_ref, ...), custom_call_target="tpu_custom_call" | custom-call | tf_op jit(solution)/shard_map/ema_apply/pallas_call | solution.py:494
  114.1 35.1 %dense.1 = (bf16[768,512]{1,0:T(8,128)(2,1)}, f32[768,512]{1,0:T(8,128)}, f32[768,512]{1,0:T(8,128)}, f32[768,128]{1,0:T(8,128)}, f32[768,128]{1,0:T(8,128)}, /*...) custom-call(bf16[768,512]{1,0:T(8,128)(2,1)} %bitcast.119, ...), custom_call_target="tpu_custom_call" | custom-call | tf_op jit(solution)/shard_map/dense/pallas_call | solution.py:787
  149.2 1.3 slice.94.refs_17_
  150.5 0.9 copy.109
  151.4 1.1 pad_maximum_fusion.refs_20_
  152.5 74.9 %back.1 = (bf16[768,512]{1,0:T(8,128)(2,1)}, bf16[64,512]{1,0:T(8,128)(2,1)}, bf16[32,1024]{1,0:T(8,128)(2,1)}, bf16[64,512]{1,0:T(8,128)(2,1)}, bf16[32,1024]{1...) custom-call(f32[768,128]{1,0:T(8,128)} %get-tuple-element.53.refs_0_, ...), custom_call_target="tpu_custom_call" | custom-call | tf_op jit(solution)/shard_map/back/pallas_call | solution.py:1224
  227.4 1.5 convert_element_type.43
  228.9 1.5 convert_element_type.45
  230.4 1.5 convert_element_type.46
  231.9 1.5 convert_element_type.47
  233.4 1.5 convert_element_type.48
  234.9 0.9 fusion.19
  240.6 1.3 slice.117
  241.9 2.1 copy.140
  (97 shorter events, 14.8 us)
Async XLA Ops:
  5.6 61.4 %copy-start.2 = (bf16[1,3,2,128,512]{4,3,2,1,0:T(8,128)(2,1)S(1)}, bf16[1,3,2,128,512]{4,3,2,1,0:T(8,128)(2,1)}, u32[]{:S(2)}) copy-start(bf16[1,3,2,128,512]{4,3,2,1,0:T(8,128)(2,1)} %param.19) | copy-start | bytes 2359300
  63.9 3.0 %copy-start.4 = (bf16[4,96,512]{2,1,0:T(8,128)(2,1)S(1)}, bf16[4,96,512]{2,1,0:T(8,128)(2,1)}, u32[]{:S(2)}) copy-start(bf16[4,96,512]{2,1,0:T(8,128)(2,1)} %get-tuple-element.46) | copy-start | bytes 1179652
  66.1 2.6 %copy-start.7 = (f32[14,64,128]{2,1,0:T(8,128)}, f32[14,64,128]{2,1,0:T(8,128)S(1)}, u32[]{:S(2)}) copy-start(f32[14,64,128]{2,1,0:T(8,128)S(1)} %constant_dynamic-update-slice_fusion.8.refs_5_) | copy-start | bytes 1376260
  68.8 11.4 %copy-start.10 = (s32[1,12]{1,0:T(1,128)S(1)}, s32[1,12]{1,0:T(1,128)}, u32[]{:S(2)}) copy-start(s32[1,12]{1,0:T(1,128)} %param.21) | copy-start | bytes 148
  81.2 31.2 %copy-start.9 = (s32[3]{0:T(128)}, s32[3]{0:T(128)S(1)}, u32[]{:S(2)}) copy-start(s32[3]{0:T(128)S(1)} %dynamic-slice_reduce_fusion.target) | copy-start | bytes 40
  81.3 31.1 %copy-start.1 = (f32[9]{0:T(128)}, f32[9]{0:T(128)S(1)}, u32[]{:S(2)}) copy-start(f32[9]{0:T(128)S(1)} %reshape.423.sel_ref.refs_13_) | copy-start | bytes 112
  100.0 0.7 copy-start
  102.4 10.5 %copy-start.8 = (f32[1,512]{1,0:T(1,128)S(1)}, f32[1,512]{1,0:T(1,128)}, u32[]{:S(2)}) copy-start(f32[1,512]{1,0:T(1,128)} %get-tuple-element.117) | copy-start | bytes 6148
  114.1 35.1 %copy-start.6 = (f32[4608,128]{1,0:T(8,128)S(1)}, f32[4608,128]{1,0:T(8,128)}, u32[]{:S(2)}) copy-start(f32[4608,128]{1,0:T(8,128)} %get-tuple-element.48.inner_ref) | copy-start | bytes 7077892
  149.2 2.2 copy-start.3
  149.2 2.2 copy-start.5

commit v2 on v1

--- a/solution.py
+++ b/solution.py
@@ -18,7 +18,7 @@
 F32 = jnp.float32
 BF16 = jnp.bfloat16
 VMEM = pl.BlockSpec(memory_space=pltpu.VMEM)
-ANY = pl.BlockSpec(memory_space=pl.ANY)
+HBM = pl.BlockSpec(memory_space=pltpu.HBM)
 SMEM = pl.BlockSpec(memory_space=pltpu.SMEM)
 
 
@@ -65,16 +65,19 @@
     lax.fori_loop(0, many * 4, body, 0)
 
 
-def ema_apply_pass(rows, x_ref, decay, mix, omega, power, inner_ref, start_ref, y_ref):
-    def body(item, carry):
-        row, lane = item // 4, item % 4
+def ema_apply_pass(rows, pick_rows, x_ref, decay, mix, omega, power, inner_ref, start_ref, y_ref):
+    first, many = pick_rows
+
+    def body(turn, carry):
+        row, lane = first + turn // 4, turn % 4
+        item = row * 4 + lane
         base = lane * (rows * 128) + row * 128
         state = [
             inner_ref[pl.ds((item * 16 + j) * 8, 8), :]
             + power[pl.ds((lane * 16 + j) * 8, 8), :] * row_of(start_ref, row * 64 + lane * 16 + j)
             for j in range(NJ)
         ]
-        skip = row_of(omega, lane)
+        skip = row_of(omega, 4 + lane)
         for step in range(SUB):
             x = x_ref[pl.ds(base + step, 8, stride=SUB), :]
             sums = [skip * x, None]
@@ -85,7 +88,7 @@
             y_ref[pl.ds(base + step, 8, stride=SUB), :] = sums[0] + sums[1]
         return carry
 
-    lax.fori_loop(0, rows * 4, body, 0)
+    lax.fori_loop(0, many * 4, body, 0)
 
 
 def ema_back_pass(
@@ -173,6 +176,13 @@
         return [1 << b for b in range(self.groups.bit_length() - 1)]
 
 
+def chosen(resumed, me):
+    def at(p, m):
+        return jnp.where(resumed[0, p * me.nq + me.q] == m, 1.0, 0.0)
+
+    return at
+
+
 def meet(peers):
     barrier = pltpu.get_barrier_semaphore()
     for peer in peers:
@@ -186,145 +196,6 @@
     )
 
 
-def gather_kernel(n, groups, s_in, a_in, b_in, x_in, s_out, a_out, b_out, x_out, ss, sr, zs, zr, ys, yr, xs, xr, cs, cr, ts, tr, ls):
-    me = Place(n, groups)
-    nq = me.nq
-    meet(me.group_peers() + [me.cross])
-    mats = ((a_in, a_out, a_in.shape[-1] // 2), (b_in, b_out, b_in.shape[-1] // 2))
-    sent = []
-
-    def send(*args):
-        copy = remote(*args)
-        copy.start()
-        sent.append(copy)
-
-    def got(ref, recv):
-        remote(ref, ref, ls.at[0], recv, me.core).wait_recv()
-
-    own = [pltpu.make_async_copy(s_in, s_out.at[me.s], ls.at[0])]
-    own += [pltpu.make_async_copy(w_in, w_out.at[me.s], ls.at[1 + i]) for i, (w_in, w_out, _) in enumerate(mats)]
-    for copy in own:
-        copy.start()
-    for k in range(1, n):
-        send(s_in, s_out.at[me.s], ss.at[k - 1], sr.at[k - 1], (me.g, (me.s + k) % n))
-
-    @pl.when(me.is_last)
-    def _():
-        for j in range(3):
-            remote(x_in.at[j], x_out.at[j], ts.at[j], tr.at[0], (me.g, 4 * (nq - 1) + j)).start()
-        pltpu.make_async_copy(x_in.at[3], x_out.at[3], ls.at[3]).start()
-
-    def half(ref, width, which):
-        return ref.at[:, pl.ds(pl.multiple_of(which * width, 128), width)]
-
-    for k in range(1, nq):
-        for i, (w_in, w_out, width) in enumerate(mats):
-            send(half(w_in, width, me.x), half(w_out.at[me.s], width, me.x), zs.at[k - 1, i], zr.at[k - 1, i], me.at_quad(me.quad(k)))
-    for i, (w_in, w_out, width) in enumerate(mats):
-        send(w_in, w_out.at[me.s], ys.at[0, i], yr.at[0, i], me.side)
-        send(w_in, w_out.at[me.s], cs.at[0, i], cr.at[0, i], me.core)
-
-    @pl.when(me.q == nq - 1)
-    def _():
-        @pl.when(me.is_last)
-        def _():
-            pltpu.make_async_copy(x_in.at[3], x_out.at[3], ls.at[3]).wait()
-
-        @pl.when(jnp.logical_not(me.is_last))
-        def _():
-            got(x_out.at[me.pos], tr.at[0])
-
-        for k in range(1, nq):
-            remote(x_out.at[me.pos], x_out.at[me.pos], ts.at[2 + k], tr.at[1], me.at_quad(me.quad(k))).start()
-
-    other = 1 - me.x
-    for k in range(1, nq):
-        shard = me.quad(nq - k) * 4 + me.pos
-        for i, (w_in, w_out, width) in enumerate(mats):
-            piece = half(w_out.at[shard], width, me.x)
-            got(piece, zr.at[k - 1, i])
-            send(piece, piece, ys.at[k, i], yr.at[k, i], me.side)
-            send(piece, piece, xs.at[k - 1, i], xr.at[k - 1, i], me.cross)
-            send(piece, piece, cs.at[k, i], cr.at[k, i], me.core)
-
-    @pl.when(me.q != nq - 1)
-    def _():
-        got(x_out.at[me.pos], tr.at[1])
-
-    mine = x_out.at[me.pos]
-    send(mine, mine, ts.at[nq + 2], tr.at[2], me.side)
-    send(mine, mine, ts.at[nq + 3], tr.at[3], me.core)
-
-    side_pos = me.pos + 2 - 4 * me.y
-    for k in range(nq):
-        shard = me.quad(nq - k) * 4 + side_pos
-        for i, (w_in, w_out, width) in enumerate(mats):
-            piece = w_out.at[shard] if k == 0 else half(w_out.at[shard], width, me.x)
-            got(piece, yr.at[k, i])
-            if k:
-                send(piece, piece, xs.at[nq - 2 + k, i], xr.at[nq - 2 + k, i], me.cross)
-            send(piece, piece, cs.at[nq + k, i], cr.at[nq + k, i], me.core)
-    theirs = x_out.at[side_pos]
-    got(theirs, tr.at[2])
-    send(theirs, theirs, ts.at[nq + 4], tr.at[4], me.core)
-    for group, pos in ((0, me.pos), (1, side_pos)):
-        for k in range(1, nq):
-            shard = me.quad(nq - k) * 4 + pos
-            at = group * (nq - 1) + k - 1
-            for i, (w_in, w_out, width) in enumerate(mats):
-                piece = half(w_out.at[shard], width, other)
-                got(piece, xr.at[at, i])
-                send(piece, piece, cs.at[2 * nq + at, i], cr.at[2 * nq + at, i], me.core)
-    flip = 1 - 2 * me.c
-    for group, pos in ((0, me.pos + flip), (1, side_pos + flip)):
-        for k in range(nq):
-            shard = me.quad(nq - k) * 4 + pos
-            for i, (w_in, w_out, width) in enumerate(mats):
-                if k == 0:
-                    got(w_out.at[shard], cr.at[group * nq, i])
-                else:
-                    got(half(w_out.at[shard], width, me.x), cr.at[group * nq + k, i])
-                    at = 2 * nq + group * (nq - 1) + k - 1
-                    got(half(w_out.at[shard], width, other), cr.at[at, i])
-    got(x_out.at[me.pos + flip], tr.at[3])
-    got(x_out.at[side_pos + flip], tr.at[4])
-    for k in range(1, n):
-        got(s_out.at[(me.s + n - k) % n], sr.at[k - 1])
-    for copy in own:
-        copy.wait()
-    for copy in sent:
-        copy.wait_send()
-
-    @pl.when(me.is_last)
-    def _():
-        for j in range(3):
-            remote(x_in.at[j], x_out.at[j], ts.at[j], tr.at[0], (me.g, 4 * (nq - 1) + j)).wait_send()
-
-    @pl.when(me.q == nq - 1)
-    def _():
-        for k in range(1, nq):
-            remote(x_out.at[me.pos], x_out.at[me.pos], ts.at[2 + k], tr.at[1], me.at_quad(me.quad(k))).wait_send()
-
-
-def gather_call(n, groups, small, mat_a, mat_b, tail):
-    nq = n // 4
-    sems = [(n - 1,), (n - 1,), (nq - 1, 2), (nq - 1, 2), (nq, 2), (nq, 2), (2 * nq - 2, 2), (2 * nq - 2, 2), (4 * nq - 2, 2), (4 * nq - 2, 2), (nq + 5,), (5,), (4,)]
-    return pl.pallas_call(
-        functools.partial(gather_kernel, n, groups),
-        out_shape=[
-            jax.ShapeDtypeStruct((n,) + small.shape, BF16),
-            jax.ShapeDtypeStruct((n,) + mat_a.shape, BF16),
-            jax.ShapeDtypeStruct((n,) + mat_b.shape, BF16),
-            jax.ShapeDtypeStruct(tail.shape, BF16),
-        ],
-        in_specs=[ANY] * 4,
-        out_specs=[ANY] * 4,
-        scratch_shapes=[pltpu.SemaphoreType.DMA(shape) for shape in sems],
-        compiler_params=pltpu.CompilerParams(collective_id=0, has_side_effects=True),
-        name="gather_weights",
-    )(small, mat_a, mat_b, tail)
-
-
 def pick(index, values):
     out = values[0]
     for k in range(1, len(values)):
@@ -332,17 +203,230 @@
     return out
 
 
-def forward_exchange(n, groups, f_ref, ab_ref, d_ref, sel_ref, s_ref, m0, r0, m1, r1, m2, r2, ss, rs, zs, zr, ps, pr):
-    me = Place(n, groups)
+def tail_flow(me, t, r1, w1, r2, w2, r3, out, send, recv):
     nq = me.nq
-    meet(me.group_peers())
-    one, two, three, four = d_ref[0], d_ref[1], d_ref[2], d_ref[3]
-    m0[...] = f_ref[0:3].astype(BF16)
+    last = me.q == nq - 1
+    out[...] = jnp.zeros_like(out)
+    copy1 = remote(t.at[:, 1 - me.c], r1, send.at[0], recv.at[0], me.core)
+    copy1.start()
+    yield
+    copy1.wait()
+    for i in range(2):
+        w1[i] = (t[i, me.c].astype(F32) + r1[i].astype(F32)).astype(BF16)
+    copy2 = remote(w1.at[1 - me.y], r2, send.at[1], recv.at[1], me.side)
+    copy2.start()
+    yield
+    copy2.wait()
+    w2[...] = (w1[me.y].astype(F32) + r2[...].astype(F32)).astype(BF16)
+    top = (me.g, (nq - 1) * 4 + me.pos)
+    end = (me.g, nq * 4 - 1)
+    for k in range(nq - 1):
+        @pl.when(me.q == k)
+        def _():
+            remote(w2, r3.at[k], send.at[2], recv.at[2 + k], top).start()
+    yield
+
+    @pl.when(last)
+    def _():
+        total = w2[...].astype(F32)
+        for k in range(nq - 1):
+            remote(r3.at[k], r3.at[k], send.at[2], recv.at[2 + k], me.core).wait_recv()
+            total = total + r3[k].astype(F32)
+        w2[...] = total.astype(BF16)
+
+        @pl.when(jnp.logical_not(me.is_last))
+        def _():
+            for j in range(3):
+                @pl.when(me.pos == j)
+                def _():
+                    remote(w2, out.at[j // 2, j % 2], send.at[2], recv.at[nq + 1 + j], end).start()
+
+        @pl.when(me.is_last)
+        def _():
+            out[1, 1] = w2[...]
+    yield
+
+    @pl.when(me.is_last)
+    def _():
+        for j in range(3):
+            dst = out.at[j // 2, j % 2]
+            remote(dst, dst, send.at[2], recv.at[nq + 1 + j], me.core).wait_recv()
+
+    @pl.when(jnp.logical_not(me.is_last))
+    def _():
+        remote(w2, w2, send.at[2], recv.at[2], me.core).wait_send()
+
+
+def tail_scratch(nq, rows, width):
+    return [
+        pltpu.VMEM((2, rows, width), BF16), pltpu.VMEM((2, rows, width), BF16),
+        pltpu.VMEM((rows, width), BF16), pltpu.VMEM((rows, width), BF16),
+        pltpu.VMEM((nq - 1, rows, width), BF16),
+    ]
+
+
+class Sender:
+    def __init__(self, spare):
+        self.spare, self.started = spare, []
+
+    def send(self, src, dst, send, recv, device, when=None):
+        copy = remote(src, dst, send, recv, device)
+        if when is None:
+            copy.start()
+        else:
+            pl.when(when)(copy.start)
+        self.started.append((copy, when))
+
+    def got(self, ref, recv):
+        remote(ref, ref, self.spare, recv, self.device).wait_recv()
+
+    def finish(self):
+        for copy, when in self.started:
+            if when is None:
+                copy.wait_send()
+            else:
+                pl.when(when)(copy.wait_send)
+
+
+def small_gather(me, out, post, ss, sr):
+    for k in range(1, me.n):
+        post.send(out.at[me.s], out.at[me.s], ss.at[k - 1], sr.at[k - 1], (me.g, (me.s + k) % me.n))
+
+
+def small_arrive(me, out, post, sr):
+    for k in range(1, me.n):
+        post.got(out.at[(me.s + me.n - k) % me.n], sr.at[k - 1])
+
+
+def gather_flow(me, post, a_own, b_own, a_out, b_out, x_in, x_out, zs, zr, ys, yr, xs, xr, cs, cr, ts, tr, local_sem):
+    nq = me.nq
+    mats = ((a_out, a_out.shape[-1] // 2), (b_out, b_out.shape[-1] // 2))
+    other = 1 - me.x
+    piece_rows = x_out.shape[1] // 4
+
+    def half(ref, width, which):
+        return ref.at[:, pl.ds(pl.multiple_of(which * width, 128), width)]
+
+    def quarter(ref, pos):
+        return ref.at[:, pl.ds(pl.multiple_of(pos * piece_rows, piece_rows), piece_rows)]
+
+    up, down = (me.g, me.s + 4), (me.g, me.s - 4)
+    has_up, has_down = me.q < nq - 1, me.q > 0
+    ours = (a_own, b_own)
+    for i, (w_out, width) in enumerate(mats):
+        piece, place = half(ours[i], width, me.x), half(w_out.at[me.s], width, me.x)
+        post.send(piece, place, zs.at[0, 0, i], zr.at[0, 0, i], up, has_up)
+        post.send(piece, place, zs.at[1, 0, i], zr.at[1, 0, i], down, has_down)
+        post.send(ours[i], w_out.at[me.s], ys.at[0, i], yr.at[0, i], me.side)
+    for i, (w_out, width) in enumerate(mats):
+        post.send(ours[i], w_out.at[me.s], cs.at[0, i], cr.at[0, i], me.core)
+    in_last = me.q == nq - 1
+    keep = pltpu.make_async_copy(quarter(x_in, me.pos), quarter(x_out, me.pos), local_sem)
+    pl.when(me.is_last)(keep.start)
+    for j in range(3):
+        post.send(quarter(x_in, j), quarter(x_out, j), ts.at[j], tr.at[0], (me.g, 4 * (nq - 1) + j), me.is_last)
+    yield
+
+    @pl.when(jnp.logical_and(in_last, jnp.logical_not(me.is_last)))
+    def _():
+        post.got(quarter(x_out, me.pos), tr.at[0])
+
+    pl.when(me.is_last)(keep.wait)
+    mine = quarter(x_out, me.pos)
+    for k in range(1, nq):
+        post.send(mine, mine, ts.at[2 + k], tr.at[1], me.at_quad(me.quad(k)), in_last)
+
+    def arrival(side, hop):
+        there = me.q - hop if side == 0 else me.q + hop
+        here = there >= 0 if side == 0 else there < nq
+        onward, to = (has_up, up) if side == 0 else (has_down, down)
+
+        def pieces(pos, which):
+            shard = jnp.clip(there, 0, nq - 1) * 4 + pos
+            return [half(w_out.at[shard], width, which) for w_out, width in mats]
+
+        return here, jnp.logical_and(here, onward), to, pieces
+
+    arrivals = [(hop, side) for hop in range(1, nq) for side in range(2)]
+    side_pos = me.pos + 2 - 4 * me.y
+    for hop, side in arrivals:
+        here, onward, to, pieces = arrival(side, hop)
+        at = (hop - 1) * 2 + side
+        for i, piece in enumerate(pieces(me.pos, me.x)):
+            pl.when(here)(functools.partial(post.got, piece, zr.at[side, hop - 1, i]))
+            if hop < nq - 1:
+                post.send(piece, piece, zs.at[side, hop, i], zr.at[side, hop, i], to, onward)
+            post.send(piece, piece, ys.at[1 + at, i], yr.at[1 + at, i], me.side, here)
+            post.send(piece, piece, xs.at[at, i], xr.at[at, i], me.cross, here)
+            post.send(piece, piece, cs.at[1 + at, i], cr.at[1 + at, i], me.core, here)
+        if side:
+            yield
+
+    @pl.when(jnp.logical_not(in_last))
+    def _():
+        post.got(mine, tr.at[1])
+
+    post.send(mine, mine, ts.at[nq + 2], tr.at[2], me.side)
+    post.send(mine, mine, ts.at[nq + 3], tr.at[3], me.core)
+    count = len(arrivals)
+    for i, (w_out, width) in enumerate(mats):
+        block = w_out.at[me.q * 4 + side_pos]
+        post.got(block, yr.at[0, i])
+        post.send(block, block, cs.at[1 + count, i], cr.at[1 + count, i], me.core)
+    for hop, side in arrivals:
+        here, _, _, pieces = arrival(side, hop)
+        at = (hop - 1) * 2 + side
+        for i, piece in enumerate(pieces(side_pos, me.x)):
+            pl.when(here)(functools.partial(post.got, piece, yr.at[1 + at, i]))
+            post.send(piece, piece, xs.at[count + at, i], xr.at[count + at, i], me.cross, here)
+            post.send(piece, piece, cs.at[2 + count + at, i], cr.at[2 + count + at, i], me.core, here)
+        if side:
+            yield
+    theirs = quarter(x_out, side_pos)
+    post.got(theirs, tr.at[2])
+    post.send(theirs, theirs, ts.at[nq + 4], tr.at[4], me.core)
+    flip = 1 - 2 * me.c
+    post.got(quarter(x_out, me.pos + flip), tr.at[3])
+    post.got(quarter(x_out, side_pos + flip), tr.at[4])
+    yield
+    for group, pos in ((0, me.pos), (1, side_pos)):
+        for hop, side in arrivals:
+            here, _, _, pieces = arrival(side, hop)
+            at = group * count + (hop - 1) * 2 + side
+            to = 2 + 2 * count + at
+            for i, piece in enumerate(pieces(pos, other)):
+                pl.when(here)(functools.partial(post.got, piece, xr.at[at, i]))
+                post.send(piece, piece, cs.at[to, i], cr.at[to, i], me.core, here)
+        yield
+    for group, pos in ((0, me.pos + flip), (1, side_pos + flip)):
+        for i, (w_out, width) in enumerate(mats):
+            post.got(w_out.at[me.q * 4 + pos], cr.at[group * (1 + count), i])
+        for hop, side in arrivals:
+            here, _, _, pieces = arrival(side, hop)
+            at = (hop - 1) * 2 + side
+            for i, piece in enumerate(pieces(pos, me.x)):
+                pl.when(here)(functools.partial(post.got, piece, cr.at[group * (1 + count) + 1 + at, i]))
+            for i, piece in enumerate(pieces(pos, other)):
+                pl.when(here)(functools.partial(post.got, piece, cr.at[2 + 2 * count + group * count + at, i]))
+
+
+def gather_sems(nq):
+    count = 2 * (nq - 1)
+    shapes = [(2, nq - 1, 2)] * 2 + [(1 + count, 2)] * 2 + [(2 * count, 2)] * 2 + [(2 + 4 * count, 2)] * 2 + [(nq + 5,), (5,)]
+    return [pltpu.SemaphoreType.DMA(shape) for shape in shapes]
+
+
+def state_flow(me, f_ref, tabs, sel, s_ref, m0, r0, m1, r1, m2, r2, ss, rs, zs, zr, ps, pr):
+    nq = me.nq
+    one, two, three, four = tabs[4], tabs[5], tabs[6], tabs[7]
+    ab = tabs[13]
+    mine = f_ref[0:384].reshape(3, 2, 64, 128)
+    m0[...] = mine.astype(BF16)
     copy = remote(m0, r0, ss.at[0], rs.at[0], me.core)
     copy.start()
+    yield
     copy.wait()
     upper_core, upper_side = me.c == 1, me.y == 1
-    mine = f_ref[0:3]
     other = r0[...].astype(F32)
     lower = jnp.where(upper_core, other, mine)
     upper = jnp.where(upper_core, mine, other)
@@ -350,9 +434,10 @@
     before = jnp.where(upper_core, other, 0.0)
     m1[0] = pair.astype(BF16)
     m1[1, :, 0] = lower[:, 0].astype(BF16)
+    m1[1, :, 1] = jnp.zeros((3, 64, 128), BF16)
     copy = remote(m1, r1, ss.at[1], rs.at[1], me.side)
-    m1[1, :, 1] = jnp.zeros_like(m1[1, :, 1])
     copy.start()
+    yield
     copy.wait()
     far = r1[0].astype(F32)
     low_pair = jnp.where(upper_side, far, pair)
@@ -376,6 +461,7 @@
         r2[nq] = m2[1]
 
     r2[me.q] = m2[0]
+    yield
     for k in range(1, nq):
         src = r2.at[me.quad(nq - k)]
         remote(src, src, zs.at[k - 1], zr.at[k - 1], me.core).wait_recv()
@@ -391,15 +477,15 @@
         if k == nq - 1:
             tail_in = three * run + r2[nq].astype(F32)
         run = four * run + r2[k].astype(F32)
-    low = (ab_ref[...] * run).astype(BF16).astype(F32)
-    safe = jnp.abs(ab_ref[...]) >= TINY
-    begin = jnp.where(safe, low / jnp.where(safe, ab_ref[...], 1.0), run)
+    low = (ab * run).astype(BF16).astype(F32)
+    safe = jnp.abs(ab) >= TINY
+    begin = jnp.where(safe, low / jnp.where(safe, ab, 1.0), run)
     lead = pick(me.pos, [jnp.ones_like(one), one, two, three])
     for p in range(3):
-        start = sel_ref[p * 3] * begin[0] + sel_ref[p * 3 + 1] * begin[1] + sel_ref[p * 3 + 2] * begin[2]
-        s_ref[2 * p] = lead * carry[p] + before[p, 0]
-        s_ref[2 * p + 1] = lead * start + before[p, 1]
-        s_ref[6 + p] = tail_in[p]
+        start = sel(p, 0) * begin[0] + sel(p, 1) * begin[1] + sel(p, 2) * begin[2]
+        s_ref[128 * p : 128 * p + 64] = lead * carry[p] + before[p, 0]
+        s_ref[128 * p + 64 : 128 * p + 128] = lead * start + before[p, 1]
+        s_ref[384 + 64 * p : 448 + 64 * p] = tail_in[p]
     for copy in sends:
         copy.wait_send()
 
@@ -409,111 +495,207 @@
             remote(m2.at[1], r2.at[nq], ps.at[k - 1], pr.at[0], me.at_quad(me.quad(k))).wait_send()
 
 
-def forward_exchange_call(n, groups, finals, ab, decays, sel):
+def front_kernel(n, groups, *refs):
+    refs = list(refs)
+
+    def take(count):
+        got = refs[:count]
+        del refs[:count]
+        return got
+
+    p_rates, p_vecs, (resumed,) = take(4), take(6), take(1)
+    h_tokens, i_value, i_reset, i_inner, i_hidden, i_outer, i_shared = take(7)
+    tabs, power, power_rev, vec_wide, vec_head, starts, w_shared = take(7)
+    o_ema, o_x, o_inner, a_out, b_out, x_out = take(6)
+    gathered, lift, a_own, b_own, tokens, tail, x_lanes, ema, inner, finals = take(10)
+    exchange = take(6)
+    load_sem, ss, sr, hs, hr = take(5)
+    gather_sem = take(10)
+    ess, ers, ezs, ezr, eps, epr = take(6)
+
+    me = Place(n, groups)
+    length = 128
+    width = tokens.shape[1]
+    lanes = width // 128
+    own = tokens.shape[0]
+    total = own + tail.shape[0] * length
+    count = own // length
+    chan = width // n
+    heads = 128 // n
+    rows_b = i_hidden.shape[0]
+    sets = count // 2
+    sel = chosen(resumed, me)
+
+    def local_copy(src, dst, at):
+        copy = pltpu.make_async_copy(src, dst, load_sem.at[at])
+        copy.start()
+        return copy
+
+    x_in = h_tokens.at[:, 0]
+    packing = [
+        local_copy(i_value, a_own.at[0:chan], 0),
+        local_copy(i_reset, a_own.at[chan : 2 * chan], 1),
+        local_copy(i_inner, a_own.at[2 * chan : 3 * chan], 2),
+        local_copy(i_hidden, b_own.at[0:rows_b], 3),
+        local_copy(i_outer, b_own.at[rows_b : 2 * rows_b], 4),
+        local_copy(i_shared, w_shared.at[me.s], 5),
+    ]
+    fetch = [local_copy(h_tokens.at[p, k], tokens.at[(p * 2 + k) * length : (p * 2 + k + 1) * length], 6 + p * 2 + k) for p in range(sets) for k in range(2)]
+    lift[...] = jnp.zeros_like(lift)
+    block = jnp.zeros((16, 128), F32)
+    for i, ref in enumerate(p_rates):
+        lift[i, :, 0:chan] = ref[...].astype(F32)
+        block = block + pltpu.roll(lift[i], 32 * i, 1)
+    for i, ref in enumerate(p_vecs):
+        lift[4, i : i + 1, 0 : ref.shape[1]] = ref[...].astype(F32)
+    gathered[me.s, 0:16] = block.astype(BF16)
+    gathered[me.s, 16:32] = lift[4].astype(BF16)
+    meet(me.group_peers() + [me.cross])
+    post = Sender(load_sem.at[12])
+    post.device = me.core
+    small_gather(me, gathered, post, ss, sr)
+    for copy in packing:
+        copy.wait()
+    placing = [local_copy(a_own, a_out.at[me.s], 14), local_copy(b_own, b_out.at[me.s], 15)]
+    gather = gather_flow(me, post, a_own, b_own, a_out, b_out, x_in, x_out, *gather_sem, load_sem.at[13])
+    next(gather)
+    small_gather(me, w_shared, post, hs, hr)
+    for copy in fetch:
+        copy.wait()
+
+    def norm_step(row, carry):
+        here = pl.ds(pl.multiple_of(row * length, length), length)
+        plain, _ = norm_rows(tokens[here, :].astype(F32))
+        for lane in range(lanes):
+            x_lanes[pl.ds(lane * total + row * length, length), :] = plain[:, lane * 128 : (lane + 1) * 128]
+        return carry
+
+    lax.fori_loop(0, count, norm_step, 0)
+    small_arrive(me, gathered, post, sr)
+    per = 128 // chan
+    column = lax.broadcasted_iota(jnp.int32, (16, 128), 1)
+    head_sum = jnp.zeros((16, 128), F32)
+    for lane in range(lanes):
+        rates = [jnp.zeros((16, 128), F32)] * 4
+        wide = jnp.zeros((16, 128), F32)
+        for k in range(per):
+            block = gathered[lane * per + k, 0:16].astype(F32)
+            for i in range(4):
+                mine = jnp.where((column >= 32 * i) & (column < 32 * i + chan), block, 0.0)
+                rates[i] = rates[i] + pltpu.roll(mine, (chan * k - 32 * i) % 128, 1)
+            rows = gathered[lane * per + k, 16:32].astype(F32)
+            wide = wide + pltpu.roll(rows, chan * k, 1)
+            head_sum = head_sum + pltpu.roll(rows, heads * (lane * per + k), 1)
+        for i in range(4):
+            tabs[9 + i, lane * 16 : lane * 16 + 16] = rates[i]
+        vec_wide[:, lane * 128 : (lane + 1) * 128] = wide[0:8]
+        vec_head[4 + lane : 5 + lane] = wide[2:3]
+    vec_head[0:3] = head_sum[3:6]
+    vec_head[3:4] = head_sum[3:4]
+    alpha, delta, beta, eta = tabs[9], tabs[10], tabs[11], tabs[12]
+    decay = 1.0 - alpha * delta
+    chain = [decay]
+    for _ in range(9):
+        chain.append(chain[-1] * chain[-1])
+    ab = alpha * beta
+    tabs[10], tabs[11] = beta, delta
+    tabs[0], tabs[1], tabs[2], tabs[3] = decay, chain[4], chain[5], chain[6]
+    tabs[4], tabs[5], tabs[6], tabs[7] = chain[7], chain[8], chain[8] * chain[7], chain[9]
+    tabs[8], tabs[13] = ab * eta, ab
+    d16, d32, d64 = chain[4], chain[5], chain[6]
+    steps = [jnp.ones_like(decay), d16, d32, d32 * d16, d64, d64 * d16, d64 * d32, d64 * d32 * d16]
+    for k in range(8):
+        power[pl.ds(k, 64, stride=8), :] = steps[k]
+        power_rev[pl.ds(7 - k, 64, stride=8), :] = steps[k]
+    for lane in range(lanes):
+        x_lanes[lane * total : lane * total + own] = x_lanes[lane * total : lane * total + own] * vec_wide[0:1, lane * 128 : (lane + 1) * 128]
+
+    def local_pass(first, many):
+        ema_local_pass(
+            total // length, (first, 1, many), x_lanes, tabs.at[0], tabs.at[1], tabs.at[2], tabs.at[3], inner, finals, False
+        )
+
+    def apply_pass(first, many):
+        ema_apply_pass(total // length, (first, many), x_lanes, tabs.at[0], tabs.at[8], vec_head, power, inner, starts, ema)
+
+    def more():
+        next(gather, None)
+
+    for part in range(2):
+        local_pass(part * (count // 2), count // 2)
+        more()
+    state = state_flow(me, finals, tabs, sel, starts, *exchange, ess, ers, ezs, ezr, eps, epr)
+    next(state)
+    keep = local_copy(inner.at[0 : own * 4], o_inner, 5)
+    more()
+    next(state)
+    more()
+    next(state)
+    more()
+    for _ in state:
+        pass
+    for part in range(3):
+        apply_pass(part * (count // 3), count // 3)
+        if part < 2:
+            more()
+    bring = local_copy(x_out, tail, 6)
+    bring.wait()
+    small_arrive(me, w_shared, post, hr)
+
+    def tail_norm(m, carry):
+        plain, _ = norm_rows(tail[m].astype(F32))
+        plain = plain * vec_wide[0:1]
+        for lane in range(lanes):
+            x_lanes[pl.ds(lane * total + own + m * length, length), :] = plain[:, lane * 128 : (lane + 1) * 128]
+        return carry
+
+    lax.fori_loop(0, sets, tail_norm, 0)
+    local_pass(count, sets)
+    keep_x = local_copy(x_lanes, o_x, 7)
+    more()
+    apply_pass(count, sets)
+    keep_ema = local_copy(ema, o_ema, 8)
+    for _ in gather:
+        pass
+    for copy in (keep, keep_x, keep_ema, *placing):
+        copy.wait()
+    post.finish()
+
+
+def front_call(n, groups, rates, vectors, resumed, tokens, weights):
     nq = n // 4
     dma = pltpu.SemaphoreType.DMA
+    vm = pltpu.VMEM
+    shape = jax.ShapeDtypeStruct
+    sets, kinds, length, width = tokens.shape
+    own = sets * kinds * length
+    total = own + sets * length
+    chan, hv = weights[0].shape
+    rows_b = weights[3].shape[0]
+    outs = [
+        shape((14, 64, 128), F32), shape((512, 128), F32), shape((512, 128), F32), shape((8, width), F32), shape((8, 128), F32),
+        shape((total // 2, 128), F32), shape((n, chan, 128), BF16),
+        shape((total * 4, 128), F32), shape((total * 4, 128), F32), shape((own * 4, 128), F32),
+        shape((n, 3 * chan, hv), BF16), shape((n, 2 * rows_b, width), BF16), shape((sets, length, width), BF16),
+    ]
+    scratch = [
+        vm((n, 32, 128), BF16), vm((5, 16, 128), F32), vm((3 * chan, hv), BF16), vm((2 * rows_b, width), BF16), vm((own, width), BF16), vm((sets, length, width), BF16),
+        vm((total * 4, 128), F32), vm((total * 4, 128), F32), vm((total * 4, 128), F32), vm((total // 2, 128), F32),
+    ]
+    scratch += [vm((3, 2, 64, 128), BF16)] * 2 + [vm((2, 3, 2, 64, 128), BF16)] * 2
+    scratch += [vm((2, 3, 64, 128), BF16), vm((nq + 1, 3, 64, 128), BF16)]
+    scratch += [dma((16,)), dma((n - 1,)), dma((n - 1,)), dma((n - 1,)), dma((n - 1,))]
+    scratch += gather_sems(nq)
+    scratch += [dma((2,)), dma((2,)), dma((nq - 1,)), dma((nq - 1,)), dma((nq - 1,)), dma((1,))]
     return pl.pallas_call(
-        functools.partial(forward_exchange, n, groups),
-        out_shape=jax.ShapeDtypeStruct((9, 64, 128), F32),
-        in_specs=[VMEM, VMEM, VMEM, SMEM],
-        out_specs=VMEM,
-        scratch_shapes=[
-            pltpu.VMEM((3, 2, 64, 128), BF16), pltpu.VMEM((3, 2, 64, 128), BF16),
-            pltpu.VMEM((2, 3, 2, 64, 128), BF16), pltpu.VMEM((2, 3, 2, 64, 128), BF16),
-            pltpu.VMEM((2, 3, 64, 128), BF16), pltpu.VMEM((nq + 1, 3, 64, 128), BF16),
-            dma((2,)), dma((2,)), dma((nq - 1,)), dma((nq - 1,)), dma((nq - 1,)), dma((1,)),
-        ],
-        compiler_params=pltpu.CompilerParams(collective_id=1, has_side_effects=True, vmem_limit_bytes=40 << 20),
-        name="forward_exchange",
-    )(finals, ab, decays, sel)
-
-
-def tail_flow(me, t, r1, w1, r2, w2, r3, out, send, recv):
-    nq = me.nq
-    last = me.q == nq - 1
-    out[...] = jnp.zeros_like(out)
-    copy1 = remote(t.at[:, 1 - me.c], r1, send.at[0], recv.at[0], me.core)
-    copy1.start()
-    yield
-    copy1.wait()
-    for i in range(2):
-        w1[i] = (t[i, me.c].astype(F32) + r1[i].astype(F32)).astype(BF16)
-    copy2 = remote(w1.at[1 - me.y], r2, send.at[1], recv.at[1], me.side)
-    copy2.start()
-    yield
-    copy2.wait()
-    w2[...] = (w1[me.y].astype(F32) + r2[...].astype(F32)).astype(BF16)
-    top = (me.g, (nq - 1) * 4 + me.pos)
-    end = (me.g, nq * 4 - 1)
-    for k in range(nq - 1):
-        @pl.when(me.q == k)
-        def _():
-            remote(w2, r3.at[k], send.at[2], recv.at[2 + k], top).start()
-    yield
-
-    @pl.when(last)
-    def _():
-        total = w2[...].astype(F32)
-        for k in range(nq - 1):
-            remote(r3.at[k], r3.at[k], send.at[2], recv.at[2 + k], me.core).wait_recv()
-            total = total + r3[k].astype(F32)
-        w2[...] = total.astype(BF16)
-
-        @pl.when(jnp.logical_not(me.is_last))
-        def _():
-            for j in range(3):
-                @pl.when(me.pos == j)
-                def _():
-                    remote(w2, out.at[j // 2, j % 2], send.at[2], recv.at[nq + 1 + j], end).start()
-
-        @pl.when(me.is_last)
-        def _():
-            out[1, 1] = w2[...]
-    yield
-
-    @pl.when(me.is_last)
-    def _():
-        for j in range(3):
-            dst = out.at[j // 2, j % 2]
-            remote(dst, dst, send.at[2], recv.at[nq + 1 + j], me.core).wait_recv()
-
-    @pl.when(jnp.logical_not(me.is_last))
-    def _():
-        remote(w2, w2, send.at[2], recv.at[2], me.core).wait_send()
-
-
-def tail_scratch(nq, rows, width):
-    return [
-        pltpu.VMEM((2, rows, width), BF16), pltpu.VMEM((2, rows, width), BF16),
-        pltpu.VMEM((rows, width), BF16), pltpu.VMEM((rows, width), BF16),
-        pltpu.VMEM((nq - 1, rows, width), BF16),
-    ]
-
-
-def ema_call(kernel, name, outs, ins, scratch=()):
-    return pl.pallas_call(
-        kernel,
-        out_shape=[jax.ShapeDtypeStruct(shape, F32) for shape in outs],
-        in_specs=[VMEM] * len(ins),
-        out_specs=[VMEM] * len(outs),
+        functools.partial(front_kernel, n, groups),
+        out_shape=outs,
+        in_specs=[VMEM] * 10 + [SMEM] + [HBM] * 7,
+        out_specs=[VMEM] * 7 + [HBM] * 6,
         scratch_shapes=scratch,
-        compiler_params=pltpu.CompilerParams(vmem_limit_bytes=56 << 20),
-        name=name,
-    )(*ins)
-
-
-def local_pass_call(rows, backward, x, dec):
-    def kernel(x_ref, d_ref, inner_ref, final_ref):
-        ema_local_pass(rows, (0, 1, rows), x_ref, d_ref.at[0], d_ref.at[1], d_ref.at[2], d_ref.at[3], inner_ref, final_ref, backward)
-
-    return ema_call(kernel, "ema_local", [(rows * 512, 128), (rows * 64, 128)], (x, dec))
-
-
-def apply_pass_call(rows, x, dec, mix, omega, power, inner, start):
-    def kernel(x_ref, d_ref, mix_ref, omega_ref, power_ref, inner_ref, start_ref, y_ref):
-        ema_apply_pass(rows, x_ref, d_ref.at[0], mix_ref, omega_ref, power_ref, inner_ref, start_ref, y_ref)
-
-    return ema_call(kernel, "ema_apply", [(rows * 512, 128)], (x, dec, mix, omega, power, inner, start))[0]
+        compiler_params=pltpu.CompilerParams(collective_id=0, has_side_effects=True, vmem_limit_bytes=60 << 20),
+        name="front",
+    )(*rates, *vectors, resumed, tokens, *weights)
 
 
 def silu_grad(pre_act):
@@ -626,7 +808,7 @@
 
     def set_step(p, carry):
         here = pl.ds(pl.multiple_of(p * 2 * length, 2 * length), 2 * length)
-        m = target[p]
+        m = target[0, p * (n // 4) + lax.axis_index("seq") // 4]
         x = tok[here, :].astype(F32)
         plain, _ = norm_rows(x)
         units = (plain * gain_one).astype(BF16)
@@ -759,8 +941,8 @@
     own, width = tok.shape
     rows_t = tail.shape[0]
     total = own + rows_t
-    sets = target.shape[0]
-    length = rows_t // sets
+    length = 128
+    sets = rows_t // length
     hv = mats_a.shape[2]
     chan = mats_a.shape[1] // 3
     rows_b = mats_b.shape[1] // 2
@@ -787,7 +969,7 @@
     return pl.pallas_call(
         functools.partial(dense_kernel, n),
         out_shape=outs,
-        in_specs=[VMEM] * 4 + [ANY] * 2 + [VMEM] * 3 + [SMEM],
+        in_specs=[VMEM] * 4 + [HBM] * 2 + [VMEM] * 3 + [SMEM],
         out_specs=[VMEM] * len(outs),
         scratch_shapes=scratch,
         compiler_params=pltpu.CompilerParams(vmem_limit_bytes=60 << 20),
@@ -926,7 +1108,7 @@
     ]
 
 
-def adjoint_flow(me, f_ref, tabs, sel_ref, s_ref, m0, r0, m1, r1, m2, r2, ss, rs, zs, zr):
+def adjoint_flow(me, f_ref, tabs, sel, s_ref, m0, r0, m1, r1, m2, r2, ss, rs, zs, zr):
     nq = me.nq
     one, two, three, four = tabs[4], tabs[5], tabs[6], tabs[7]
     mine = f_ref[...].reshape(3, 2, 64, 128)
@@ -953,7 +1135,7 @@
     after = jnp.where(upper_side, 0.0, jnp.where(upper_core, far, one * far)) + after
     m2[0] = total[:, 0].astype(BF16)
     for m in range(3):
-        m2[1, m] = (sel_ref[m] * total[0, 1] + sel_ref[3 + m] * total[1, 1] + sel_ref[6 + m] * total[2, 1]).astype(BF16)
+        m2[1, m] = (sel(0, m) * total[0, 1] + sel(1, m) * total[1, 1] + sel(2, m) * total[2, 1]).astype(BF16)
     sends = []
     for k in range(1, nq):
         copy = remote(m2, r2.at[me.q], zs.at[k - 1], zr.at[k - 1], me.at_quad(me.quad(k)))
@@ -1008,8 +1190,8 @@
         del refs[:count]
         return got
 
-    base, slope_s, shared, t_keys, w_shared, tabs, power, power_rev, vec_wide, vec_head, starts, sum_wide, sum_head, sel = take(14)
-    h_act, h_ema, h_x, h_inner, h_units, h_middle, h_tokens = take(7)
+    base, slope_s, shared, t_keys, w_shared, tabs, power, power_rev, vec_wide, vec_head, starts, sum_wide, sum_head, resumed = take(14)
+    h_act, h_ema, h_x, h_inner, h_units, h_middle, h_tokens, h_tail = take(8)
     grads = take(N_BIG)
     (input_grad,) = take(1)
     outs = take(N_BIG)
@@ -1032,8 +1214,10 @@
     count = own // length
     lanes = width // 128
     chan = width // n
-    hbm = [h_act, h_ema, h_x, h_inner, h_units, h_middle, h_tokens]
-    arrive = [pltpu.make_async_copy(src, dst, load_sem.at[i]) for i, (src, dst) in enumerate(zip(hbm, loads))]
+    sel = chosen(resumed, me)
+    hbm = [h_act, h_ema, h_x, h_inner, h_units, h_middle, h_tokens, h_tail]
+    places = loads[:6] + [tokens.at[0:own], tokens.at[own:total]]
+    arrive = [pltpu.make_async_copy(src, dst, load_sem.at[i]) for i, (src, dst) in enumerate(zip(hbm, places))]
     for copy in arrive:
         copy.start()
     meet(me.group_peers() + [me.cross_bit(bit) for bit in me.cross_bits()])
@@ -1104,6 +1288,7 @@
     steps(2, 3)
     arrive[4].wait()
     arrive[6].wait()
+    arrive[7].wait()
     piece = (total - own) // 4
     for part in range(4):
         t_grad[part // 2, part % 2] = norm_rows_back(own + part * piece, piece, None).astype(BF16)
@@ -1197,12 +1382,13 @@
     dma = pltpu.SemaphoreType.DMA
     vm = pltpu.VMEM
     shape = jax.ShapeDtypeStruct
-    own, total, width = ins[0].shape[0], hbm[6].shape[0], hbm[6].shape[1]
+    own, width = hbm[6].shape
+    total = own + hbm[7].shape[0]
     chan = width // n
     small_rows = 2 * chan + 16
     piece = (total - own) // 4
     outs = [shape((own, width), BF16)] + [shape(grad.shape[-2:], BF16) for grad in grads] + [shape((small_rows, 128), BF16)]
-    scratch = [vm(part.shape, part.dtype) for part in hbm]
+    scratch = [vm(part.shape, part.dtype) for part in hbm[:6]] + [vm((total, width), BF16)]
     scratch += [
         vm((own * 4, 128), F32), vm((own, width), BF16), vm((own, 128), BF16), vm((own * 4, 128), F32),
         vm((own // 2, 128), F32), vm((own // 2, 128), F32), vm((own * 4, 128), F32), vm((64, 128), F32), vm((64, 128), F32),
@@ -1218,13 +1404,13 @@
     sems = nq + 3 + max(groups.bit_length() - 2, 1)
     small_sems = 2 * nq + groups.bit_length() - 1
     scratch += [
-        dma((7,)), dma((N_BIG, sems)), dma((N_BIG, sems)), dma((N_BIG,)), dma((small_sems,)), dma((small_sems,)),
+        dma((8,)), dma((N_BIG, sems)), dma((N_BIG, sems)), dma((N_BIG,)), dma((small_sems,)), dma((small_sems,)),
         dma((3,)), dma((nq + 4,)), dma((3,)), dma((nq + 4,)), dma((2,)), dma((2,)), dma((nq - 1,)), dma((nq - 1,)),
     ]
     return pl.pallas_call(
         functools.partial(back_kernel, n, groups),
         out_shape=outs,
-        in_specs=[VMEM] * 13 + [SMEM] + [ANY] * (7 + N_BIG),
+        in_specs=[VMEM] * 13 + [SMEM] + [HBM] * (8 + N_BIG),
         out_specs=[VMEM] * len(outs),
         scratch_shapes=scratch,
         compiler_params=pltpu.CompilerParams(collective_id=2, has_side_effects=True, vmem_limit_bytes=60 << 20),
@@ -1232,16 +1418,39 @@
     )(*ins, *hbm, *grads)
 
 
-def lanes_first(rows):
-    return rows.reshape(-1, 4, 128).transpose(1, 0, 2).reshape(-1, 128)
-
-
-def rows_first(lanes):
-    return lanes.reshape(4, -1, 128).transpose(1, 0, 2).reshape(-1, 512)
-
-
-def dot(lhs, rhs, dims):
-    return lax.dot_general(lhs, rhs, ((dims[:1], dims[1:]), ((), ())), preferred_element_type=F32)
+def finish_kernel(heads, grad_in, *refs):
+    sums, small, grad_out = refs[:N_BIG], refs[N_BIG], refs[N_BIG + 1]
+    outs = refs[N_BIG + 2 : 2 * N_BIG + 2]
+    shared, rates, vecs = refs[2 * N_BIG + 2], refs[2 * N_BIG + 3 : 2 * N_BIG + 7], refs[2 * N_BIG + 7 : 2 * N_BIG + 13]
+    grad_out[...] = grad_in[...]
+    for src, dst in zip(sums, outs):
+        dst[...] = src[...].astype(F32)
+    chan = shared.shape[0]
+    shared[...] = small[chan : 2 * chan].astype(F32)
+    block = small[0:chan].astype(F32).T
+    for i, ref in enumerate(rates):
+        ref[...] = block[16 * i : 16 * i + 16]
+    for i in range(3):
+        vecs[i][...] = block[64 + i : 65 + i]
+    mine = lax.axis_index("seq") * heads
+    rows = pltpu.roll(small[2 * chan : 2 * chan + 16].astype(F32), (128 - mine) % 128, 1)
+    for i in range(3):
+        vecs[3 + i][...] = rows[i : i + 1, 0:heads]
+
+
+def finish_call(n, heads, input_grad, sums, small):
+    shape = jax.ShapeDtypeStruct
+    chan = (small.shape[0] - 16) // 2
+    outs = [shape(input_grad.shape, BF16)] + [shape(part.shape, F32) for part in sums] + [shape((chan, 128), F32)]
+    outs += [shape((16, chan), F32)] * 4 + [shape((1, chan), F32)] * 3 + [shape((1, heads), F32)] * 3
+    return pl.pallas_call(
+        functools.partial(finish_kernel, heads),
+        out_shape=outs,
+        in_specs=[VMEM] * (N_BIG + 2),
+        out_specs=[VMEM] * len(outs),
+        compiler_params=pltpu.CompilerParams(vmem_limit_bytes=60 << 20),
+        name="finish",
+    )(input_grad, *sums, small)
 
 
 def local(
@@ -1255,93 +1464,42 @@
     sets, kinds, length, width = hidden_in.shape[1:]
     chan = width // n
     heads = query_scale.shape[0]
-    tokens_low = hidden_in[0]
-    vectors = jnp.stack((query_scale, query_shift, key_scale), axis=1)
-    small = jnp.concatenate(
-        (
-            ema_alpha, ema_delta, ema_beta, ema_eta, ema_omega[:, None], norm_gain[:, None], ffn_gain[:, None],
-            jnp.pad(vectors, ((0, chan - heads), (0, 0))), jnp.zeros((chan, 58), BF16),
-        ),
-        axis=1,
+    own_rows = sets * kinds * length
+    vectors = (norm_gain, ffn_gain, ema_omega, query_scale, query_shift, key_scale)
+    (
+        tabs, power, power_rev, vec_wide, vec_head, starts, mat_shared, ema_lanes, x_lanes, inner, all_a, all_b, tail_low,
+    ) = front_call(
+        n, groups, [part.T for part in (ema_alpha, ema_delta, ema_beta, ema_eta)], [part[None] for part in vectors],
+        cont_prompt, hidden_in[0],
+        (value_proj, reset_proj, inner_proj, hidden_proj, outer_proj, shared_proj),
     )
-    small = jnp.concatenate((small, shared_proj), axis=0)
-    mat_a = jnp.concatenate((value_proj, reset_proj, inner_proj), axis=0)
-    mat_b = jnp.concatenate((hidden_proj, outer_proj), axis=0)
-    rows_b = hidden_proj.shape[0]
-    all_small, all_a, all_b, tail_low = gather_call(
-        n, groups, small, mat_a, mat_b, tokens_low[:, 0].reshape(4, sets * length // 4, width)
-    )
-    mat_shared = all_small[:, chan:].reshape(width, 128)
-    flat = all_small[:, :chan].astype(F32)
-    table = flat.reshape(width, 128).T
-    vecs = flat[:, :heads, 67:70].reshape(-1, 3)
-    query_mul, query_add, key_mul = vecs[:, 0], vecs[:, 1], vecs[:, 2]
-
-    def by_lane(part):
-        return part.reshape(16, 4, 128).transpose(1, 0, 2).reshape(64, 128)
-
-    alpha, delta, beta, eta = (by_lane(table[16 * i : 16 * i + 16]) for i in range(4))
-    omega, gain_one, gain_two = table[64], table[65], table[66]
-    omega_lanes = omega.reshape(4, 128)
-    decay = 1.0 - alpha * delta
-    decay2 = decay * decay
-    decay4 = decay2 * decay2
-    decay8 = decay4 * decay4
-    decay16 = decay8 * decay8
-    decay32 = decay16 * decay16
-    decay64 = decay32 * decay32
-    decay128 = decay64 * decay64
-    decay256 = decay128 * decay128
-    dec = jnp.stack((decay, decay16, decay32, decay64))
-    far = jnp.stack((decay128, decay256, decay256 * decay128, decay256 * decay256))
-    steps = [jnp.ones_like(decay), decay16, decay32, decay32 * decay16, decay64, decay64 * decay16, decay64 * decay32, decay64 * decay32 * decay16]
-    power = jnp.stack(steps, axis=1).reshape(512, 128)
-    power_rev = jnp.stack(steps[::-1], axis=1).reshape(512, 128)
-    ab = alpha * beta
-    mix = ab * eta
-    targets = lax.dynamic_slice_in_dim(
-        cont_prompt[0].reshape(sets, nq), seq_index // 4, 1, 1
-    )[:, 0]
-    select = (targets[:, None] == jnp.arange(sets, dtype=jnp.int32)[None, :]).astype(F32)
-    sel = select.reshape(-1)
-    own_rows = sets * kinds * length
-    rows_low = jnp.concatenate((tokens_low.reshape(own_rows, width), tail_low.reshape(-1, width)), axis=0)
-    tokens = rows_low.astype(F32)
-    plain_in, inv_in = norm_rows(tokens)
-    normed = plain_in * gain_one
-    x_lanes = lanes_first(normed)
-    inner, finals = local_pass_call(9, False, x_lanes, dec)
-    starts = forward_exchange_call(n, groups, finals[: 6 * 64].reshape(3, 2, 64, 128), ab, far, sel)
-    starts = starts.reshape(9 * 64, 128)
-    ema_lanes = apply_pass_call(9, x_lanes, dec, mix, omega_lanes, power, inner, starts)
+    mat_shared = mat_shared.reshape(width, 128)
+    own_low, tail_low = hidden_in[0].reshape(own_rows, width), tail_low.reshape(-1, width)
     grad_outer = cotangent[0].reshape(own_rows, width)
-    vec_wide = jnp.pad(jnp.stack((gain_one, gain_two)), ((0, 6), (0, 0)))
-    vec_head = jnp.concatenate((jnp.stack((query_mul, query_add, key_mul, key_mul)), omega_lanes), axis=0)
     (
         result, grad_middle, grad_act, grad_base, slope_shared, shared, grad_units, sum_outer, sum_inner, sum_hidden,
         sum_reset, sum_value, sent_keys, sum_wide, sum_head,
     ) = dense_call(
-        n, rows_low[:own_rows], rows_low[own_rows:], ema_lanes, grad_outer, all_a, all_b, mat_shared, vec_wide, vec_head, targets
+        n, own_low, tail_low, ema_lanes, grad_outer, all_a, all_b, mat_shared, vec_wide, vec_head, cont_prompt
     )
-    tabs = jnp.concatenate((dec, far, jnp.stack((mix, alpha, beta, delta, eta, ab))))
 
     def shards(grad):
         return grad.reshape(nq, 2, 2, -1, grad.shape[-1])
 
     ins = (
         grad_base, slope_shared, shared, sent_keys.reshape(2, 2, -1, 128), mat_shared, tabs, power, power_rev, vec_wide,
-        vec_head, starts, sum_wide, sum_head, sel,
+        vec_head, starts, sum_wide, sum_head, cont_prompt,
     )
-    hbm = (grad_act, ema_lanes, x_lanes, inner[: own_rows * 4], grad_units, grad_middle, rows_low)
+    hbm = (grad_act, ema_lanes, x_lanes, inner, grad_units, grad_middle, own_low, tail_low)
     grads = [shards(part) for part in (sum_outer, sum_inner, sum_hidden, sum_reset, sum_value)]
     input_grad, *sums, d_small = back_call(n, groups, ins, hbm, grads)
-    d_outer, d_inner, d_hidden, d_reset, d_value, d_small = [part.astype(F32) for part in (*sums, d_small)]
-    d_heads = lax.dynamic_slice(d_small, (2 * chan, seq_index * heads), (3, heads))
+    wide = finish_call(n, heads, input_grad, sums, d_small)
+    input_grad, d_outer, d_inner, d_hidden, d_reset, d_value, d_shared = wide[:7]
+    rates = [part.T for part in wide[7:11]]
+    vecs = [part.reshape(part.shape[1]) for part in wide[11:17]]
     return (
-        result.reshape(hidden_in.shape), input_grad.reshape(hidden_in.shape), d_value, d_small[chan : 2 * chan], d_reset,
-        d_hidden, d_inner, d_outer, d_small[:chan, 0:16], d_small[:chan, 16:32], d_small[:chan, 32:48],
-        d_small[:chan, 48:64], d_small[:chan, 64], d_small[:chan, 65], d_small[:chan, 66],
-        d_heads[0], d_heads[1], d_heads[2],
+        result.reshape(hidden_in.shape), input_grad.reshape(hidden_in.shape), d_value, d_shared, d_reset, d_hidden, d_inner,
+        d_outer, *rates, *vecs,
     )
 
 

time: 245 us -> 175 us (0.71)
  local copies, waits for them, and re-layouts: 26.3 us -> 0 us
  Pallas kernels: 196 us -> 174 us
  other arithmetic: 20.6 us -> 0 us
    pallas_call x4 -> x2, Pallas kernels: 85.9 us -> 62.1 us  [the longest x1 59.7 us: front_call(): pl.pallas_call(functools.partial(front_kernel, n, groups), out_shape=outs...]
    unnamed x41 -> x0, local copies, waits for them, and re-layouts: 9.37 us -> none
    convert_element_type x7 -> x0, other arithmetic: 8.32 us -> none  [the longest x6 8.25 us: local(): part.astype(F32)]
    slice x8 -> x0, local copies, waits for them, and re-layouts: 7.6 us -> none  [the longest x1 1.77 us: local(): tokens_low[:, 0].reshape(4, sets * length // 4, width)]
    concatenate x4 -> x0, other arithmetic: 5.56 us -> none  [the longest x1 1.59 us: local(): mat_a = jnp.concatenate((value_proj, reset_proj, inner_proj), axis=0)]
    another operation x8 -> x0, local copies, waits for them, and re-layouts: 4.18 us -> none  [the longest x3 2.3 us: local(): vectors = jnp.stack((query_scale, query_shift, key_scale), axis=1)]
    mul x4 -> x0, other arithmetic: 2.54 us -> none  [the longest x1 1.89 us: local(): normed = plain_in * gain_one]
where the time goes in v2:
time: 175 us
  Pallas kernels  174 us (99%)
    pallas_call x1, Pallas kernels, back_call(): pl.pallas_call(functools.partial(back_kernel, n, groups), out_shape=outs,...  76.6 us
    pallas_call x1, Pallas kernels, front_call(): pl.pallas_call(functools.partial(front_kernel, n, groups), out_shape=outs...  59.7 us
    pallas_call x1, Pallas kernels, dense_call(): pl.pallas_call(functools.partial(dense_kernel, n), out_shape=outs, in_spe...  35.1 us

profile of v2, /device:TPU:0, one launch (start us, length us, event | category | flops | bytes accessed | tf_op | source)
XLA Modules:
  0.0 174.6 jit_solution(7667155370750304928)
XLA Ops:
  0.7 59.7 %front.1 = (f32[14,64,128]{2,1,0:T(8,128)}, f32[512,128]{1,0:T(8,128)}, f32[512,128]{1,0:T(8,128)}, f32[8,512]{1,0:T(8,128)}, f32[8,128]{1,0:T(8,128)}, /*index=...) custom-call(bf16[16,32]{1,0:T(8,128)(2,1)} %bitcast.47, ...), custom_call_target="tpu_custom_call" | custom-call | tf_op jit(solution)/shard_map/front/pallas_call | solution.py:690
  60.4 35.1 %dense.1 = (bf16[768,512]{1,0:T(8,128)(2,1)}, f32[768,512]{1,0:T(8,128)}, f32[768,512]{1,0:T(8,128)}, f32[768,128]{1,0:T(8,128)}, f32[768,128]{1,0:T(8,128)}, /*...) custom-call(bf16[768,512]{1,0:T(8,128)(2,1)} %bitcast.34, ...), custom_call_target="tpu_custom_call" | custom-call | tf_op jit(solution)/shard_map/dense/pallas_call | solution.py:969
  95.5 76.6 %back.1 = (bf16[768,512]{1,0:T(8,128)(2,1)}, bf16[64,512]{1,0:T(8,128)(2,1)}, bf16[32,1024]{1,0:T(8,128)(2,1)}, bf16[64,512]{1,0:T(8,128)(2,1)}, bf16[32,1024]{1...) custom-call(f32[768,128]{1,0:T(8,128)} %get-tuple-element.78.refs_0_, ...), custom_call_target="tpu_custom_call" | custom-call | tf_op jit(solution)/shard_map/back/pallas_call | solution.py:1410
  172.1 2.4 %finish.1 = (bf16[768,512]{1,0:T(8,128)(2,1)}, f32[64,512]{1,0:T(8,128)}, f32[32,1024]{1,0:T(8,128)}, f32[64,512]{1,0:T(8,128)}, f32[32,1024]{1,0:T(8,128)}, /*i...) custom-call(bf16[768,512]{1,0:T(8,128)(2,1)} %get-tuple-element.98.g, ...), custom_call_target="tpu_custom_call" | custom-call | tf_op jit(solution)/shard_map/finish/pallas_call | solution.py:1446

commit v3 on v2

--- a/solution.py
+++ b/solution.py
@@ -298,43 +298,24 @@
         post.got(out.at[(me.s + me.n - k) % me.n], sr.at[k - 1])
 
 
-def gather_flow(me, post, a_own, b_own, a_out, b_out, x_in, x_out, zs, zr, ys, yr, xs, xr, cs, cr, ts, tr, local_sem):
+def gather_flow(me, post, mats, zs, zr, ys, yr, xs, xr, cs, cr):
     nq = me.nq
-    mats = ((a_out, a_out.shape[-1] // 2), (b_out, b_out.shape[-1] // 2))
+    mats = [(own, out, out.shape[-1] // 2) for own, out in mats]
     other = 1 - me.x
-    piece_rows = x_out.shape[1] // 4
 
     def half(ref, width, which):
         return ref.at[:, pl.ds(pl.multiple_of(which * width, 128), width)]
 
-    def quarter(ref, pos):
-        return ref.at[:, pl.ds(pl.multiple_of(pos * piece_rows, piece_rows), piece_rows)]
-
     up, down = (me.g, me.s + 4), (me.g, me.s - 4)
     has_up, has_down = me.q < nq - 1, me.q > 0
-    ours = (a_own, b_own)
-    for i, (w_out, width) in enumerate(mats):
-        piece, place = half(ours[i], width, me.x), half(w_out.at[me.s], width, me.x)
+    for i, (own, out, width) in enumerate(mats):
+        piece, place = half(own, width, me.x), half(out.at[me.s], width, me.x)
         post.send(piece, place, zs.at[0, 0, i], zr.at[0, 0, i], up, has_up)
         post.send(piece, place, zs.at[1, 0, i], zr.at[1, 0, i], down, has_down)
-        post.send(ours[i], w_out.at[me.s], ys.at[0, i], yr.at[0, i], me.side)
-    for i, (w_out, width) in enumerate(mats):
-        post.send(ours[i], w_out.at[me.s], cs.at[0, i], cr.at[0, i], me.core)
-    in_last = me.q == nq - 1
-    keep = pltpu.make_async_copy(quarter(x_in, me.pos), quarter(x_out, me.pos), local_sem)
-    pl.when(me.is_last)(keep.start)
-    for j in range(3):
-        post.send(quarter(x_in, j), quarter(x_out, j), ts.at[j], tr.at[0], (me.g, 4 * (nq - 1) + j), me.is_last)
-    yield
-
-    @pl.when(jnp.logical_and(in_last, jnp.logical_not(me.is_last)))
-    def _():
-        post.got(quarter(x_out, me.pos), tr.at[0])
-
-    pl.when(me.is_last)(keep.wait)
-    mine = quarter(x_out, me.pos)
-    for k in range(1, nq):
-        post.send(mine, mine, ts.at[2 + k], tr.at[1], me.at_quad(me.quad(k)), in_last)
+        post.send(own, out.at[me.s], ys.at[0, i], yr.at[0, i], me.side)
+    for i, (own, out, width) in enumerate(mats):
+        post.send(own, out.at[me.s], cs.at[0, i], cr.at[0, i], me.core)
+    yield
 
     def arrival(side, hop):
         there = me.q - hop if side == 0 else me.q + hop
@@ -343,7 +324,7 @@
 
         def pieces(pos, which):
             shard = jnp.clip(there, 0, nq - 1) * 4 + pos
-            return [half(w_out.at[shard], width, which) for w_out, width in mats]
+            return [half(out.at[shard], width, which) for _, out, width in mats]
 
         return here, jnp.logical_and(here, onward), to, pieces
 
@@ -361,16 +342,9 @@
             post.send(piece, piece, cs.at[1 + at, i], cr.at[1 + at, i], me.core, here)
         if side:
             yield
-
-    @pl.when(jnp.logical_not(in_last))
-    def _():
-        post.got(mine, tr.at[1])
-
-    post.send(mine, mine, ts.at[nq + 2], tr.at[2], me.side)
-    post.send(mine, mine, ts.at[nq + 3], tr.at[3], me.core)
     count = len(arrivals)
-    for i, (w_out, width) in enumerate(mats):
-        block = w_out.at[me.q * 4 + side_pos]
+    for i, (_, out, _) in enumerate(mats):
+        block = out.at[me.q * 4 + side_pos]
         post.got(block, yr.at[0, i])
         post.send(block, block, cs.at[1 + count, i], cr.at[1 + count, i], me.core)
     for hop, side in arrivals:
@@ -382,13 +356,7 @@
             post.send(piece, piece, cs.at[2 + count + at, i], cr.at[2 + count + at, i], me.core, here)
         if side:
             yield
-    theirs = quarter(x_out, side_pos)
-    post.got(theirs, tr.at[2])
-    post.send(theirs, theirs, ts.at[nq + 4], tr.at[4], me.core)
     flip = 1 - 2 * me.c
-    post.got(quarter(x_out, me.pos + flip), tr.at[3])
-    post.got(quarter(x_out, side_pos + flip), tr.at[4])
-    yield
     for group, pos in ((0, me.pos), (1, side_pos)):
         for hop, side in arrivals:
             here, _, _, pieces = arrival(side, hop)
@@ -399,8 +367,8 @@
                 post.send(piece, piece, cs.at[to, i], cr.at[to, i], me.core, here)
         yield
     for group, pos in ((0, me.pos + flip), (1, side_pos + flip)):
-        for i, (w_out, width) in enumerate(mats):
-            post.got(w_out.at[me.q * 4 + pos], cr.at[group * (1 + count), i])
+        for i, (_, out, _) in enumerate(mats):
+            post.got(out.at[me.q * 4 + pos], cr.at[group * (1 + count), i])
         for hop, side in arrivals:
             here, _, _, pieces = arrival(side, hop)
             at = (hop - 1) * 2 + side
@@ -410,9 +378,49 @@
                 pl.when(here)(functools.partial(post.got, piece, cr.at[2 + 2 * count + group * count + at, i]))
 
 
-def gather_sems(nq):
+def tokens_flow(me, post, x_in, x_out, ts, tr, local_sem):
+    nq = me.nq
+    rows = x_out.shape[1] // 4
+
+    def quarter(ref, pos):
+        return ref.at[:, pl.ds(pl.multiple_of(pos * rows, rows), rows)]
+
+    in_last = me.q == nq - 1
+    side_pos, flip = me.pos + 2 - 4 * me.y, 1 - 2 * me.c
+    keep = pltpu.make_async_copy(quarter(x_in, me.pos), quarter(x_out, me.pos), local_sem)
+    pl.when(me.is_last)(keep.start)
+    for j in range(3):
+        post.send(quarter(x_in, j), quarter(x_out, j), ts.at[j], tr.at[0], (me.g, 4 * (nq - 1) + j), me.is_last)
+    yield
+
+    @pl.when(jnp.logical_and(in_last, jnp.logical_not(me.is_last)))
+    def _():
+        post.got(quarter(x_out, me.pos), tr.at[0])
+
+    pl.when(me.is_last)(keep.wait)
+    mine = quarter(x_out, me.pos)
+    for k in range(1, nq):
+        post.send(mine, mine, ts.at[2 + k], tr.at[1], me.at_quad(me.quad(k)), in_last)
+    yield
+
+    @pl.when(jnp.logical_not(in_last))
+    def _():
+        post.got(mine, tr.at[1])
+
+    post.send(mine, mine, ts.at[nq + 2], tr.at[2], me.side)
+    post.send(mine, mine, ts.at[nq + 3], tr.at[3], me.core)
+    yield
+    theirs = quarter(x_out, side_pos)
+    post.got(theirs, tr.at[2])
+    post.send(theirs, theirs, ts.at[nq + 4], tr.at[4], me.core)
+    yield
+    post.got(quarter(x_out, me.pos + flip), tr.at[3])
+    post.got(quarter(x_out, side_pos + flip), tr.at[4])
+
+
+def gather_sems(nq, mats):
     count = 2 * (nq - 1)
-    shapes = [(2, nq - 1, 2)] * 2 + [(1 + count, 2)] * 2 + [(2 * count, 2)] * 2 + [(2 + 4 * count, 2)] * 2 + [(nq + 5,), (5,)]
+    shapes = [(2, nq - 1, mats)] * 2 + [(1 + count, mats)] * 2 + [(2 * count, mats)] * 2 + [(2 + 4 * count, mats)] * 2
     return [pltpu.SemaphoreType.DMA(shape) for shape in shapes]
 
 
@@ -495,7 +503,48 @@
             remote(m2.at[1], r2.at[nq], ps.at[k - 1], pr.at[0], me.at_quad(me.quad(k))).wait_send()
 
 
-def front_kernel(n, groups, *refs):
+def silu_grad(pre_act):
+    sigmoid_val = jax.nn.sigmoid(pre_act)
+    return sigmoid_val * (1.0 + pre_act * (1.0 - sigmoid_val))
+
+
+def norm_rows(row_data):
+    centered = row_data - jnp.mean(row_data, axis=-1, keepdims=True)
+    scale_inv = lax.rsqrt(jnp.mean(centered * centered, axis=-1, keepdims=True) + NORM_EPS)
+    return (centered * scale_inv, scale_inv)
+
+
+def norm_back(grad_rows, plain, scale_inv, gain_vec):
+    grad_norm = grad_rows * gain_vec
+    inner_term = (
+        grad_norm
+        - jnp.mean(grad_norm, axis=-1, keepdims=True)
+        - plain * jnp.mean(grad_norm * plain, axis=-1, keepdims=True)
+    )
+    return inner_term * scale_inv
+
+
+def nt(lhs, rhs):
+    return lax.dot_general(lhs, rhs, (((1,), (1,)), ((), ())), preferred_element_type=F32)
+
+
+def tn(lhs, rhs):
+    return lax.dot_general(lhs, rhs, (((0,), (0,)), ((), ())), preferred_element_type=F32)
+
+
+def nn(lhs, rhs):
+    return lax.dot_general(lhs, rhs, (((1,), (0,)), ((), ())), preferred_element_type=F32)
+
+
+def silu_pair(pre):
+    sig = jax.nn.sigmoid(pre)
+    return pre * sig, sig * (1.0 + pre * (1.0 - sig))
+
+
+CHUNK = 256
+
+
+def layer_kernel(n, groups, *refs):
     refs = list(refs)
 
     def take(count):
@@ -504,20 +553,29 @@
         return got
 
     p_rates, p_vecs, (resumed,) = take(4), take(6), take(1)
-    h_tokens, i_value, i_reset, i_inner, i_hidden, i_outer, i_shared = take(7)
+    cot, h_tokens, i_value, i_reset, i_inner, i_hidden, i_outer, i_shared = take(8)
     tabs, power, power_rev, vec_wide, vec_head, starts, w_shared = take(7)
-    o_ema, o_x, o_inner, a_out, b_out, x_out = take(6)
-    gathered, lift, a_own, b_own, tokens, tail, x_lanes, ema, inner, finals = take(10)
+    (
+        result, g_middle, g_act, g_base, slope_s, shared_out, g_units, o_outer, o_inner, o_hidden, o_reset, o_value,
+        tail_keys, sum_wide, sum_head,
+    ) = take(15)
+    o_ema, o_x, o_state, o_tail = take(4)
+    gathered, lift, tok, tail, x_lanes, ema, inner, finals = take(8)
+    early_own, hidden_own, inner_own, outer_own, early_all, w_hidden, w_inner, w_outer = take(8)
+    (
+        values, slope_v, t_values, t_slope, t_keys, t_dv, t_dk, k_units, k_activ, k_gated, k_mid, k_inner, k_branch, k_gin,
+        k_greset, k_gvalue, reset_pre, mixed, slope_i,
+    ) = take(19)
     exchange = take(6)
-    load_sem, ss, sr, hs, hr = take(5)
-    gather_sem = take(10)
+    load_sem, ss, sr, hs, hr, ts, tr = take(7)
+    early_sem, late_sem = take(8), take(8)
     ess, ers, ezs, ezr, eps, epr = take(6)
 
     me = Place(n, groups)
     length = 128
-    width = tokens.shape[1]
+    width = tok.shape[1]
     lanes = width // 128
-    own = tokens.shape[0]
+    own = tok.shape[0]
     total = own + tail.shape[0] * length
     count = own // length
     chan = width // n
@@ -533,14 +591,14 @@
 
     x_in = h_tokens.at[:, 0]
     packing = [
-        local_copy(i_value, a_own.at[0:chan], 0),
-        local_copy(i_reset, a_own.at[chan : 2 * chan], 1),
-        local_copy(i_inner, a_own.at[2 * chan : 3 * chan], 2),
-        local_copy(i_hidden, b_own.at[0:rows_b], 3),
-        local_copy(i_outer, b_own.at[rows_b : 2 * rows_b], 4),
+        local_copy(i_value, early_own.at[0:chan], 0),
+        local_copy(i_reset, early_own.at[chan : 2 * chan], 1),
+        local_copy(i_hidden, hidden_own, 2),
+        local_copy(i_inner, inner_own, 3),
+        local_copy(i_outer, outer_own, 4),
         local_copy(i_shared, w_shared.at[me.s], 5),
     ]
-    fetch = [local_copy(h_tokens.at[p, k], tokens.at[(p * 2 + k) * length : (p * 2 + k + 1) * length], 6 + p * 2 + k) for p in range(sets) for k in range(2)]
+    fetch = [local_copy(h_tokens.at[p, k], tok.at[(p * 2 + k) * length : (p * 2 + k + 1) * length], 6 + p * 2 + k) for p in range(sets) for k in range(2)]
     lift[...] = jnp.zeros_like(lift)
     block = jnp.zeros((16, 128), F32)
     for i, ref in enumerate(p_rates):
@@ -556,16 +614,21 @@
     small_gather(me, gathered, post, ss, sr)
     for copy in packing:
         copy.wait()
-    placing = [local_copy(a_own, a_out.at[me.s], 14), local_copy(b_own, b_out.at[me.s], 15)]
-    gather = gather_flow(me, post, a_own, b_own, a_out, b_out, x_in, x_out, *gather_sem, load_sem.at[13])
-    next(gather)
+    pairs = ((early_own, early_all), (hidden_own, w_hidden), (inner_own, w_inner), (outer_own, w_outer))
+    early = gather_flow(me, post, pairs[:1], *early_sem)
+    late = gather_flow(me, post, pairs[1:], *late_sem)
+    words = tokens_flow(me, post, x_in, tail, ts, tr, load_sem.at[13])
+    next(early)
+    next(words)
+    next(late)
+    placing = [local_copy(own_part, all_part.at[me.s], 14 + i) for i, (own_part, all_part) in enumerate(pairs)]
     small_gather(me, w_shared, post, hs, hr)
     for copy in fetch:
         copy.wait()
 
     def norm_step(row, carry):
         here = pl.ds(pl.multiple_of(row * length, length), length)
-        plain, _ = norm_rows(tokens[here, :].astype(F32))
+        plain, _ = norm_rows(tok[here, :].astype(F32))
         for lane in range(lanes):
             x_lanes[pl.ds(lane * total + row * length, length), :] = plain[:, lane * 128 : (lane + 1) * 128]
         return carry
@@ -618,29 +681,32 @@
     def apply_pass(first, many):
         ema_apply_pass(total // length, (first, many), x_lanes, tabs.at[0], tabs.at[8], vec_head, power, inner, starts, ema)
 
-    def more():
-        next(gather, None)
-
-    for part in range(2):
-        local_pass(part * (count // 2), count // 2)
-        more()
+    def step(*flows):
+        for flow in flows:
+            next(flow, None)
+
+    step(words, early)
+    local_pass(0, count // 2)
+    step(late, early)
+    local_pass(count // 2, count // 2)
     state = state_flow(me, finals, tabs, sel, starts, *exchange, ess, ers, ezs, ezr, eps, epr)
-    next(state)
-    keep = local_copy(inner.at[0 : own * 4], o_inner, 5)
-    more()
-    next(state)
-    more()
-    next(state)
-    more()
-    for _ in state:
-        pass
+    step(state)
+    keep = [local_copy(inner.at[0 : own * 4], o_state, 0)]
+    step(late, early)
+    step(state)
+    step(words, early, late)
+    step(state)
+    step(early, early)
+    step(state)
+    step(words)
     for part in range(3):
         apply_pass(part * (count // 3), count // 3)
-        if part < 2:
-            more()
-    bring = local_copy(x_out, tail, 6)
-    bring.wait()
-    small_arrive(me, w_shared, post, hr)
+        step(early)
+        if part:
+            step(late)
+    for _ in words:
+        pass
+    keep.append(local_copy(tail, o_tail, 1))
 
     def tail_norm(m, carry):
         plain, _ = norm_rows(tail[m].astype(F32))
@@ -651,120 +717,27 @@
 
     lax.fori_loop(0, sets, tail_norm, 0)
     local_pass(count, sets)
-    keep_x = local_copy(x_lanes, o_x, 7)
-    more()
+    keep.append(local_copy(x_lanes, o_x, 2))
+    step(late)
     apply_pass(count, sets)
-    keep_ema = local_copy(ema, o_ema, 8)
-    for _ in gather:
+    keep.append(local_copy(ema, o_ema, 3))
+    small_arrive(me, w_shared, post, hr)
+    for _ in early:
         pass
-    for copy in (keep, keep_x, keep_ema, *placing):
+    for copy in placing:
         copy.wait()
-    post.finish()
-
-
-def front_call(n, groups, rates, vectors, resumed, tokens, weights):
-    nq = n // 4
-    dma = pltpu.SemaphoreType.DMA
-    vm = pltpu.VMEM
-    shape = jax.ShapeDtypeStruct
-    sets, kinds, length, width = tokens.shape
-    own = sets * kinds * length
-    total = own + sets * length
-    chan, hv = weights[0].shape
-    rows_b = weights[3].shape[0]
-    outs = [
-        shape((14, 64, 128), F32), shape((512, 128), F32), shape((512, 128), F32), shape((8, width), F32), shape((8, 128), F32),
-        shape((total // 2, 128), F32), shape((n, chan, 128), BF16),
-        shape((total * 4, 128), F32), shape((total * 4, 128), F32), shape((own * 4, 128), F32),
-        shape((n, 3 * chan, hv), BF16), shape((n, 2 * rows_b, width), BF16), shape((sets, length, width), BF16),
-    ]
-    scratch = [
-        vm((n, 32, 128), BF16), vm((5, 16, 128), F32), vm((3 * chan, hv), BF16), vm((2 * rows_b, width), BF16), vm((own, width), BF16), vm((sets, length, width), BF16),
-        vm((total * 4, 128), F32), vm((total * 4, 128), F32), vm((total * 4, 128), F32), vm((total // 2, 128), F32),
-    ]
-    scratch += [vm((3, 2, 64, 128), BF16)] * 2 + [vm((2, 3, 2, 64, 128), BF16)] * 2
-    scratch += [vm((2, 3, 64, 128), BF16), vm((nq + 1, 3, 64, 128), BF16)]
-    scratch += [dma((16,)), dma((n - 1,)), dma((n - 1,)), dma((n - 1,)), dma((n - 1,))]
-    scratch += gather_sems(nq)
-    scratch += [dma((2,)), dma((2,)), dma((nq - 1,)), dma((nq - 1,)), dma((nq - 1,)), dma((1,))]
-    return pl.pallas_call(
-        functools.partial(front_kernel, n, groups),
-        out_shape=outs,
-        in_specs=[VMEM] * 10 + [SMEM] + [HBM] * 7,
-        out_specs=[VMEM] * 7 + [HBM] * 6,
-        scratch_shapes=scratch,
-        compiler_params=pltpu.CompilerParams(collective_id=0, has_side_effects=True, vmem_limit_bytes=60 << 20),
-        name="front",
-    )(*rates, *vectors, resumed, tokens, *weights)
-
-
-def silu_grad(pre_act):
-    sigmoid_val = jax.nn.sigmoid(pre_act)
-    return sigmoid_val * (1.0 + pre_act * (1.0 - sigmoid_val))
-
-
-def norm_rows(row_data):
-    centered = row_data - jnp.mean(row_data, axis=-1, keepdims=True)
-    scale_inv = lax.rsqrt(jnp.mean(centered * centered, axis=-1, keepdims=True) + NORM_EPS)
-    return (centered * scale_inv, scale_inv)
-
-
-def norm_back(grad_rows, plain, scale_inv, gain_vec):
-    grad_norm = grad_rows * gain_vec
-    inner_term = (
-        grad_norm
-        - jnp.mean(grad_norm, axis=-1, keepdims=True)
-        - plain * jnp.mean(grad_norm * plain, axis=-1, keepdims=True)
-    )
-    return inner_term * scale_inv
-
-
-def nt(lhs, rhs):
-    return lax.dot_general(lhs, rhs, (((1,), (1,)), ((), ())), preferred_element_type=F32)
-
-
-def tn(lhs, rhs):
-    return lax.dot_general(lhs, rhs, (((0,), (0,)), ((), ())), preferred_element_type=F32)
-
-
-def nn(lhs, rhs):
-    return lax.dot_general(lhs, rhs, (((1,), (0,)), ((), ())), preferred_element_type=F32)
-
-
-def silu_pair(pre):
-    sig = jax.nn.sigmoid(pre)
-    return pre * sig, sig * (1.0 + pre * (1.0 - sig))
-
-
-CHUNK = 256
-
-
-def dense_kernel(
-    n, tok, tail, ema, cot, mats_a, mats_b, w_shared, vec_wide, vec_head, target,
-    result, g_middle, g_act, g_base, slope_s, shared_out, g_units, o_outer, o_inner, o_hidden, o_reset, o_value,
-    tail_keys, sum_wide, sum_head,
-    w_value, w_reset, w_inner, w_hidden, w_outer, values, slope_v, t_values, t_slope, t_keys, t_dv, t_dk,
-    k_units, k_activ, k_gated, k_mid, k_inner, k_branch, k_gin, k_greset, k_gvalue, reset_pre, mixed, slope_i, sem,
-):
-    sets = t_keys.shape[0]
-    length = t_keys.shape[1]
-    own = tok.shape[0]
-    total = own + tail.shape[0]
-    width = tok.shape[1]
-    chan = w_value.shape[1]
-    rows_b = w_hidden.shape[1]
+    w_value, w_reset = early_all.at[:, 0:chan], early_all.at[:, chan : 2 * chan]
     hv = w_value.shape[2]
     parts = hv // CHUNK
     scale = 1.0 / math.sqrt(128.0)
-    copies = [
-        pltpu.make_async_copy(mats_a.at[:, 0:chan], w_value, sem.at[0]),
-        pltpu.make_async_copy(mats_a.at[:, chan : 2 * chan], w_reset, sem.at[1]),
-        pltpu.make_async_copy(mats_b.at[:, 0:rows_b], w_hidden, sem.at[2]),
-        pltpu.make_async_copy(mats_a.at[:, 2 * chan : 3 * chan], w_inner, sem.at[3]),
-        pltpu.make_async_copy(mats_b.at[:, rows_b : 2 * rows_b], w_outer, sem.at[4]),
-    ]
-    for copy in copies:
-        copy.start()
+
+    def ready(name):
+        if name == "hidden":
+            for _ in late:
+                pass
+        elif name in ("tail", "reset"):
+            step(late)
+
     gain_one, gain_two = vec_wide[0:1], vec_wide[1:2]
     q_mul, q_add, k_mul = vec_head[0:1], vec_head[1:2], vec_head[2:3]
     t_dv[...] = jnp.zeros_like(t_dv)
@@ -783,12 +756,9 @@
     def ema_rows(start, count):
         return jnp.concatenate([ema[pl.ds(lane * total + start, count), :] for lane in range(4)], axis=1)
 
-    copies[0].wait()
-
     def tail_step(m, carry):
         at = pl.multiple_of(m * length, length)
-        here = pl.ds(at, length)
-        plain, _ = norm_rows(tail[here, :].astype(F32))
+        plain, _ = norm_rows(tail[m].astype(F32))
         units = (plain * gain_one).astype(BF16)
         k_units[pl.ds(own + at, length), :] = units
         for part in range(parts):
@@ -797,18 +767,17 @@
             t_slope[m, :, part * CHUNK : (part + 1) * CHUNK] = slope.astype(BF16)
         pre = ema_rows(own + at, length)
         activ = (pre * jax.nn.sigmoid(pre)).astype(BF16)
-        shared = nn(activ, w_shared[...])
+        shared = nn(activ, w_shared[...].reshape(width, 128))
         t_keys[m] = (shared * jax.nn.sigmoid(shared) * k_mul).astype(BF16)
         return carry
 
     lax.fori_loop(0, sets, tail_step, 0)
-    for copy in copies[1:]:
-        copy.wait()
+    ready("tail")
     causal = lax.broadcasted_iota(jnp.int32, (length, length), 0) >= lax.broadcasted_iota(jnp.int32, (length, length), 1)
 
-    def set_step(p, carry):
+    def set_step(p, ready):
         here = pl.ds(pl.multiple_of(p * 2 * length, 2 * length), 2 * length)
-        m = target[0, p * (n // 4) + lax.axis_index("seq") // 4]
+        m = resumed[0, p * me.nq + me.q]
         x = tok[here, :].astype(F32)
         plain, _ = norm_rows(x)
         units = (plain * gain_one).astype(BF16)
@@ -818,10 +787,11 @@
             value, slope = silu_pair(nn(units, columns(w_value, part)))
             values[:, cut] = value.astype(BF16)
             slope_v[:, cut] = slope.astype(BF16)
+        ready("reset")
         pre = ema_rows(p * 2 * length, 2 * length)
         activ = (pre * jax.nn.sigmoid(pre)).astype(BF16)
         k_activ[here, :] = activ
-        shared, slope = silu_pair(nn(activ, w_shared[...]))
+        shared, slope = silu_pair(nn(activ, w_shared[...].reshape(width, 128)))
         slope_s[here, :] = slope
         shared_out[here, :] = shared
         queries = (shared * q_mul + q_add).astype(BF16)
@@ -848,15 +818,18 @@
             mixed[:, cut] = mix
             gate = reset_pre[:, cut]
             k_gated[here, cut] = (gate * jax.nn.sigmoid(gate) * mix).astype(BF16)
+        ready("hidden")
         middle = x + nn(k_gated[here, :], w_hidden[...].reshape(-1, width))
         plain_mid, inv_mid = norm_rows(middle)
         mid_low = (plain_mid * gain_two).astype(BF16)
         k_mid[here, :] = mid_low
+        ready("inner")
         for part in range(parts):
             cut = slice(part * CHUNK, (part + 1) * CHUNK)
             inner, slope = silu_pair(nn(mid_low, columns(w_inner, part)))
             k_inner[here, cut] = inner.astype(BF16)
             slope_i[:, cut] = slope
+        ready("outer")
         result[here, :] = (middle + nn(k_inner[here, :], w_outer[...].reshape(-1, width))).astype(BF16)
         top = cot[here, :]
         for part in range(parts):
@@ -880,7 +853,8 @@
             dp_c += nt(g_mix[length:], jnp.concatenate((t_values[m, :, cut], values[length:, cut]), axis=0))
             dv_p = tn(p_low, g_mix[:length])
             dv_c = tn(c_low, g_mix[length:])
-            t_dv[m, :, cut] += dv_c[:length]
+            for to in range(sets):
+                t_dv[to, :, cut] += sel(p, to) * dv_c[:length]
             dv = jnp.concatenate((dv_p, dv_c[length:]), axis=0)
             k_gvalue[here, cut] = (dv * slope_v[:, cut].astype(F32)).astype(BF16)
         g_act[here, :] = nt(k_greset[here, :], w_reset[...].reshape(width, -1))
@@ -891,15 +865,23 @@
         p_ds, c_ds = score_back(p_probs, dp_p), score_back(c_probs, dp_c)
         d_q = jnp.concatenate((nn(p_ds, p_k), nn(c_ds, jnp.concatenate((e_k, c_k), axis=0))), axis=0) * scale
         dk_c = tn(c_ds, c_q) * scale
-        t_dk[m] += dk_c[:length]
+        for to in range(sets):
+            t_dk[to] += sel(p, to) * dk_c[:length]
         d_k = jnp.concatenate((tn(p_ds, p_q) * scale, dk_c[length:]), axis=0)
         sum_head[0:1] += jnp.sum(d_q * shared, axis=0, keepdims=True)
         sum_head[1:2] += jnp.sum(d_q, axis=0, keepdims=True)
         sum_head[2:3] += jnp.sum(d_k * shared, axis=0, keepdims=True)
         g_base[here, :] = d_q * q_mul + d_k * k_mul
+
+    def quiet(name):
+        return None
+
+    def later_step(p, carry):
+        set_step(p, quiet)
         return carry
 
-    lax.fori_loop(0, sets, set_step, 0)
+    set_step(0, ready)
+    lax.fori_loop(1, sets, later_step, 0)
     tail_keys[...] = t_dk[...].astype(BF16)
 
     def tail_back(m, carry):
@@ -914,10 +896,9 @@
         g_units[here, :] = nt(k_gvalue[here, :], w_value[...].reshape(width, -1))
         return carry
 
-    lax.fori_loop(0, total // CHUNK, units_step, 0) if total % CHUNK == 0 else None
+    lax.fori_loop(0, total // CHUNK, units_step, 0)
     if total % CHUNK:
         here = slice(total // CHUNK * CHUNK, total)
-        lax.fori_loop(0, total // CHUNK, units_step, 0)
         g_units[here, :] = nt(k_gvalue[here, :], w_value[...].reshape(width, -1))
 
     def weight_grad(lhs, rhs, out, count):
@@ -937,44 +918,57 @@
     weight_grad(k_units, k_gvalue, o_value, total)
 
 
-def dense_call(n, tok, tail, ema, cot, mats_a, mats_b, w_shared, vec_wide, vec_head, target):
-    own, width = tok.shape
-    rows_t = tail.shape[0]
-    total = own + rows_t
-    length = 128
-    sets = rows_t // length
-    hv = mats_a.shape[2]
-    chan = mats_a.shape[1] // 3
-    rows_b = mats_b.shape[1] // 2
+    for copy in keep:
+        copy.wait()
+    post.finish()
+
+
+def layer_call(n, groups, rates, vectors, resumed, cot, tokens, weights):
+    nq = n // 4
+    dma = pltpu.SemaphoreType.DMA
+    vm = pltpu.VMEM
     shape = jax.ShapeDtypeStruct
-    vm = pltpu.VMEM
+    sets, kinds, length, width = tokens.shape
+    own = sets * kinds * length
+    total = own + sets * length
+    chan, hv = weights[0].shape
+    rows_b = weights[3].shape[0]
     outs = [
+        shape((14, 64, 128), F32), shape((512, 128), F32), shape((512, 128), F32), shape((8, width), F32), shape((8, 128), F32),
+        shape((total // 2, 128), F32), shape((n, chan, 128), BF16),
         shape((own, width), BF16), shape((own, width), F32), shape((own, width), F32), shape((own, 128), F32),
         shape((own, 128), F32), shape((own, 128), F32), shape((total, width), F32),
         shape((n, rows_b, width), BF16), shape((n, chan, hv), BF16), shape((n, rows_b, width), BF16),
         shape((n, chan, hv), BF16), shape((n, chan, hv), BF16),
         shape((sets, length, 128), BF16), shape((8, width), F32), shape((8, 128), F32),
+        shape((total * 4, 128), F32), shape((total * 4, 128), F32), shape((own * 4, 128), F32), shape((sets, length, width), BF16),
     ]
     scratch = [
-        vm((n, chan, hv), BF16), vm((n, chan, hv), BF16), vm((n, chan, hv), BF16),
-        vm((n, rows_b, width), BF16), vm((n, rows_b, width), BF16),
+        vm((n, 32, 128), BF16), vm((5, 16, 128), F32), vm((own, width), BF16), vm((sets, length, width), BF16),
+        vm((total * 4, 128), F32), vm((total * 4, 128), F32), vm((total * 4, 128), F32), vm((total // 2, 128), F32),
+        vm((2 * chan, hv), BF16), vm((rows_b, width), BF16), vm((chan, hv), BF16), vm((rows_b, width), BF16),
+        vm((n, 2 * chan, hv), BF16), vm((n, rows_b, width), BF16), vm((n, chan, hv), BF16), vm((n, rows_b, width), BF16),
         vm((2 * length, hv), BF16), vm((2 * length, hv), BF16),
         vm((sets, length, hv), BF16), vm((sets, length, hv), BF16), vm((sets, length, 128), BF16),
         vm((sets, length, hv), F32), vm((sets, length, 128), F32),
         vm((total, width), BF16), vm((own, width), BF16), vm((own, hv), BF16), vm((own, width), BF16),
         vm((own, hv), BF16), vm((own, width), BF16), vm((own, hv), BF16), vm((own, hv), BF16), vm((total, hv), BF16),
         vm((2 * length, hv), F32), vm((2 * length, hv), F32), vm((2 * length, hv), F32),
-        pltpu.SemaphoreType.DMA((5,)),
     ]
+    scratch += [vm((3, 2, 64, 128), BF16)] * 2 + [vm((2, 3, 2, 64, 128), BF16)] * 2
+    scratch += [vm((2, 3, 64, 128), BF16), vm((nq + 1, 3, 64, 128), BF16)]
+    scratch += [dma((18,)), dma((n - 1,)), dma((n - 1,)), dma((n - 1,)), dma((n - 1,)), dma((nq + 5,)), dma((5,))]
+    scratch += gather_sems(nq, 1) + gather_sems(nq, 3)
+    scratch += [dma((2,)), dma((2,)), dma((nq - 1,)), dma((nq - 1,)), dma((nq - 1,)), dma((1,))]
     return pl.pallas_call(
-        functools.partial(dense_kernel, n),
+        functools.partial(layer_kernel, n, groups),
         out_shape=outs,
-        in_specs=[VMEM] * 4 + [HBM] * 2 + [VMEM] * 3 + [SMEM],
-        out_specs=[VMEM] * len(outs),
+        in_specs=[VMEM] * 10 + [SMEM, VMEM] + [HBM] * 7,
+        out_specs=[VMEM] * 22 + [HBM] * 4,
         scratch_shapes=scratch,
-        compiler_params=pltpu.CompilerParams(vmem_limit_bytes=60 << 20),
-        name="dense",
-    )(tok, tail, ema, cot, mats_a, mats_b, w_shared, vec_wide, vec_head, target)
+        compiler_params=pltpu.CompilerParams(collective_id=0, has_side_effects=True, vmem_limit_bytes=62 << 20),
+        name="layer",
+    )(*rates, *vectors, resumed, cot, tokens, *weights)
 
 
 def big_flow(me, cross_first, grads, r1, w1, r2, w2, r3, w3, r4, rx, out, send, recv, local_sem):
@@ -1466,22 +1460,17 @@
     heads = query_scale.shape[0]
     own_rows = sets * kinds * length
     vectors = (norm_gain, ffn_gain, ema_omega, query_scale, query_shift, key_scale)
+    own_low = hidden_in[0].reshape(own_rows, width)
     (
-        tabs, power, power_rev, vec_wide, vec_head, starts, mat_shared, ema_lanes, x_lanes, inner, all_a, all_b, tail_low,
-    ) = front_call(
+        tabs, power, power_rev, vec_wide, vec_head, starts, mat_shared,
+        result, grad_middle, grad_act, grad_base, slope_shared, shared, grad_units, sum_outer, sum_inner, sum_hidden,
+        sum_reset, sum_value, sent_keys, sum_wide, sum_head, ema_lanes, x_lanes, inner, tail_low,
+    ) = layer_call(
         n, groups, [part.T for part in (ema_alpha, ema_delta, ema_beta, ema_eta)], [part[None] for part in vectors],
-        cont_prompt, hidden_in[0],
+        cont_prompt, cotangent[0].reshape(own_rows, width), hidden_in[0],
         (value_proj, reset_proj, inner_proj, hidden_proj, outer_proj, shared_proj),
     )
-    mat_shared = mat_shared.reshape(width, 128)
-    own_low, tail_low = hidden_in[0].reshape(own_rows, width), tail_low.reshape(-1, width)
-    grad_outer = cotangent[0].reshape(own_rows, width)
-    (
-        result, grad_middle, grad_act, grad_base, slope_shared, shared, grad_units, sum_outer, sum_inner, sum_hidden,
-        sum_reset, sum_value, sent_keys, sum_wide, sum_head,
-    ) = dense_call(
-        n, own_low, tail_low, ema_lanes, grad_outer, all_a, all_b, mat_shared, vec_wide, vec_head, cont_prompt
-    )
+    mat_shared, tail_low = mat_shared.reshape(width, 128), tail_low.reshape(-1, width)
 
     def shards(grad):
         return grad.reshape(nq, 2, 2, -1, grad.shape[-1])

time: 175 us -> 169 us (0.966)
  Pallas kernels: 174 us -> 168 us
    pallas_call x2 -> x1, Pallas kernels: 94.8 us -> 88.8 us  [layer_call(): pl.pallas_call(functools.partial(layer_kernel, n, groups), out_shape=outs...]
where the time goes in v3:
time: 169 us
  Pallas kernels  168 us (99%)
    pallas_call x1, Pallas kernels, layer_call(): pl.pallas_call(functools.partial(layer_kernel, n, groups), out_shape=outs...  88.8 us
    pallas_call x1, Pallas kernels, back_call(): pl.pallas_call(functools.partial(back_kernel, n, groups), out_shape=outs,...  76.5 us

profile of v3, /device:TPU:0, one launch (start us, length us, event | category | flops | bytes accessed | tf_op | source)
XLA Modules:
  0.0 169.2 jit_solution(13354740831626493199)
XLA Ops:
  0.7 88.8 %layer.1 = (f32[14,64,128]{2,1,0:T(8,128)}, f32[512,128]{1,0:T(8,128)}, f32[512,128]{1,0:T(8,128)}, f32[8,512]{1,0:T(8,128)}, f32[8,128]{1,0:T(8,128)}, /*index=...) custom-call(bf16[16,32]{1,0:T(8,128)(2,1)} %bitcast.45, ...), custom_call_target="tpu_custom_call" | custom-call | tf_op jit(solution)/shard_map/layer/pallas_call | solution.py:963
  89.4 0.0 copy-start
  89.4 76.5 %back.1 = (bf16[768,512]{1,0:T(8,128)(2,1)}, bf16[64,512]{1,0:T(8,128)(2,1)}, bf16[32,1024]{1,0:T(8,128)(2,1)}, bf16[64,512]{1,0:T(8,128)(2,1)}, bf16[32,1024]{1...) custom-call(f32[768,128]{1,0:T(8,128)} %get-tuple-element.69.refs_0_, ...), custom_call_target="tpu_custom_call" | custom-call | tf_op jit(solution)/shard_map/back/pallas_call | solution.py:1404
  165.9 2.4 %finish.1 = (bf16[768,512]{1,0:T(8,128)(2,1)}, f32[64,512]{1,0:T(8,128)}, f32[32,1024]{1,0:T(8,128)}, f32[64,512]{1,0:T(8,128)}, f32[32,1024]{1,0:T(8,128)}, /*i...) custom-call(bf16[768,512]{1,0:T(8,128)(2,1)} %get-tuple-element.94.g, ...), custom_call_target="tpu_custom_call" | custom-call | tf_op jit(solution)/shard_map/finish/pallas_call | solution.py:1440
  168.3 0.0 copy-done
  168.4 0.9 copy.38
Async XLA Ops:
  89.4 78.9 %copy-start = (bf16[768,512]{1,0:T(8,128)(2,1)S(1)}, bf16[768,512]{1,0:T(8,128)(2,1)}, u32[]{:S(2)}) copy-start(bf16[768,512]{1,0:T(8,128)(2,1)} %get-tuple-element.68) | copy-start | bytes 2359300

commit v4 on v3

--- a/solution.py
+++ b/solution.py
@@ -127,7 +127,7 @@
             for step in range(SUB - 1, -1, -1):
                 x = x_ref[pl.ds(x_base + step, 8, stride=SUB), :]
                 g = g_ref[pl.ds(base + step, 8, stride=SUB), :]
-                sums = [skip * g if part == 0 else dx_ref[pl.ds(base + step, 8, stride=SUB), :], None]
+                sums = [dx_ref[pl.ds(base + step, 8, stride=SUB), :], skip * g if part == 0 else None]
                 for i in range(half):
                     full = adj[i] + g
                     term = weight[i] * full
@@ -257,12 +257,9 @@
         remote(w2, w2, send.at[2], recv.at[2], me.core).wait_send()
 
 
-def tail_scratch(nq, rows, width):
-    return [
-        pltpu.VMEM((2, rows, width), BF16), pltpu.VMEM((2, rows, width), BF16),
-        pltpu.VMEM((rows, width), BF16), pltpu.VMEM((rows, width), BF16),
-        pltpu.VMEM((nq - 1, rows, width), BF16),
-    ]
+def tail_scratch(nq, shape):
+    vm = pltpu.VMEM
+    return [vm((2, *shape), BF16), vm((2, *shape), BF16), vm(shape, BF16), vm(shape, BF16), vm((nq - 1, *shape), BF16)]
 
 
 class Sender:
@@ -300,7 +297,7 @@
 
 def gather_flow(me, post, mats, zs, zr, ys, yr, xs, xr, cs, cr):
     nq = me.nq
-    mats = [(own, out, out.shape[-1] // 2) for own, out in mats]
+    mats = [(out, out.shape[-1] // 2) for out in mats]
     other = 1 - me.x
 
     def half(ref, width, which):
@@ -308,13 +305,14 @@
 
     up, down = (me.g, me.s + 4), (me.g, me.s - 4)
     has_up, has_down = me.q < nq - 1, me.q > 0
-    for i, (own, out, width) in enumerate(mats):
-        piece, place = half(own, width, me.x), half(out.at[me.s], width, me.x)
-        post.send(piece, place, zs.at[0, 0, i], zr.at[0, 0, i], up, has_up)
-        post.send(piece, place, zs.at[1, 0, i], zr.at[1, 0, i], down, has_down)
-        post.send(own, out.at[me.s], ys.at[0, i], yr.at[0, i], me.side)
-    for i, (own, out, width) in enumerate(mats):
-        post.send(own, out.at[me.s], cs.at[0, i], cr.at[0, i], me.core)
+    for i, (out, width) in enumerate(mats):
+        mine = out.at[me.s]
+        piece = half(mine, width, me.x)
+        post.send(piece, piece, zs.at[0, 0, i], zr.at[0, 0, i], up, has_up)
+        post.send(piece, piece, zs.at[1, 0, i], zr.at[1, 0, i], down, has_down)
+        post.send(mine, mine, ys.at[0, i], yr.at[0, i], me.side)
+    for i, (out, width) in enumerate(mats):
+        post.send(out.at[me.s], out.at[me.s], cs.at[0, i], cr.at[0, i], me.core)
     yield
 
     def arrival(side, hop):
@@ -324,7 +322,7 @@
 
         def pieces(pos, which):
             shard = jnp.clip(there, 0, nq - 1) * 4 + pos
-            return [half(out.at[shard], width, which) for _, out, width in mats]
+            return [half(out.at[shard], width, which) for out, width in mats]
 
         return here, jnp.logical_and(here, onward), to, pieces
 
@@ -343,7 +341,7 @@
         if side:
             yield
     count = len(arrivals)
-    for i, (_, out, _) in enumerate(mats):
+    for i, (out, _) in enumerate(mats):
         block = out.at[me.q * 4 + side_pos]
         post.got(block, yr.at[0, i])
         post.send(block, block, cs.at[1 + count, i], cr.at[1 + count, i], me.core)
@@ -367,7 +365,7 @@
                 post.send(piece, piece, cs.at[to, i], cr.at[to, i], me.core, here)
         yield
     for group, pos in ((0, me.pos + flip), (1, side_pos + flip)):
-        for i, (_, out, _) in enumerate(mats):
+        for i, (out, _) in enumerate(mats):
             post.got(out.at[me.q * 4 + pos], cr.at[group * (1 + count), i])
         for hop, side in arrivals:
             here, _, _, pieces = arrival(side, hop)
@@ -544,6 +542,216 @@
 CHUNK = 256
 
 
+def big_flow(me, cross_first, grads, r1, r2, r3, r4, rx, out, send, recv):
+    nq = me.nq
+    rows, width = out.shape
+    wide = width // 2
+    ours = pl.ds(pl.multiple_of(me.x * wide, 128), wide)
+    others = pl.ds(pl.multiple_of((1 - me.x) * wide, 128), wide)
+    copy1 = remote(grads.at[:, 1 - me.c], r1, send.at[0], recv.at[0], me.core)
+    copy1.start()
+    yield
+    copy1.wait()
+
+    def add1(i, carry):
+        r1[i] = (grads[i, me.c].astype(F32) + r1[i].astype(F32)).astype(BF16)
+        return carry
+
+    lax.fori_loop(0, 2 * nq, add1, 0)
+    if cross_first:
+        copy2 = remote(r1.at[:, :, others], r2, send.at[1], recv.at[1], me.cross)
+        copy2.start()
+    else:
+        copies2 = []
+        for k in range(nq):
+            copy = remote(r1.at[2 * k + 1 - me.y], r2.at[k], send.at[nq + 3 + k], recv.at[nq + 3 + k], me.side)
+            copy.start()
+            copies2.append(copy)
+    yield
+    if cross_first:
+        copy2.wait()
+
+        def add2(i, carry):
+            r2[i] = (r1[i, :, ours].astype(F32) + r2[i].astype(F32)).astype(BF16)
+            return carry
+
+        lax.fori_loop(0, 2 * nq, add2, 0)
+        copies3 = []
+        for k in range(nq):
+            copy = remote(r2.at[2 * k + 1 - me.y], r3.at[k], send.at[nq + 3 + k], recv.at[nq + 3 + k], me.side)
+            copy.start()
+            copies3.append(copy)
+    else:
+        for copy in copies2:
+            copy.wait()
+
+        def add2(i, carry):
+            r2[i] = (r1[2 * i + me.y].astype(F32) + r2[i].astype(F32)).astype(BF16)
+            return carry
+
+        lax.fori_loop(0, nq, add2, 0)
+        copies3 = [remote(r2.at[:, :, others], r3, send.at[2], recv.at[2], me.cross)]
+        copies3[0].start()
+    yield
+    for copy in copies3:
+        copy.wait()
+
+    def add3(i, carry):
+        mine = r2[2 * i + me.y] if cross_first else r2[i, :, ours]
+        r3[i] = (mine.astype(F32) + r3[i].astype(F32)).astype(BF16)
+        return carry
+
+    lax.fori_loop(0, nq, add3, 0)
+    copies = []
+    for k in range(1, nq):
+        copy = remote(r3.at[me.quad(k)], r4.at[k - 1], send.at[2 + k], recv.at[2 + k], me.at_quad(me.quad(k)))
+        copy.start()
+        copies.append(copy)
+    yield
+    total = r3[me.q].astype(F32)
+    for k in range(1, nq):
+        copies[k - 1].wait()
+        total = total + r4[k - 1].astype(F32)
+    out[:, ours] = total.astype(BF16)
+    copy5 = remote(out.at[:, ours], out.at[:, ours], send.at[nq + 2], recv.at[nq + 2], me.cross)
+    copy5.start()
+    yield
+    remote(out.at[:, others], out.at[:, others], send.at[nq + 2], recv.at[nq + 2], me.cross).wait_recv()
+    copy5.wait_send()
+    for at, bit in enumerate(me.cross_bits()[1:]):
+        copy = remote(out, rx.at[at], send.at[2 * nq + 3 + at], recv.at[2 * nq + 3 + at], me.cross_bit(bit))
+        copy.start()
+        copy.wait()
+        out[...] = (out[...].astype(F32) + rx[at].astype(F32)).astype(BF16)
+
+
+def big_scratch(nq, groups, cross_first, rows, width):
+    extra = max(groups.bit_length() - 2, 1)
+    half = width // 2
+    second = (2 * nq, rows, half) if cross_first else (nq, rows, width)
+    spare = (extra, rows, width) if groups > 2 else (1, 16, 128)
+    shapes = [(2 * nq, rows, width), second, (nq, rows, half), (nq - 1, rows, half), spare]
+    return [pltpu.VMEM(shape, BF16) for shape in shapes]
+
+
+def small_flow(me, grads, r1, w1, r2, w2, rx, out, send, recv):
+    many = 2 * me.nq
+    copy1 = remote(grads.at[:, 1 - me.c], r1, send.at[0], recv.at[0], me.core)
+    copy1.start()
+    yield
+    copy1.wait()
+
+    def add(i, carry):
+        w1[i] = (grads[i, me.c].astype(F32) + r1[i].astype(F32)).astype(BF16)
+        return carry
+
+    lax.fori_loop(0, many, add, 0)
+    mine = me.q * 2 + me.y
+    copies = []
+    for k in range(1, many):
+        to = (mine + k) % many
+        copy = remote(w1.at[to], r2.at[k - 1], send.at[k], recv.at[k], (me.g, to * 2 + me.c))
+        copy.start()
+        copies.append(copy)
+    yield
+    total = w1[mine].astype(F32)
+    for k in range(1, many):
+        copies[k - 1].wait()
+        total = total + r2[k - 1].astype(F32)
+    bits = me.cross_bits()
+    for at, bit in enumerate(bits):
+        w2[at] = total.astype(BF16)
+        copy = remote(w2.at[at], rx.at[at], send.at[many + at], recv.at[many + at], me.cross_bit(bit))
+        copy.start()
+        if at == 0:
+            yield
+        copy.wait()
+        total = total + rx[at].astype(F32)
+    out[...] = total.astype(BF16)
+
+
+def small_scratch(nq, groups, rows):
+    bits = groups.bit_length() - 1
+    return [
+        pltpu.VMEM((2 * nq, rows, 128), BF16), pltpu.VMEM((2 * nq, rows, 128), BF16),
+        pltpu.VMEM((2 * nq - 1, rows, 128), BF16), pltpu.VMEM((bits, rows, 128), BF16), pltpu.VMEM((bits, rows, 128), BF16),
+    ]
+
+
+def adjoint_flow(me, f_ref, tabs, sel, s_ref, m0, r0, m1, r1, m2, r2, ss, rs, zs, zr):
+    nq = me.nq
+    one, two, three, four = tabs[4], tabs[5], tabs[6], tabs[7]
+    mine = f_ref[...].reshape(3, 2, 64, 128)
+    m0[...] = mine.astype(BF16)
+    copy = remote(m0, r0, ss.at[0], rs.at[0], me.core)
+    copy.start()
+    yield
+    copy.wait()
+    upper_core, upper_side = me.c == 1, me.y == 1
+    other = r0[...].astype(F32)
+    lower = jnp.where(upper_core, other, mine)
+    upper = jnp.where(upper_core, mine, other)
+    pair = lower + one * upper
+    after = jnp.where(upper_core, 0.0, other)
+    m1[...] = pair.astype(BF16)
+    copy = remote(m1, r1, ss.at[1], rs.at[1], me.side)
+    copy.start()
+    yield
+    copy.wait()
+    far = r1[...].astype(F32)
+    low_pair = jnp.where(upper_side, far, pair)
+    high_pair = jnp.where(upper_side, pair, far)
+    total = low_pair + two * high_pair
+    after = jnp.where(upper_side, 0.0, jnp.where(upper_core, far, one * far)) + after
+    m2[0] = total[:, 0].astype(BF16)
+    for m in range(3):
+        m2[1, m] = (sel(0, m) * total[0, 1] + sel(1, m) * total[1, 1] + sel(2, m) * total[2, 1]).astype(BF16)
+    sends = []
+    for k in range(1, nq):
+        copy = remote(m2, r2.at[me.q], zs.at[k - 1], zr.at[k - 1], me.at_quad(me.quad(k)))
+        copy.start()
+        sends.append(copy)
+    r2[me.q] = m2[...]
+    yield
+    for k in range(1, nq):
+        src = r2.at[me.quad(nq - k)]
+        remote(src, src, zs.at[k - 1], zr.at[k - 1], me.core).wait_recv()
+    run = r2[0, 1].astype(F32)
+    for k in range(1, nq):
+        run = run + r2[k, 1].astype(F32)
+    carry = run
+    for k in range(nq - 1, -1, -1):
+        carry = jnp.where(me.q == k, run, carry)
+        run = four * run + r2[k, 0].astype(F32)
+    lead = pick(me.pos, [three, two, one, jnp.ones_like(one)])
+    for p in range(3):
+        s_ref[2 * p * 64 : (2 * p + 1) * 64] = lead * carry[p] + after[p, 0]
+        s_ref[(2 * p + 1) * 64 : (2 * p + 2) * 64] = after[p, 1]
+    for copy in sends:
+        copy.wait_send()
+
+
+class Steps:
+    def __init__(self, flows):
+        self.flows, self.live = flows, [True] * len(flows)
+
+    def __call__(self, *which):
+        for i in which:
+            if self.live[i]:
+                try:
+                    next(self.flows[i])
+                except StopIteration:
+                    self.live[i] = False
+
+    def finish(self):
+        while any(self.live):
+            self(*range(len(self.flows)))
+
+
+ORDERS = (True, False, True, False, True)
+N_BIG = 5
+
+
 def layer_kernel(n, groups, *refs):
     refs = list(refs)
 
@@ -554,22 +762,27 @@
 
     p_rates, p_vecs, (resumed,) = take(4), take(6), take(1)
     cot, h_tokens, i_value, i_reset, i_inner, i_hidden, i_outer, i_shared = take(8)
+    o_result, o_input = take(2)
+    sums, (out_small,), (staged,) = take(N_BIG), take(1), take(1)
     tabs, power, power_rev, vec_wide, vec_head, starts, w_shared = take(7)
-    (
-        result, g_middle, g_act, g_base, slope_s, shared_out, g_units, o_outer, o_inner, o_hidden, o_reset, o_value,
-        tail_keys, sum_wide, sum_head,
-    ) = take(15)
-    o_ema, o_x, o_state, o_tail = take(4)
+    g_middle, g_act, g_base, slope_s, shared_out = take(5)
+    grads, (t_keys_sent, sum_wide, sum_head) = take(N_BIG), take(3)
     gathered, lift, tok, tail, x_lanes, ema, inner, finals = take(8)
-    early_own, hidden_own, inner_own, outer_own, early_all, w_hidden, w_inner, w_outer = take(8)
+    early_all, w_hidden, w_inner, w_outer = take(4)
     (
         values, slope_v, t_values, t_slope, t_keys, t_dv, t_dk, k_units, k_activ, k_gated, k_mid, k_inner, k_branch, k_gin,
-        k_greset, k_gvalue, reset_pre, mixed, slope_i,
-    ) = take(19)
+        k_greset, k_gvalue,
+    ) = take(16)
+    g_lanes, b_inner, dx_lanes, k_gs, b_start, acc_in, acc_decay, acc_out, kept, omega_acc, gain_acc = take(11)
+    b_flow = finals.at[0:384]
+    t_sum, t_grad, t_out, g_small = take(4)
+    big = [take(5) for _ in range(N_BIG)]
+    small, keys_s, tail_s, back_exchange = take(5), take(5), take(5), take(6)
     exchange = take(6)
     load_sem, ss, sr, hs, hr, ts, tr = take(7)
     early_sem, late_sem = take(8), take(8)
     ess, ers, ezs, ezr, eps, epr = take(6)
+    big_send, big_recv, small_send, small_recv, k_send, k_recv, t_send, t_recv, bss, brs, bzs, bzr = take(12)
 
     me = Place(n, groups)
     length = 128
@@ -591,11 +804,11 @@
 
     x_in = h_tokens.at[:, 0]
     packing = [
-        local_copy(i_value, early_own.at[0:chan], 0),
-        local_copy(i_reset, early_own.at[chan : 2 * chan], 1),
-        local_copy(i_hidden, hidden_own, 2),
-        local_copy(i_inner, inner_own, 3),
-        local_copy(i_outer, outer_own, 4),
+        local_copy(i_value, early_all.at[me.s, 0:chan], 0),
+        local_copy(i_reset, early_all.at[me.s, chan : 2 * chan], 1),
+        local_copy(i_hidden, w_hidden.at[me.s], 2),
+        local_copy(i_inner, w_inner.at[me.s], 3),
+        local_copy(i_outer, w_outer.at[me.s], 4),
         local_copy(i_shared, w_shared.at[me.s], 5),
     ]
     fetch = [local_copy(h_tokens.at[p, k], tok.at[(p * 2 + k) * length : (p * 2 + k + 1) * length], 6 + p * 2 + k) for p in range(sets) for k in range(2)]
@@ -608,20 +821,18 @@
         lift[4, i : i + 1, 0 : ref.shape[1]] = ref[...].astype(F32)
     gathered[me.s, 0:16] = block.astype(BF16)
     gathered[me.s, 16:32] = lift[4].astype(BF16)
-    meet(me.group_peers() + [me.cross])
+    meet(me.group_peers() + [me.cross_bit(bit) for bit in me.cross_bits()])
     post = Sender(load_sem.at[12])
     post.device = me.core
     small_gather(me, gathered, post, ss, sr)
     for copy in packing:
         copy.wait()
-    pairs = ((early_own, early_all), (hidden_own, w_hidden), (inner_own, w_inner), (outer_own, w_outer))
-    early = gather_flow(me, post, pairs[:1], *early_sem)
-    late = gather_flow(me, post, pairs[1:], *late_sem)
+    early = gather_flow(me, post, [early_all], *early_sem)
+    late = gather_flow(me, post, [w_hidden, w_inner, w_outer], *late_sem)
     words = tokens_flow(me, post, x_in, tail, ts, tr, load_sem.at[13])
     next(early)
     next(words)
     next(late)
-    placing = [local_copy(own_part, all_part.at[me.s], 14 + i) for i, (own_part, all_part) in enumerate(pairs)]
     small_gather(me, w_shared, post, hs, hr)
     for copy in fetch:
         copy.wait()
@@ -691,7 +902,6 @@
     local_pass(count // 2, count // 2)
     state = state_flow(me, finals, tabs, sel, starts, *exchange, ess, ers, ezs, ezr, eps, epr)
     step(state)
-    keep = [local_copy(inner.at[0 : own * 4], o_state, 0)]
     step(late, early)
     step(state)
     step(words, early, late)
@@ -706,7 +916,6 @@
             step(late)
     for _ in words:
         pass
-    keep.append(local_copy(tail, o_tail, 1))
 
     def tail_norm(m, carry):
         plain, _ = norm_rows(tail[m].astype(F32))
@@ -717,15 +926,11 @@
 
     lax.fori_loop(0, sets, tail_norm, 0)
     local_pass(count, sets)
-    keep.append(local_copy(x_lanes, o_x, 2))
     step(late)
     apply_pass(count, sets)
-    keep.append(local_copy(ema, o_ema, 3))
     small_arrive(me, w_shared, post, hr)
     for _ in early:
         pass
-    for copy in placing:
-        copy.wait()
     w_value, w_reset = early_all.at[:, 0:chan], early_all.at[:, chan : 2 * chan]
     hv = w_value.shape[2]
     parts = hv // CHUNK
@@ -774,6 +979,17 @@
     lax.fori_loop(0, sets, tail_step, 0)
     ready("tail")
     causal = lax.broadcasted_iota(jnp.int32, (length, length), 0) >= lax.broadcasted_iota(jnp.int32, (length, length), 1)
+
+    reset_pre, mixed, slope_i = g_lanes, b_inner, dx_lanes
+
+    def put(ref, part, value):
+        for i in range(CHUNK // 128):
+            at = (part * (CHUNK // 128) + i) * 2 * length
+            ref[at : at + 2 * length] = value[:, i * 128 : (i + 1) * 128]
+
+    def get(ref, part):
+        at = [(part * (CHUNK // 128) + i) * 2 * length for i in range(CHUNK // 128)]
+        return jnp.concatenate([ref[start : start + 2 * length] for start in at], axis=1)
 
     def set_step(p, ready):
         here = pl.ds(pl.multiple_of(p * 2 * length, 2 * length), 2 * length)
@@ -797,7 +1013,7 @@
         queries = (shared * q_mul + q_add).astype(BF16)
         keys = (shared * k_mul).astype(BF16)
         for part in range(parts):
-            reset_pre[:, part * CHUNK : (part + 1) * CHUNK] = nn(activ, columns(w_reset, part))
+            put(reset_pre, part, nn(activ, columns(w_reset, part)))
         p_q, c_q, p_k, c_k = queries[:length], queries[length:], keys[:length], keys[length:]
         e_k = t_keys[m]
 
@@ -815,8 +1031,8 @@
             mix_p = nn(p_low, values[:length, cut])
             mix_c = nn(c_low, jnp.concatenate((t_values[m, :, cut], values[length:, cut]), axis=0))
             mix = jnp.concatenate((mix_p, mix_c), axis=0)
-            mixed[:, cut] = mix
-            gate = reset_pre[:, cut]
+            put(mixed, part, mix)
+            gate = get(reset_pre, part)
             k_gated[here, cut] = (gate * jax.nn.sigmoid(gate) * mix).astype(BF16)
         ready("hidden")
         middle = x + nn(k_gated[here, :], w_hidden[...].reshape(-1, width))
@@ -828,13 +1044,13 @@
             cut = slice(part * CHUNK, (part + 1) * CHUNK)
             inner, slope = silu_pair(nn(mid_low, columns(w_inner, part)))
             k_inner[here, cut] = inner.astype(BF16)
-            slope_i[:, cut] = slope
+            put(slope_i, part, slope)
         ready("outer")
-        result[here, :] = (middle + nn(k_inner[here, :], w_outer[...].reshape(-1, width))).astype(BF16)
+        staged[here, :] = (middle + nn(k_inner[here, :], w_outer[...].reshape(-1, width))).astype(BF16)
         top = cot[here, :]
         for part in range(parts):
             cut = slice(part * CHUNK, (part + 1) * CHUNK)
-            k_gin[here, cut] = (nt(top, rows(w_outer, part)) * slope_i[:, cut]).astype(BF16)
+            k_gin[here, cut] = (nt(top, rows(w_outer, part)) * get(slope_i, part)).astype(BF16)
         back = nt(k_gin[here, :], w_inner[...].reshape(width, -1))
         sum_wide[0:1] += jnp.sum(back * plain_mid, axis=0, keepdims=True)
         g_mid = top.astype(F32) + norm_back(back, plain_mid, inv_mid, gain_two)
@@ -846,9 +1062,9 @@
         for part in range(parts):
             cut = slice(part * CHUNK, (part + 1) * CHUNK)
             gated_back = nt(branch, rows(w_hidden, part))
-            gate, slope = silu_pair(reset_pre[:, cut])
+            gate, slope = silu_pair(get(reset_pre, part))
             g_mix = (gated_back * gate).astype(BF16)
-            k_greset[here, cut] = (gated_back * mixed[:, cut] * slope).astype(BF16)
+            k_greset[here, cut] = (gated_back * get(mixed, part) * slope).astype(BF16)
             dp_p += nt(g_mix[:length], values[:length, cut])
             dp_c += nt(g_mix[length:], jnp.concatenate((t_values[m, :, cut], values[length:, cut]), axis=0))
             dv_p = tn(p_low, g_mix[:length])
@@ -882,377 +1098,36 @@
 
     set_step(0, ready)
     lax.fori_loop(1, sets, later_step, 0)
-    tail_keys[...] = t_dk[...].astype(BF16)
-
-    def tail_back(m, carry):
-        at = pl.multiple_of(own + m * length, length)
-        k_gvalue[pl.ds(at, length), :] = (t_dv[m] * t_slope[m].astype(F32)).astype(BF16)
-        return carry
-
-    lax.fori_loop(0, sets, tail_back, 0)
-
-    def units_step(i, carry):
-        here = pl.ds(pl.multiple_of(i * CHUNK, CHUNK), CHUNK)
-        g_units[here, :] = nt(k_gvalue[here, :], w_value[...].reshape(width, -1))
-        return carry
-
-    lax.fori_loop(0, total // CHUNK, units_step, 0)
-    if total % CHUNK:
-        here = slice(total // CHUNK * CHUNK, total)
-        g_units[here, :] = nt(k_gvalue[here, :], w_value[...].reshape(width, -1))
-
-    def weight_grad(lhs, rhs, out, count):
-        per = CHUNK // out.shape[1]
-
-        def step(i, carry):
-            block = tn(lhs[0:count, pl.ds(pl.multiple_of(i * CHUNK, CHUNK), CHUNK)], rhs[0:count, :])
-            out[pl.ds(i * per, per)] = block.astype(BF16).reshape(per, out.shape[1], out.shape[2])
-            return carry
-
-        lax.fori_loop(0, lhs.shape[1] // CHUNK, step, 0)
-
-    weight_grad(k_inner, cot, o_outer, own)
-    weight_grad(k_mid, k_gin, o_inner, own)
-    weight_grad(k_gated, k_branch, o_hidden, own)
-    weight_grad(k_activ, k_greset, o_reset, own)
-    weight_grad(k_units, k_gvalue, o_value, total)
-
-
-    for copy in keep:
-        copy.wait()
-    post.finish()
-
-
-def layer_call(n, groups, rates, vectors, resumed, cot, tokens, weights):
-    nq = n // 4
-    dma = pltpu.SemaphoreType.DMA
-    vm = pltpu.VMEM
-    shape = jax.ShapeDtypeStruct
-    sets, kinds, length, width = tokens.shape
-    own = sets * kinds * length
-    total = own + sets * length
-    chan, hv = weights[0].shape
-    rows_b = weights[3].shape[0]
-    outs = [
-        shape((14, 64, 128), F32), shape((512, 128), F32), shape((512, 128), F32), shape((8, width), F32), shape((8, 128), F32),
-        shape((total // 2, 128), F32), shape((n, chan, 128), BF16),
-        shape((own, width), BF16), shape((own, width), F32), shape((own, width), F32), shape((own, 128), F32),
-        shape((own, 128), F32), shape((own, 128), F32), shape((total, width), F32),
-        shape((n, rows_b, width), BF16), shape((n, chan, hv), BF16), shape((n, rows_b, width), BF16),
-        shape((n, chan, hv), BF16), shape((n, chan, hv), BF16),
-        shape((sets, length, 128), BF16), shape((8, width), F32), shape((8, 128), F32),
-        shape((total * 4, 128), F32), shape((total * 4, 128), F32), shape((own * 4, 128), F32), shape((sets, length, width), BF16),
-    ]
-    scratch = [
-        vm((n, 32, 128), BF16), vm((5, 16, 128), F32), vm((own, width), BF16), vm((sets, length, width), BF16),
-        vm((total * 4, 128), F32), vm((total * 4, 128), F32), vm((total * 4, 128), F32), vm((total // 2, 128), F32),
-        vm((2 * chan, hv), BF16), vm((rows_b, width), BF16), vm((chan, hv), BF16), vm((rows_b, width), BF16),
-        vm((n, 2 * chan, hv), BF16), vm((n, rows_b, width), BF16), vm((n, chan, hv), BF16), vm((n, rows_b, width), BF16),
-        vm((2 * length, hv), BF16), vm((2 * length, hv), BF16),
-        vm((sets, length, hv), BF16), vm((sets, length, hv), BF16), vm((sets, length, 128), BF16),
-        vm((sets, length, hv), F32), vm((sets, length, 128), F32),
-        vm((total, width), BF16), vm((own, width), BF16), vm((own, hv), BF16), vm((own, width), BF16),
-        vm((own, hv), BF16), vm((own, width), BF16), vm((own, hv), BF16), vm((own, hv), BF16), vm((total, hv), BF16),
-        vm((2 * length, hv), F32), vm((2 * length, hv), F32), vm((2 * length, hv), F32),
-    ]
-    scratch += [vm((3, 2, 64, 128), BF16)] * 2 + [vm((2, 3, 2, 64, 128), BF16)] * 2
-    scratch += [vm((2, 3, 64, 128), BF16), vm((nq + 1, 3, 64, 128), BF16)]
-    scratch += [dma((18,)), dma((n - 1,)), dma((n - 1,)), dma((n - 1,)), dma((n - 1,)), dma((nq + 5,)), dma((5,))]
-    scratch += gather_sems(nq, 1) + gather_sems(nq, 3)
-    scratch += [dma((2,)), dma((2,)), dma((nq - 1,)), dma((nq - 1,)), dma((nq - 1,)), dma((1,))]
-    return pl.pallas_call(
-        functools.partial(layer_kernel, n, groups),
-        out_shape=outs,
-        in_specs=[VMEM] * 10 + [SMEM, VMEM] + [HBM] * 7,
-        out_specs=[VMEM] * 22 + [HBM] * 4,
-        scratch_shapes=scratch,
-        compiler_params=pltpu.CompilerParams(collective_id=0, has_side_effects=True, vmem_limit_bytes=62 << 20),
-        name="layer",
-    )(*rates, *vectors, resumed, cot, tokens, *weights)
-
-
-def big_flow(me, cross_first, grads, r1, w1, r2, w2, r3, w3, r4, rx, out, send, recv, local_sem):
-    nq = me.nq
-    rows, width = out.shape
-    wide = width // 2
-    ours = pl.ds(pl.multiple_of(me.x * wide, 128), wide)
-    others = pl.ds(pl.multiple_of((1 - me.x) * wide, 128), wide)
-    copy1 = remote(grads.at[:, :, 1 - me.c], r1, send.at[0], recv.at[0], me.core)
-    copy1.start()
-    kept = pltpu.make_async_copy(grads.at[:, :, me.c], w1, local_sem)
-    kept.start()
-    yield
-    kept.wait()
-    copy1.wait()
-
-    def add1(i, carry):
-        w1[i // 2, i % 2] = (w1[i // 2, i % 2].astype(F32) + r1[i // 2, i % 2].astype(F32)).astype(BF16)
-        return carry
-
-    lax.fori_loop(0, 2 * nq, add1, 0)
-    if cross_first:
-        copy2 = remote(w1.at[:, :, :, others], r2, send.at[1], recv.at[1], me.cross)
-    else:
-        copy2 = remote(w1.at[:, 1 - me.y], r2, send.at[1], recv.at[1], me.side)
-    copy2.start()
-    yield
-    copy2.wait()
-    if cross_first:
-        def add2(i, carry):
-            w2[i // 2, i % 2] = (w1[i // 2, i % 2, :, ours].astype(F32) + r2[i // 2, i % 2].astype(F32)).astype(BF16)
-            return carry
-
-        lax.fori_loop(0, 2 * nq, add2, 0)
-        copy3 = remote(w2.at[:, 1 - me.y], r3, send.at[2], recv.at[2], me.side)
-    else:
-        def add2(i, carry):
-            w2[i] = (w1[i, me.y].astype(F32) + r2[i].astype(F32)).astype(BF16)
-            return carry
-
-        lax.fori_loop(0, nq, add2, 0)
-        copy3 = remote(w2.at[:, :, others], r3, send.at[2], recv.at[2], me.cross)
-    copy3.start()
-    yield
-    copy3.wait()
-
-    def add3(i, carry):
-        mine = w2[i, me.y] if cross_first else w2[i, :, ours]
-        w3[i] = (mine.astype(F32) + r3[i].astype(F32)).astype(BF16)
-        return carry
-
-    lax.fori_loop(0, nq, add3, 0)
-    copies = []
-    for k in range(1, nq):
-        copy = remote(w3.at[me.quad(k)], r4.at[k - 1], send.at[2 + k], recv.at[2 + k], me.at_quad(me.quad(k)))
-        copy.start()
-        copies.append(copy)
-    yield
-    total = w3[me.q].astype(F32)
-    for k in range(1, nq):
-        copies[k - 1].wait()
-        total = total + r4[k - 1].astype(F32)
-    out[:, ours] = total.astype(BF16)
-    copy5 = remote(out.at[:, ours], out.at[:, ours], send.at[nq + 2], recv.at[nq + 2], me.cross)
-    copy5.start()
-    yield
-    remote(out.at[:, others], out.at[:, others], send.at[nq + 2], recv.at[nq + 2], me.cross).wait_recv()
-    copy5.wait_send()
-    for at, bit in enumerate(me.cross_bits()[1:]):
-        copy = remote(out, rx.at[at], send.at[nq + 3 + at], recv.at[nq + 3 + at], me.cross_bit(bit))
-        copy.start()
-        copy.wait()
-        out[...] = (out[...].astype(F32) + rx[at].astype(F32)).astype(BF16)
-
-
-def big_scratch(nq, groups, cross_first, rows, width):
-    extra = max(groups.bit_length() - 2, 1)
-    half = width // 2
-    full = [pltpu.VMEM((nq, 2, rows, width), BF16)] * 2
-    if cross_first:
-        mid = [pltpu.VMEM((nq, 2, rows, half), BF16)] * 2
-    else:
-        mid = [pltpu.VMEM((nq, rows, width), BF16)] * 2
-    return full + mid + [
-        pltpu.VMEM((nq, rows, half), BF16), pltpu.VMEM((nq, rows, half), BF16),
-        pltpu.VMEM((nq - 1, rows, half), BF16), pltpu.VMEM((extra, rows, width), BF16),
-    ]
-
-
-def small_flow(me, grads, r1, w1, r2, w2, rx, out, send, recv):
-    many = 2 * me.nq
-    copy1 = remote(grads.at[:, 1 - me.c], r1, send.at[0], recv.at[0], me.core)
-    copy1.start()
-    yield
-    copy1.wait()
-
-    def add(i, carry):
-        w1[i] = (grads[i, me.c].astype(F32) + r1[i].astype(F32)).astype(BF16)
-        return carry
-
-    lax.fori_loop(0, many, add, 0)
-    mine = me.q * 2 + me.y
-    copies = []
-    for k in range(1, many):
-        to = (mine + k) % many
-        copy = remote(w1.at[to], r2.at[k - 1], send.at[k], recv.at[k], (me.g, to * 2 + me.c))
-        copy.start()
-        copies.append(copy)
-    yield
-    total = w1[mine].astype(F32)
-    for k in range(1, many):
-        copies[k - 1].wait()
-        total = total + r2[k - 1].astype(F32)
-    bits = me.cross_bits()
-    for at, bit in enumerate(bits):
-        w2[at] = total.astype(BF16)
-        copy = remote(w2.at[at], rx.at[at], send.at[many + at], recv.at[many + at], me.cross_bit(bit))
-        copy.start()
-        if at == 0:
-            yield
-        copy.wait()
-        total = total + rx[at].astype(F32)
-    out[...] = total.astype(BF16)
-
-
-def small_scratch(nq, groups, rows):
-    bits = groups.bit_length() - 1
-    return [
-        pltpu.VMEM((2 * nq, rows, 128), BF16), pltpu.VMEM((2 * nq, rows, 128), BF16),
-        pltpu.VMEM((2 * nq - 1, rows, 128), BF16), pltpu.VMEM((bits, rows, 128), BF16), pltpu.VMEM((bits, rows, 128), BF16),
-    ]
-
-
-def adjoint_flow(me, f_ref, tabs, sel, s_ref, m0, r0, m1, r1, m2, r2, ss, rs, zs, zr):
-    nq = me.nq
-    one, two, three, four = tabs[4], tabs[5], tabs[6], tabs[7]
-    mine = f_ref[...].reshape(3, 2, 64, 128)
-    m0[...] = mine.astype(BF16)
-    copy = remote(m0, r0, ss.at[0], rs.at[0], me.core)
-    copy.start()
-    yield
-    copy.wait()
-    upper_core, upper_side = me.c == 1, me.y == 1
-    other = r0[...].astype(F32)
-    lower = jnp.where(upper_core, other, mine)
-    upper = jnp.where(upper_core, mine, other)
-    pair = lower + one * upper
-    after = jnp.where(upper_core, 0.0, other)
-    m1[...] = pair.astype(BF16)
-    copy = remote(m1, r1, ss.at[1], rs.at[1], me.side)
-    copy.start()
-    yield
-    copy.wait()
-    far = r1[...].astype(F32)
-    low_pair = jnp.where(upper_side, far, pair)
-    high_pair = jnp.where(upper_side, pair, far)
-    total = low_pair + two * high_pair
-    after = jnp.where(upper_side, 0.0, jnp.where(upper_core, far, one * far)) + after
-    m2[0] = total[:, 0].astype(BF16)
-    for m in range(3):
-        m2[1, m] = (sel(0, m) * total[0, 1] + sel(1, m) * total[1, 1] + sel(2, m) * total[2, 1]).astype(BF16)
-    sends = []
-    for k in range(1, nq):
-        copy = remote(m2, r2.at[me.q], zs.at[k - 1], zr.at[k - 1], me.at_quad(me.quad(k)))
-        copy.start()
-        sends.append(copy)
-    r2[me.q] = m2[...]
-    yield
-    for k in range(1, nq):
-        src = r2.at[me.quad(nq - k)]
-        remote(src, src, zs.at[k - 1], zr.at[k - 1], me.core).wait_recv()
-    run = r2[0, 1].astype(F32)
-    for k in range(1, nq):
-        run = run + r2[k, 1].astype(F32)
-    carry = run
-    for k in range(nq - 1, -1, -1):
-        carry = jnp.where(me.q == k, run, carry)
-        run = four * run + r2[k, 0].astype(F32)
-    lead = pick(me.pos, [three, two, one, jnp.ones_like(one)])
-    for p in range(3):
-        s_ref[2 * p * 64 : (2 * p + 1) * 64] = lead * carry[p] + after[p, 0]
-        s_ref[(2 * p + 1) * 64 : (2 * p + 2) * 64] = after[p, 1]
-    for copy in sends:
-        copy.wait_send()
-
-
-class Steps:
-    def __init__(self, flows):
-        self.flows, self.live = flows, [True] * len(flows)
-
-    def __call__(self, *which):
-        for i in which:
-            if self.live[i]:
-                try:
-                    next(self.flows[i])
-                except StopIteration:
-                    self.live[i] = False
-
-    def finish(self):
-        while any(self.live):
-            self(*range(len(self.flows)))
-
-
-ORDERS = (True, False, True, False, True)
-N_BIG = 5
-
-
-def back_kernel(n, groups, *refs):
-    refs = list(refs)
-
-    def take(count):
-        got = refs[:count]
-        del refs[:count]
-        return got
-
-    base, slope_s, shared, t_keys, w_shared, tabs, power, power_rev, vec_wide, vec_head, starts, sum_wide, sum_head, resumed = take(14)
-    h_act, h_ema, h_x, h_inner, h_units, h_middle, h_tokens, h_tail = take(8)
-    grads = take(N_BIG)
-    (input_grad,) = take(1)
-    outs = take(N_BIG)
-    (out_small,) = take(1)
-    loads = take(7)
-    g_act, ema, x_lanes, inner, g_units, g_middle, tokens = loads
-    g_lanes, k_activ, k_gs, b_inner, b_flow, b_start, dx_lanes, acc_in, acc_decay, acc_out, kept, omega_acc, gain_acc = take(13)
-    t_sum, t_rows, t_grad, t_out, grad_in, g_small = take(6)
-    big = [take(8) for _ in range(N_BIG)]
-    small = take(5)
-    keys_s, tail_s = take(5), take(5)
-    exchange = take(6)
-    load_sem, big_send, big_recv, big_local, small_send, small_recv, k_send, k_recv, t_send, t_recv, ess, ers, ezs, ezr = take(14)
-
-    me = Place(n, groups)
-    own = base.shape[0]
-    total = tokens.shape[0]
-    width = tokens.shape[1]
-    length = 128
-    count = own // length
-    lanes = width // 128
-    chan = width // n
-    sel = chosen(resumed, me)
-    hbm = [h_act, h_ema, h_x, h_inner, h_units, h_middle, h_tokens, h_tail]
-    places = loads[:6] + [tokens.at[0:own], tokens.at[own:total]]
-    arrive = [pltpu.make_async_copy(src, dst, load_sem.at[i]) for i, (src, dst) in enumerate(zip(hbm, places))]
-    for copy in arrive:
-        copy.start()
-    meet(me.group_peers() + [me.cross_bit(bit) for bit in me.cross_bits()])
-    keys = tail_flow(me, t_keys, *keys_s, t_sum, k_send, k_recv)
+    leave = local_copy(staged, o_result, 0)
+    tail_rows = length // 4
+    for part in range(4):
+        t_keys_sent[part // 2, part % 2] = t_dk[:, part * tail_rows : (part + 1) * tail_rows].astype(BF16)
+    keys = tail_flow(me, t_keys_sent, *keys_s, t_sum, k_send, k_recv)
     next(keys)
-    steps = Steps(
-        [
-            big_flow(me, ORDERS[i], grads[i], *big[i], outs[i], big_send.at[i], big_recv.at[i], big_local.at[i])
-            for i in range(N_BIG)
-        ]
-    )
-    steps(*range(N_BIG))
-    k_mul = vec_head[2:3]
-    gain_one = vec_wide[0:1]
     for ref in (omega_acc, gain_acc, acc_in, acc_decay, acc_out):
         ref[...] = jnp.zeros_like(ref)
-    for i in range(3):
-        arrive[i].wait()
 
     def grad_rows(row, with_tail):
         at = pl.multiple_of(row * length, length)
         here = pl.ds(at, length)
-        d_shared = base[here, :]
+        d_shared = g_base[here, :]
         if with_tail:
-            extra = t_rows[pl.ds(pl.multiple_of(row // 2 * length, length), length), :]
+            extra = jnp.concatenate([t_sum[part // 2, part % 2, row // 2] for part in range(4)], axis=0).astype(F32)
             d_shared = d_shared + extra * k_mul
-            gain_acc[1:2, 0:128] += jnp.sum(extra * shared[here, :], axis=0, keepdims=True)
+            gain_acc[1:2, 0:128] += jnp.sum(extra * shared_out[here, :], axis=0, keepdims=True)
         gs = (d_shared * slope_s[here, :]).astype(BF16)
         k_gs[here, :] = gs
         for lane in range(lanes):
             cut = slice(lane * 128, (lane + 1) * 128)
             pre = ema[pl.ds(lane * total + at, length), :]
             sig = jax.nn.sigmoid(pre)
-            k_activ[here, cut] = (pre * sig).astype(BF16)
-            back = g_act[here, cut] + nt(gs, w_shared[cut, :])
+            back = g_act[here, cut] + nt(gs, w_shared[lane * per : (lane + 1) * per].reshape(128, 128))
             back = back * (sig * (1.0 + pre * (1.0 - sig)))
             g_lanes[pl.ds(lane * own + at, length), :] = back
             x = x_lanes[pl.ds(lane * total + at, length), :]
             omega_acc[lane : lane + 1] += jnp.sum(back * x, axis=0, keepdims=True)
 
-    def local_pass(first):
+    def local_back(first):
         ema_local_pass(
             count, (first, 2, count // 2), g_lanes, tabs.at[0], tabs.at[1], tabs.at[2], tabs.at[3], b_inner, b_flow, True
         )
@@ -1265,65 +1140,95 @@
         grad_rows(2 * p, True)
         return carry
 
-    def norm_rows_back(at, size, extra):
-        here = pl.ds(at, size)
-        plain, inv = norm_rows(tokens[here, :].astype(F32))
-        units = g_units[here, :]
-        if extra is not None:
-            units = units + extra
+    def norm_rows_back(x, units):
+        plain, inv = norm_rows(x.astype(F32))
         gain_acc[0:1] += jnp.sum(units * plain, axis=0, keepdims=True)
         return norm_back(units, plain, inv, gain_one)
 
+    def weight_grad(lhs, rhs, out, many):
+        block_rows = CHUNK // out.shape[2] // 2
+
+        def step(i, carry):
+            block = tn(lhs[0:many, pl.ds(pl.multiple_of(i * CHUNK, CHUNK), CHUNK)], rhs[0:many, :])
+            out[pl.ds(i * block_rows, block_rows)] = block.astype(BF16).reshape(block_rows, 2, out.shape[2], out.shape[3])
+            return carry
+
+        lax.fori_loop(0, lhs.shape[1] // CHUNK, step, 0)
+
+    steps = Steps(
+        [big_flow(me, ORDERS[i], grads[i], *big[i], sums[i], big_send.at[i], big_recv.at[i]) for i in range(N_BIG)]
+    )
+    weight_grad(k_inner, cot, grads[0], own)
+    steps(0)
+    next(keys)
+    weight_grad(k_mid, k_gin, grads[1], own)
+    steps(1, 0)
     lax.fori_loop(0, count // 2, cont_rows, 0)
     next(keys)
-    steps(0, 1)
-    local_pass(1)
+    weight_grad(k_gated, k_branch, grads[2], own)
+    steps(2, 1)
+    local_back(1)
     next(keys)
-    steps(2, 3)
-    arrive[4].wait()
-    arrive[6].wait()
-    arrive[7].wait()
-    piece = (total - own) // 4
-    for part in range(4):
-        t_grad[part // 2, part % 2] = norm_rows_back(own + part * piece, piece, None).astype(BF16)
-    tail = tail_flow(me, t_grad, *tail_s, t_out, t_send, t_recv)
-    next(tail)
-    next(keys)
-    steps(4)
+    weight_grad(k_activ, k_greset, grads[3], own)
+    steps(3, 2)
     for _ in keys:
         pass
-    for part in range(4):
-        t_rows[part * piece : (part + 1) * piece] = t_sum[part // 2, part % 2].astype(F32)
     lax.fori_loop(0, count // 2, prompt_rows, 0)
-    local_pass(0)
-    adjoint = adjoint_flow(me, b_flow, tabs, sel, b_start, *exchange, ess, ers, ezs, ezr)
+    local_back(0)
+    adjoint = adjoint_flow(me, b_flow, tabs, sel, b_start, *back_exchange, bss, brs, bzs, bzr)
     next(adjoint)
-    steps(0, 1)
+    steps(3, 0)
+
+    def tail_back(m, carry):
+        at = pl.multiple_of(own + m * length, length)
+        k_gvalue[pl.ds(at, length), :] = (t_dv[m] * t_slope[m].astype(F32)).astype(BF16)
+        return carry
+
+    lax.fori_loop(0, sets, tail_back, 0)
     next(adjoint)
-    next(tail)
-    steps(2)
+    weight_grad(k_units, k_gvalue, grads[4], total)
+    steps(4, 1)
     next(adjoint)
-    next(tail)
-    steps(3)
+
+    def units_step(i, carry):
+        at = pl.multiple_of(i * CHUNK, CHUNK)
+        block = nt(k_gvalue[pl.ds(at, CHUNK), :], w_value[...].reshape(width, -1))
+        for lane in range(lanes):
+            dx_lanes[pl.ds(lane * own + at, CHUNK), :] = block[:, lane * 128 : (lane + 1) * 128]
+        return carry
+
+    lax.fori_loop(0, own // CHUNK, units_step, 0)
+
+    def tail_grad_step(m, carry):
+        at = pl.multiple_of(own + m * length, length)
+        units = nt(k_gvalue[pl.ds(at, length), :], w_value[...].reshape(width, -1))
+        block = norm_rows_back(tail[m], units).astype(BF16)
+        for part in range(4):
+            t_grad[part // 2, part % 2, m] = block[part * tail_rows : (part + 1) * tail_rows]
+        return carry
+
+    lax.fori_loop(0, sets, tail_grad_step, 0)
+    ends = tail_flow(me, t_grad, *tail_s, t_out, t_send, t_recv)
+    next(ends)
+    steps(2, 4)
     for _ in adjoint:
         pass
-    arrive[3].wait()
     for row in range(count):
         ema_back_pass(
             count, total // length, row, x_lanes, g_lanes, tabs.at[0], tabs.at[8], vec_head, power, inner, starts,
             power_rev, b_inner, b_start, dx_lanes, acc_in, acc_decay, acc_out, kept,
         )
-        if row == 0:
-            steps(4)
-            next(tail)
-        elif row < count - 1:
+        if row < 3:
+            next(ends)
+        if row < count - 1:
             steps(*range(N_BIG))
-    arrive[5].wait()
 
     def own_rows(row, carry):
-        at = pl.multiple_of(row * length, length)
-        extra = jnp.concatenate([dx_lanes[pl.ds(lane * own + at, length), :] for lane in range(lanes)], axis=1)
-        grad_in[pl.ds(at, length), :] = g_middle[pl.ds(at, length), :] + norm_rows_back(at, length, extra)
+        here = pl.ds(pl.multiple_of(row * length, length), length)
+        units = jnp.concatenate(
+            [dx_lanes[pl.ds(lane * own + row * length, length), :] for lane in range(lanes)], axis=1
+        )
+        g_middle[here, :] = g_middle[here, :] + norm_rows_back(tok[here, :], units)
         return carry
 
     lax.fori_loop(0, count, own_rows, 0)
@@ -1344,72 +1249,96 @@
     g_small[:, :, 2 * chan :] = heads
     little = small_flow(me, g_small, *small, out_small, small_send, small_recv)
     next(little)
-    for _ in tail:
+    for _ in ends:
         pass
     next(little)
     steps(*range(N_BIG))
+    for part in range(4):
+        for m in range(sets):
+            at = 2 * m * length + part * tail_rows
+            here = slice(at, at + tail_rows)
+            g_middle[here] = g_middle[here] + t_out[part // 2, part % 2, m].astype(F32)
 
     def cast_rows(row, carry):
         here = pl.ds(pl.multiple_of(row * length, length), length)
-        input_grad[here, :] = grad_in[here, :].astype(BF16)
-        return carry
-
-    for part in range(4):
-        t_wide = t_out[part // 2, part % 2].astype(F32)
-        at = part * piece
-        while at < (part + 1) * piece:
-            m = at // length
-            stop = min((m + 1) * length, (part + 1) * piece)
-            here = slice(at + m * length, stop + m * length)
-            grad_in[here] = grad_in[here] + t_wide[at - part * piece : stop - part * piece]
-            at = stop
+        staged[here, :] = g_middle[here, :].astype(BF16)
+        return carry
+
+    leave.wait()
     lax.fori_loop(0, count, cast_rows, 0)
+    leave = local_copy(staged, o_input, 1)
     next(little)
     steps(*range(N_BIG))
     for _ in little:
         pass
     steps.finish()
-
-
-def back_call(n, groups, ins, hbm, grads):
+    post.finish()
+    leave.wait()
+
+
+def layer_call(n, groups, rates, vectors, resumed, cot, tokens, weights):
     nq = n // 4
     dma = pltpu.SemaphoreType.DMA
     vm = pltpu.VMEM
     shape = jax.ShapeDtypeStruct
-    own, width = hbm[6].shape
-    total = own + hbm[7].shape[0]
-    chan = width // n
+    sets, kinds, length, width = tokens.shape
+    own = sets * kinds * length
+    total = own + sets * length
+    chan, hv = weights[0].shape
+    rows_b = weights[3].shape[0]
     small_rows = 2 * chan + 16
-    piece = (total - own) // 4
-    outs = [shape((own, width), BF16)] + [shape(grad.shape[-2:], BF16) for grad in grads] + [shape((small_rows, 128), BF16)]
-    scratch = [vm(part.shape, part.dtype) for part in hbm[:6]] + [vm((total, width), BF16)]
+    wide, tall = (n // 2, 2, chan, hv), (n // 2, 2, rows_b, width)
+    shapes = [tall, wide, tall, wide, wide]
+    piece = (sets, length // 4)
+    outs = [shape((own, width), BF16)] * 2 + [shape(part[2:], BF16) for part in shapes] + [shape((small_rows, 128), BF16)]
+    scratch = [
+        vm((own, width), BF16), vm((14, 64, 128), F32), vm((512, 128), F32), vm((512, 128), F32), vm((8, width), F32), vm((8, 128), F32),
+        vm((total // 2, 128), F32), vm((n, chan, 128), BF16),
+        vm((own, width), F32), vm((own, width), F32), vm((own, 128), F32), vm((own, 128), F32), vm((own, 128), F32),
+    ]
+    scratch += [vm(part, BF16) for part in shapes]
+    scratch += [vm((2, 2, *piece, 128), BF16), vm((8, width), F32), vm((8, 128), F32)]
     scratch += [
-        vm((own * 4, 128), F32), vm((own, width), BF16), vm((own, 128), BF16), vm((own * 4, 128), F32),
-        vm((own // 2, 128), F32), vm((own // 2, 128), F32), vm((own * 4, 128), F32), vm((64, 128), F32), vm((64, 128), F32),
-        vm((64, 128), F32), vm((128, 8, 128), F32), vm((8, 128), F32), vm((8, width), F32),
-        vm((2, 2, piece, 128), BF16), vm((4 * piece, 128), F32), vm((2, 2, piece, width), BF16), vm((2, 2, piece, width), BF16),
-        vm((own, width), F32), vm((n // 2, 2, small_rows, 128), BF16),
+        vm((n, 32, 128), BF16), vm((5, 16, 128), F32), vm((own, width), BF16), vm((sets, length, width), BF16),
+        vm((total * 4, 128), F32), vm((total * 4, 128), F32), vm((total * 4, 128), F32), vm((total // 2, 128), F32),
+        vm((n, 2 * chan, hv), BF16), vm((n, rows_b, width), BF16), vm((n, chan, hv), BF16), vm((n, rows_b, width), BF16),
+        vm((2 * length, hv), BF16), vm((2 * length, hv), BF16),
+        vm((sets, length, hv), BF16), vm((sets, length, hv), BF16), vm((sets, length, 128), BF16),
+        vm((sets, length, hv), F32), vm((sets, length, 128), F32),
+        vm((total, width), BF16), vm((own, width), BF16), vm((own, hv), BF16), vm((own, width), BF16),
+        vm((own, hv), BF16), vm((own, width), BF16), vm((own, hv), BF16), vm((own, hv), BF16), vm((total, hv), BF16),
     ]
-    for i, grad in enumerate(grads):
-        scratch += big_scratch(nq, groups, ORDERS[i], grad.shape[-2], grad.shape[-1])
+    scratch += [vm((own * 4, 128), F32)] * 3 + [vm((own, 128), BF16), vm((own // 2, 128), F32)]
+    scratch += [vm((64, 128), F32)] * 3 + [vm((128, 8, 128), F32), vm((8, 128), F32), vm((8, width), F32)]
+    scratch += [
+        vm((2, 2, *piece, 128), BF16), vm((2, 2, *piece, width), BF16),
+        vm((2, 2, *piece, width), BF16), vm((n // 2, 2, small_rows, 128), BF16),
+    ]
+    for i, part in enumerate(shapes):
+        scratch += big_scratch(nq, groups, ORDERS[i], *part[2:])
     scratch += small_scratch(nq, groups, small_rows)
-    scratch += tail_scratch(nq, piece, 128) + tail_scratch(nq, piece, width)
+    scratch += tail_scratch(nq, (*piece, 128)) + tail_scratch(nq, (*piece, width))
     scratch += [vm((3, 2, 64, 128), BF16)] * 4 + [vm((2, 3, 64, 128), BF16), vm((nq, 2, 3, 64, 128), BF16)]
-    sems = nq + 3 + max(groups.bit_length() - 2, 1)
+    scratch += [vm((3, 2, 64, 128), BF16)] * 2 + [vm((2, 3, 2, 64, 128), BF16)] * 2
+    scratch += [vm((2, 3, 64, 128), BF16), vm((nq + 1, 3, 64, 128), BF16)]
+    scratch += [dma((18,)), dma((n - 1,)), dma((n - 1,)), dma((n - 1,)), dma((n - 1,)), dma((nq + 5,)), dma((5,))]
+    scratch += gather_sems(nq, 1) + gather_sems(nq, 3)
+    scratch += [dma((2,)), dma((2,)), dma((nq - 1,)), dma((nq - 1,)), dma((nq - 1,)), dma((1,))]
+    sems = 2 * nq + 3 + max(groups.bit_length() - 2, 1)
     small_sems = 2 * nq + groups.bit_length() - 1
     scratch += [
-        dma((8,)), dma((N_BIG, sems)), dma((N_BIG, sems)), dma((N_BIG,)), dma((small_sems,)), dma((small_sems,)),
-        dma((3,)), dma((nq + 4,)), dma((3,)), dma((nq + 4,)), dma((2,)), dma((2,)), dma((nq - 1,)), dma((nq - 1,)),
+        dma((N_BIG, sems)), dma((N_BIG, sems)), dma((small_sems,)), dma((small_sems,)), dma((3,)), dma((nq + 4,)),
+        dma((3,)), dma((nq + 4,)), dma((2,)), dma((2,)), dma((nq - 1,)), dma((nq - 1,)),
     ]
     return pl.pallas_call(
-        functools.partial(back_kernel, n, groups),
+        functools.partial(layer_kernel, n, groups),
         out_shape=outs,
-        in_specs=[VMEM] * 13 + [SMEM] + [HBM] * (8 + N_BIG),
-        out_specs=[VMEM] * len(outs),
+        in_specs=[VMEM] * 10 + [SMEM, VMEM] + [HBM] * 7,
+        out_specs=[HBM] * 2 + [VMEM] * (len(outs) - 2),
         scratch_shapes=scratch,
-        compiler_params=pltpu.CompilerParams(collective_id=2, has_side_effects=True, vmem_limit_bytes=60 << 20),
-        name="back",
-    )(*ins, *hbm, *grads)
+        compiler_params=pltpu.CompilerParams(collective_id=0, has_side_effects=True, vmem_limit_bytes=63 << 20),
+        name="layer",
+    )(*rates, *vectors, resumed, cot, tokens, *weights)
 
 
 def finish_kernel(heads, grad_in, *refs):
@@ -1453,35 +1382,15 @@
     query_shift, key_scale,
 ):
     n, groups = lax.axis_size("seq"), lax.axis_size("grp")
-    nq = n // 4
-    seq_index = lax.axis_index("seq")
     sets, kinds, length, width = hidden_in.shape[1:]
-    chan = width // n
     heads = query_scale.shape[0]
     own_rows = sets * kinds * length
     vectors = (norm_gain, ffn_gain, ema_omega, query_scale, query_shift, key_scale)
-    own_low = hidden_in[0].reshape(own_rows, width)
-    (
-        tabs, power, power_rev, vec_wide, vec_head, starts, mat_shared,
-        result, grad_middle, grad_act, grad_base, slope_shared, shared, grad_units, sum_outer, sum_inner, sum_hidden,
-        sum_reset, sum_value, sent_keys, sum_wide, sum_head, ema_lanes, x_lanes, inner, tail_low,
-    ) = layer_call(
+    result, input_grad, *sums, d_small = layer_call(
         n, groups, [part.T for part in (ema_alpha, ema_delta, ema_beta, ema_eta)], [part[None] for part in vectors],
         cont_prompt, cotangent[0].reshape(own_rows, width), hidden_in[0],
         (value_proj, reset_proj, inner_proj, hidden_proj, outer_proj, shared_proj),
     )
-    mat_shared, tail_low = mat_shared.reshape(width, 128), tail_low.reshape(-1, width)
-
-    def shards(grad):
-        return grad.reshape(nq, 2, 2, -1, grad.shape[-1])
-
-    ins = (
-        grad_base, slope_shared, shared, sent_keys.reshape(2, 2, -1, 128), mat_shared, tabs, power, power_rev, vec_wide,
-        vec_head, starts, sum_wide, sum_head, cont_prompt,
-    )
-    hbm = (grad_act, ema_lanes, x_lanes, inner, grad_units, grad_middle, own_low, tail_low)
-    grads = [shards(part) for part in (sum_outer, sum_inner, sum_hidden, sum_reset, sum_value)]
-    input_grad, *sums, d_small = back_call(n, groups, ins, hbm, grads)
     wide = finish_call(n, heads, input_grad, sums, d_small)
     input_grad, d_outer, d_inner, d_hidden, d_reset, d_value, d_shared = wide[:7]
     rates = [part.T for part in wide[7:11]]

time: 169 us -> 154 us (0.911)
  Pallas kernels: 168 us -> 153 us
    pallas_call x1 -> x0, Pallas kernels: 76.5 us -> none  [back_call(): pl.pallas_call(functools.partial(back_kernel, n, groups), out_shape=outs,...]
    pallas_call x1, Pallas kernels: 88.8 us -> 150 us  [layer_call(): pl.pallas_call(functools.partial(layer_kernel, n, groups), out_shape=outs...]
where the time goes in v4:
time: 154 us
  Pallas kernels  153 us (99%)
    pallas_call x1, Pallas kernels, layer_call(): pl.pallas_call(functools.partial(layer_kernel, n, groups), out_shape=outs...  150 us

profile of v4, /device:TPU:0, one launch (start us, length us, event | category | flops | bytes accessed | tf_op | source)
XLA Modules:
  0.0 154.2 jit_solution(1737164358492985914)
XLA Ops:
  0.7 150.2 %layer.1 = (bf16[768,512]{1,0:T(8,128)(2,1)}, bf16[768,512]{1,0:T(8,128)(2,1)}, bf16[64,512]{1,0:T(8,128)(2,1)}, bf16[32,1024]{1,0:T(8,128)(2,1)}, bf16[64,512]{...) custom-call(bf16[16,32]{1,0:T(8,128)(2,1)} %bitcast.27, ...), custom_call_target="tpu_custom_call" | custom-call | tf_op jit(solution)/shard_map/layer/pallas_call | solution.py:1333
  150.8 0.0 copy-start
  150.8 2.4 %finish.1 = (bf16[768,512]{1,0:T(8,128)(2,1)}, f32[64,512]{1,0:T(8,128)}, f32[32,1024]{1,0:T(8,128)}, f32[64,512]{1,0:T(8,128)}, f32[32,1024]{1,0:T(8,128)}, /*i...) custom-call(bf16[768,512]{1,0:T(8,128)(2,1)} %get-tuple-element.44.g, ...), custom_call_target="tpu_custom_call" | custom-call | tf_op jit(solution)/shard_map/finish/pallas_call | solution.py:1369
  153.3 0.0 copy-done
  153.3 0.9 copy.38
Async XLA Ops:
  150.8 2.5 %copy-start = (bf16[768,512]{1,0:T(8,128)(2,1)S(1)}, bf16[768,512]{1,0:T(8,128)(2,1)}, u32[]{:S(2)}) copy-start(bf16[768,512]{1,0:T(8,128)(2,1)} %get-tuple-element.43) | copy-start | bytes 2359300

commit v5 on v4

--- a/solution.py
+++ b/solution.py
@@ -111,7 +111,11 @@
                 for j in js
             ]
             for step in range(SUB):
-                x = x_ref[pl.ds(x_base + step, 8, stride=SUB), :]
+                if part == 0:
+                    x = x_ref[pl.ds(x_base + step, 8, stride=SUB), :]
+                    kept[SUB * half + step] = x
+                else:
+                    x = kept[SUB * half + step]
                 for i in range(half):
                     kept[step * half + i] = state[i]
                     state[i] = dec[i] * state[i] + x
@@ -125,9 +129,15 @@
             edge = [-(adj[i] * state[i]) for i in range(half)]
             first, second = [None] * half, [None] * half
             for step in range(SUB - 1, -1, -1):
-                x = x_ref[pl.ds(x_base + step, 8, stride=SUB), :]
-                g = g_ref[pl.ds(base + step, 8, stride=SUB), :]
-                sums = [dx_ref[pl.ds(base + step, 8, stride=SUB), :], skip * g if part == 0 else None]
+                x = kept[SUB * half + step]
+                at = pl.ds(base + step, 8, stride=SUB)
+                if part == 0:
+                    g = g_ref[at, :]
+                    kept[SUB * (half + 1) + step] = g
+                    sums = [dx_ref[at, :], skip * g]
+                else:
+                    g = kept[SUB * (half + 1) + step]
+                    sums = [kept[SUB * (half + 2) + step], None]
                 for i in range(half):
                     full = adj[i] + g
                     term = weight[i] * full
@@ -136,7 +146,10 @@
                     first[i] = with_x if first[i] is None else first[i] + with_x
                     second[i] = with_s if second[i] is None else second[i] + with_s
                     adj[i] = dec[i] * full
-                dx_ref[pl.ds(base + step, 8, stride=SUB), :] = sums[0] + sums[1]
+                if part == 0:
+                    kept[SUB * (half + 2) + step] = sums[0] + sums[1]
+                else:
+                    dx_ref[at, :] = sums[0] + sums[1]
             for i, j in enumerate(js):
                 at = pl.ds(lane * 16 + j, 1)
                 flow = edge[i] + adj[i] * kept[i]
@@ -303,77 +316,52 @@
     def half(ref, width, which):
         return ref.at[:, pl.ds(pl.multiple_of(which * width, 128), width)]
 
-    up, down = (me.g, me.s + 4), (me.g, me.s - 4)
-    has_up, has_down = me.q < nq - 1, me.q > 0
+    def pieces(k, pos, which):
+        shard = me.quad(nq - k) * 4 + pos
+        return [half(out.at[shard], width, which) for out, width in mats]
+
     for i, (out, width) in enumerate(mats):
         mine = out.at[me.s]
         piece = half(mine, width, me.x)
-        post.send(piece, piece, zs.at[0, 0, i], zr.at[0, 0, i], up, has_up)
-        post.send(piece, piece, zs.at[1, 0, i], zr.at[1, 0, i], down, has_down)
+        for k in range(1, nq):
+            post.send(piece, piece, zs.at[k - 1, i], zr.at[k - 1, i], me.at_quad(me.quad(k)))
         post.send(mine, mine, ys.at[0, i], yr.at[0, i], me.side)
     for i, (out, width) in enumerate(mats):
         post.send(out.at[me.s], out.at[me.s], cs.at[0, i], cr.at[0, i], me.core)
     yield
-
-    def arrival(side, hop):
-        there = me.q - hop if side == 0 else me.q + hop
-        here = there >= 0 if side == 0 else there < nq
-        onward, to = (has_up, up) if side == 0 else (has_down, down)
-
-        def pieces(pos, which):
-            shard = jnp.clip(there, 0, nq - 1) * 4 + pos
-            return [half(out.at[shard], width, which) for out, width in mats]
-
-        return here, jnp.logical_and(here, onward), to, pieces
-
-    arrivals = [(hop, side) for hop in range(1, nq) for side in range(2)]
     side_pos = me.pos + 2 - 4 * me.y
-    for hop, side in arrivals:
-        here, onward, to, pieces = arrival(side, hop)
-        at = (hop - 1) * 2 + side
-        for i, piece in enumerate(pieces(me.pos, me.x)):
-            pl.when(here)(functools.partial(post.got, piece, zr.at[side, hop - 1, i]))
-            if hop < nq - 1:
-                post.send(piece, piece, zs.at[side, hop, i], zr.at[side, hop, i], to, onward)
-            post.send(piece, piece, ys.at[1 + at, i], yr.at[1 + at, i], me.side, here)
-            post.send(piece, piece, xs.at[at, i], xr.at[at, i], me.cross, here)
-            post.send(piece, piece, cs.at[1 + at, i], cr.at[1 + at, i], me.core, here)
-        if side:
+    for k in range(1, nq):
+        for i, piece in enumerate(pieces(k, me.pos, me.x)):
+            post.got(piece, zr.at[k - 1, i])
+            post.send(piece, piece, ys.at[k, i], yr.at[k, i], me.side)
+            post.send(piece, piece, xs.at[k - 1, i], xr.at[k - 1, i], me.cross)
+            post.send(piece, piece, cs.at[k, i], cr.at[k, i], me.core)
+        yield
+    for k in range(nq):
+        blocks = pieces(k, side_pos, me.x) if k else [out.at[me.q * 4 + side_pos] for out, _ in mats]
+        for i, piece in enumerate(blocks):
+            post.got(piece, yr.at[k, i])
+            if k:
+                post.send(piece, piece, xs.at[nq - 2 + k, i], xr.at[nq - 2 + k, i], me.cross)
+            post.send(piece, piece, cs.at[nq + k, i], cr.at[nq + k, i], me.core)
+        if k:
             yield
-    count = len(arrivals)
-    for i, (out, _) in enumerate(mats):
-        block = out.at[me.q * 4 + side_pos]
-        post.got(block, yr.at[0, i])
-        post.send(block, block, cs.at[1 + count, i], cr.at[1 + count, i], me.core)
-    for hop, side in arrivals:
-        here, _, _, pieces = arrival(side, hop)
-        at = (hop - 1) * 2 + side
-        for i, piece in enumerate(pieces(side_pos, me.x)):
-            pl.when(here)(functools.partial(post.got, piece, yr.at[1 + at, i]))
-            post.send(piece, piece, xs.at[count + at, i], xr.at[count + at, i], me.cross, here)
-            post.send(piece, piece, cs.at[2 + count + at, i], cr.at[2 + count + at, i], me.core, here)
-        if side:
-            yield
+    for group, pos in ((0, me.pos), (1, side_pos)):
+        for k in range(1, nq):
+            at = group * (nq - 1) + k - 1
+            for i, piece in enumerate(pieces(k, pos, other)):
+                post.got(piece, xr.at[at, i])
+                post.send(piece, piece, cs.at[2 * nq + at, i], cr.at[2 * nq + at, i], me.core)
+        yield
     flip = 1 - 2 * me.c
-    for group, pos in ((0, me.pos), (1, side_pos)):
-        for hop, side in arrivals:
-            here, _, _, pieces = arrival(side, hop)
-            at = group * count + (hop - 1) * 2 + side
-            to = 2 + 2 * count + at
-            for i, piece in enumerate(pieces(pos, other)):
-                pl.when(here)(functools.partial(post.got, piece, xr.at[at, i]))
-                post.send(piece, piece, cs.at[to, i], cr.at[to, i], me.core, here)
-        yield
     for group, pos in ((0, me.pos + flip), (1, side_pos + flip)):
         for i, (out, _) in enumerate(mats):
-            post.got(out.at[me.q * 4 + pos], cr.at[group * (1 + count), i])
-        for hop, side in arrivals:
-            here, _, _, pieces = arrival(side, hop)
-            at = (hop - 1) * 2 + side
-            for i, piece in enumerate(pieces(pos, me.x)):
-                pl.when(here)(functools.partial(post.got, piece, cr.at[group * (1 + count) + 1 + at, i]))
-            for i, piece in enumerate(pieces(pos, other)):
-                pl.when(here)(functools.partial(post.got, piece, cr.at[2 + 2 * count + group * count + at, i]))
+            post.got(out.at[me.q * 4 + pos], cr.at[group * nq, i])
+        for k in range(1, nq):
+            for i, piece in enumerate(pieces(k, pos, me.x)):
+                post.got(piece, cr.at[group * nq + k, i])
+            for i, piece in enumerate(pieces(k, pos, other)):
+                post.got(piece, cr.at[2 * nq + group * (nq - 1) + k - 1, i])
 
 
 def tokens_flow(me, post, x_in, x_out, ts, tr, local_sem):
@@ -417,8 +405,7 @@
 
 
 def gather_sems(nq, mats):
-    count = 2 * (nq - 1)
-    shapes = [(2, nq - 1, mats)] * 2 + [(1 + count, mats)] * 2 + [(2 * count, mats)] * 2 + [(2 + 4 * count, mats)] * 2
+    shapes = [(nq - 1, mats)] * 2 + [(nq, mats)] * 2 + [(2 * nq - 2, mats)] * 2 + [(4 * nq - 2, mats)] * 2
     return [pltpu.SemaphoreType.DMA(shape) for shape in shapes]
 
 
@@ -502,7 +489,7 @@
 
 
 def silu_grad(pre_act):
-    sigmoid_val = jax.nn.sigmoid(pre_act)
+    sigmoid_val = sigmoid(pre_act)
     return sigmoid_val * (1.0 + pre_act * (1.0 - sigmoid_val))
 
 
@@ -534,8 +521,12 @@
     return lax.dot_general(lhs, rhs, (((1,), (0,)), ((), ())), preferred_element_type=F32)
 
 
+def sigmoid(value):
+    return 0.5 * jnp.tanh(0.5 * value) + 0.5
+
+
 def silu_pair(pre):
-    sig = jax.nn.sigmoid(pre)
+    sig = sigmoid(pre)
     return pre * sig, sig * (1.0 + pre * (1.0 - sig))
 
 
@@ -548,56 +539,43 @@
     wide = width // 2
     ours = pl.ds(pl.multiple_of(me.x * wide, 128), wide)
     others = pl.ds(pl.multiple_of((1 - me.x) * wide, 128), wide)
-    copy1 = remote(grads.at[:, 1 - me.c], r1, send.at[0], recv.at[0], me.core)
+    copy1 = remote(grads.at[:, :, 1 - me.c], r1, send.at[0], recv.at[0], me.core)
     copy1.start()
     yield
     copy1.wait()
 
     def add1(i, carry):
-        r1[i] = (grads[i, me.c].astype(F32) + r1[i].astype(F32)).astype(BF16)
+        r1[i // 2, i % 2] = (grads[i // 2, i % 2, me.c].astype(F32) + r1[i // 2, i % 2].astype(F32)).astype(BF16)
         return carry
 
     lax.fori_loop(0, 2 * nq, add1, 0)
     if cross_first:
-        copy2 = remote(r1.at[:, :, others], r2, send.at[1], recv.at[1], me.cross)
-        copy2.start()
+        copy2 = remote(r1.at[:, :, :, others], r2, send.at[1], recv.at[1], me.cross)
     else:
-        copies2 = []
-        for k in range(nq):
-            copy = remote(r1.at[2 * k + 1 - me.y], r2.at[k], send.at[nq + 3 + k], recv.at[nq + 3 + k], me.side)
-            copy.start()
-            copies2.append(copy)
-    yield
+        copy2 = remote(r1.at[:, 1 - me.y], r2, send.at[1], recv.at[1], me.side)
+    copy2.start()
+    yield
+    copy2.wait()
     if cross_first:
-        copy2.wait()
-
         def add2(i, carry):
-            r2[i] = (r1[i, :, ours].astype(F32) + r2[i].astype(F32)).astype(BF16)
+            r2[i // 2, i % 2] = (r1[i // 2, i % 2, :, ours].astype(F32) + r2[i // 2, i % 2].astype(F32)).astype(BF16)
             return carry
 
         lax.fori_loop(0, 2 * nq, add2, 0)
-        copies3 = []
-        for k in range(nq):
-            copy = remote(r2.at[2 * k + 1 - me.y], r3.at[k], send.at[nq + 3 + k], recv.at[nq + 3 + k], me.side)
-            copy.start()
-            copies3.append(copy)
+        copy3 = remote(r2.at[:, 1 - me.y], r3, send.at[2], recv.at[2], me.side)
     else:
-        for copy in copies2:
-            copy.wait()
-
         def add2(i, carry):
-            r2[i] = (r1[2 * i + me.y].astype(F32) + r2[i].astype(F32)).astype(BF16)
+            r2[i] = (r1[i, me.y].astype(F32) + r2[i].astype(F32)).astype(BF16)
             return carry
 
         lax.fori_loop(0, nq, add2, 0)
-        copies3 = [remote(r2.at[:, :, others], r3, send.at[2], recv.at[2], me.cross)]
-        copies3[0].start()
-    yield
-    for copy in copies3:
-        copy.wait()
+        copy3 = remote(r2.at[:, :, others], r3, send.at[2], recv.at[2], me.cross)
+    copy3.start()
+    yield
+    copy3.wait()
 
     def add3(i, carry):
-        mine = r2[2 * i + me.y] if cross_first else r2[i, :, ours]
+        mine = r2[i, me.y] if cross_first else r2[i, :, ours]
         r3[i] = (mine.astype(F32) + r3[i].astype(F32)).astype(BF16)
         return carry
 
@@ -619,7 +597,7 @@
     remote(out.at[:, others], out.at[:, others], send.at[nq + 2], recv.at[nq + 2], me.cross).wait_recv()
     copy5.wait_send()
     for at, bit in enumerate(me.cross_bits()[1:]):
-        copy = remote(out, rx.at[at], send.at[2 * nq + 3 + at], recv.at[2 * nq + 3 + at], me.cross_bit(bit))
+        copy = remote(out, rx.at[at], send.at[nq + 3 + at], recv.at[nq + 3 + at], me.cross_bit(bit))
         copy.start()
         copy.wait()
         out[...] = (out[...].astype(F32) + rx[at].astype(F32)).astype(BF16)
@@ -628,9 +606,9 @@
 def big_scratch(nq, groups, cross_first, rows, width):
     extra = max(groups.bit_length() - 2, 1)
     half = width // 2
-    second = (2 * nq, rows, half) if cross_first else (nq, rows, width)
+    second = (nq, 2, rows, half) if cross_first else (nq, rows, width)
     spare = (extra, rows, width) if groups > 2 else (1, 16, 128)
-    shapes = [(2 * nq, rows, width), second, (nq, rows, half), (nq - 1, rows, half), spare]
+    shapes = [(nq, 2, rows, width), second, (nq, rows, half), (nq - 1, rows, half), spare]
     return [pltpu.VMEM(shape, BF16) for shape in shapes]
 
 
@@ -748,8 +726,9 @@
             self(*range(len(self.flows)))
 
 
-ORDERS = (True, False, True, False, True)
+ORDERS = (True, True, True, True, True)
 N_BIG = 5
+TURNS = ((0, 1), (2, 3), (0, 1, 4), (2, 3), (0, 1, 4), (2, 3))
 
 
 def layer_kernel(n, groups, *refs):
@@ -763,26 +742,26 @@
     p_rates, p_vecs, (resumed,) = take(4), take(6), take(1)
     cot, h_tokens, i_value, i_reset, i_inner, i_hidden, i_outer, i_shared = take(8)
     o_result, o_input = take(2)
-    sums, (out_small,), (staged,) = take(N_BIG), take(1), take(1)
+    sums, (out_early, out_late), (staged,) = take(N_BIG), take(2), take(1)
     tabs, power, power_rev, vec_wide, vec_head, starts, w_shared = take(7)
     g_middle, g_act, g_base, slope_s, shared_out = take(5)
     grads, (t_keys_sent, sum_wide, sum_head) = take(N_BIG), take(3)
     gathered, lift, tok, tail, x_lanes, ema, inner, finals = take(8)
-    early_all, w_hidden, w_inner, w_outer = take(4)
+    early_all, late_all = take(2)
     (
         values, slope_v, t_values, t_slope, t_keys, t_dv, t_dk, k_units, k_activ, k_gated, k_mid, k_inner, k_branch, k_gin,
         k_greset, k_gvalue,
     ) = take(16)
     g_lanes, b_inner, dx_lanes, k_gs, b_start, acc_in, acc_decay, acc_out, kept, omega_acc, gain_acc = take(11)
     b_flow = finals.at[0:384]
-    t_sum, t_grad, t_out, g_small = take(4)
+    t_sum, t_grad, t_out, g_early, g_late = take(5)
     big = [take(5) for _ in range(N_BIG)]
-    small, keys_s, tail_s, back_exchange = take(5), take(5), take(5), take(6)
+    small_early, small_late, keys_s, tail_s, back_exchange = take(5), take(5), take(5), take(5), take(6)
     exchange = take(6)
     load_sem, ss, sr, hs, hr, ts, tr = take(7)
     early_sem, late_sem = take(8), take(8)
     ess, ers, ezs, ezr, eps, epr = take(6)
-    big_send, big_recv, small_send, small_recv, k_send, k_recv, t_send, t_recv, bss, brs, bzs, bzr = take(12)
+    big_send, big_recv, fs, fr, small_send, small_recv, k_send, k_recv, t_send, t_recv, bss, brs, bzs, bzr = take(14)
 
     me = Place(n, groups)
     length = 128
@@ -806,9 +785,10 @@
     packing = [
         local_copy(i_value, early_all.at[me.s, 0:chan], 0),
         local_copy(i_reset, early_all.at[me.s, chan : 2 * chan], 1),
-        local_copy(i_hidden, w_hidden.at[me.s], 2),
-        local_copy(i_inner, w_inner.at[me.s], 3),
-        local_copy(i_outer, w_outer.at[me.s], 4),
+        local_copy(i_hidden, late_all.at[me.s, 0:rows_b], 2),
+        local_copy(i_outer, late_all.at[me.s, rows_b : 2 * rows_b], 3),
+        local_copy(i_inner.at[:, 0:width], late_all.at[me.s, 2 * rows_b : 2 * rows_b + chan], 4),
+        local_copy(i_inner.at[:, width : 2 * width], late_all.at[me.s, 2 * rows_b + chan : 2 * rows_b + 2 * chan], 14),
         local_copy(i_shared, w_shared.at[me.s], 5),
     ]
     fetch = [local_copy(h_tokens.at[p, k], tok.at[(p * 2 + k) * length : (p * 2 + k + 1) * length], 6 + p * 2 + k) for p in range(sets) for k in range(2)]
@@ -828,7 +808,7 @@
     for copy in packing:
         copy.wait()
     early = gather_flow(me, post, [early_all], *early_sem)
-    late = gather_flow(me, post, [w_hidden, w_inner, w_outer], *late_sem)
+    late = gather_flow(me, post, [late_all], *late_sem)
     words = tokens_flow(me, post, x_in, tail, ts, tr, load_sem.at[13])
     next(early)
     next(words)
@@ -898,22 +878,19 @@
 
     step(words, early)
     local_pass(0, count // 2)
-    step(late, early)
+    step(early, early)
     local_pass(count // 2, count // 2)
     state = state_flow(me, finals, tabs, sel, starts, *exchange, ess, ers, ezs, ezr, eps, epr)
     step(state)
-    step(late, early)
     step(state)
-    step(words, early, late)
+    step(words, early)
     step(state)
-    step(early, early)
+    step(late, early, early)
     step(state)
-    step(words)
+    step(words, late, late)
     for part in range(3):
         apply_pass(part * (count // 3), count // 3)
         step(early)
-        if part:
-            step(late)
     for _ in words:
         pass
 
@@ -924,14 +901,18 @@
             x_lanes[pl.ds(lane * total + own + m * length, length), :] = plain[:, lane * 128 : (lane + 1) * 128]
         return carry
 
+    step(late)
     lax.fori_loop(0, sets, tail_norm, 0)
     local_pass(count, sets)
     step(late)
     apply_pass(count, sets)
+    step(late)
     small_arrive(me, w_shared, post, hr)
     for _ in early:
         pass
     w_value, w_reset = early_all.at[:, 0:chan], early_all.at[:, chan : 2 * chan]
+    w_hidden, w_outer = late_all.at[:, 0:rows_b], late_all.at[:, rows_b : 2 * rows_b]
+    w_inner = [late_all.at[:, 2 * rows_b + i * chan : 2 * rows_b + (i + 1) * chan] for i in range(2)]
     hv = w_value.shape[2]
     parts = hv // CHUNK
     scale = 1.0 / math.sqrt(128.0)
@@ -940,7 +921,9 @@
         if name == "hidden":
             for _ in late:
                 pass
-        elif name in ("tail", "reset"):
+        elif name == "tail":
+            step(late, late)
+        elif name == "reset":
             step(late)
 
     gain_one, gain_two = vec_wide[0:1], vec_wide[1:2]
@@ -971,9 +954,9 @@
             t_values[m, :, part * CHUNK : (part + 1) * CHUNK] = value.astype(BF16)
             t_slope[m, :, part * CHUNK : (part + 1) * CHUNK] = slope.astype(BF16)
         pre = ema_rows(own + at, length)
-        activ = (pre * jax.nn.sigmoid(pre)).astype(BF16)
+        activ = (pre * sigmoid(pre)).astype(BF16)
         shared = nn(activ, w_shared[...].reshape(width, 128))
-        t_keys[m] = (shared * jax.nn.sigmoid(shared) * k_mul).astype(BF16)
+        t_keys[m] = (shared * sigmoid(shared) * k_mul).astype(BF16)
         return carry
 
     lax.fori_loop(0, sets, tail_step, 0)
@@ -1005,7 +988,7 @@
             slope_v[:, cut] = slope.astype(BF16)
         ready("reset")
         pre = ema_rows(p * 2 * length, 2 * length)
-        activ = (pre * jax.nn.sigmoid(pre)).astype(BF16)
+        activ = (pre * sigmoid(pre)).astype(BF16)
         k_activ[here, :] = activ
         shared, slope = silu_pair(nn(activ, w_shared[...].reshape(width, 128)))
         slope_s[here, :] = slope
@@ -1033,7 +1016,7 @@
             mix = jnp.concatenate((mix_p, mix_c), axis=0)
             put(mixed, part, mix)
             gate = get(reset_pre, part)
-            k_gated[here, cut] = (gate * jax.nn.sigmoid(gate) * mix).astype(BF16)
+            k_gated[here, cut] = (gate * sigmoid(gate) * mix).astype(BF16)
         ready("hidden")
         middle = x + nn(k_gated[here, :], w_hidden[...].reshape(-1, width))
         plain_mid, inv_mid = norm_rows(middle)
@@ -1042,7 +1025,7 @@
         ready("inner")
         for part in range(parts):
             cut = slice(part * CHUNK, (part + 1) * CHUNK)
-            inner, slope = silu_pair(nn(mid_low, columns(w_inner, part)))
+            inner, slope = silu_pair(nn(mid_low, columns(w_inner[part * CHUNK // width], part % (width // CHUNK))))
             k_inner[here, cut] = inner.astype(BF16)
             put(slope_i, part, slope)
         ready("outer")
@@ -1051,7 +1034,8 @@
         for part in range(parts):
             cut = slice(part * CHUNK, (part + 1) * CHUNK)
             k_gin[here, cut] = (nt(top, rows(w_outer, part)) * get(slope_i, part)).astype(BF16)
-        back = nt(k_gin[here, :], w_inner[...].reshape(width, -1))
+        back = nt(k_gin[here, 0:width], w_inner[0][...].reshape(width, width))
+        back = back + nt(k_gin[here, width : 2 * width], w_inner[1][...].reshape(width, width))
         sum_wide[0:1] += jnp.sum(back * plain_mid, axis=0, keepdims=True)
         g_mid = top.astype(F32) + norm_back(back, plain_mid, inv_mid, gain_two)
         g_middle[here, :] = g_mid
@@ -1120,7 +1104,7 @@
         for lane in range(lanes):
             cut = slice(lane * 128, (lane + 1) * 128)
             pre = ema[pl.ds(lane * total + at, length), :]
-            sig = jax.nn.sigmoid(pre)
+            sig = sigmoid(pre)
             back = g_act[here, cut] + nt(gs, w_shared[lane * per : (lane + 1) * per].reshape(128, 128))
             back = back * (sig * (1.0 + pre * (1.0 - sig)))
             g_lanes[pl.ds(lane * own + at, length), :] = back
@@ -1146,11 +1130,11 @@
         return norm_back(units, plain, inv, gain_one)
 
     def weight_grad(lhs, rhs, out, many):
-        block_rows = CHUNK // out.shape[2] // 2
+        quads = CHUNK // out.shape[3] // 4
 
         def step(i, carry):
             block = tn(lhs[0:many, pl.ds(pl.multiple_of(i * CHUNK, CHUNK), CHUNK)], rhs[0:many, :])
-            out[pl.ds(i * block_rows, block_rows)] = block.astype(BF16).reshape(block_rows, 2, out.shape[2], out.shape[3])
+            out[pl.ds(i * quads, quads)] = block.astype(BF16).reshape(quads, *out.shape[1:])
             return carry
 
         lax.fori_loop(0, lhs.shape[1] // CHUNK, step, 0)
@@ -1177,7 +1161,7 @@
     local_back(0)
     adjoint = adjoint_flow(me, b_flow, tabs, sel, b_start, *back_exchange, bss, brs, bzs, bzr)
     next(adjoint)
-    steps(3, 0)
+    steps(3)
 
     def tail_back(m, carry):
         at = pl.multiple_of(own + m * length, length)
@@ -1185,10 +1169,18 @@
         return carry
 
     lax.fori_loop(0, sets, tail_back, 0)
+    block = tn(k_activ[...], k_gs[...]).astype(BF16)
+    g_early[:, :, 0:chan] = block.reshape(n // 2, 2, chan, 128)
+    tops = jnp.concatenate((sum_head[0:2], sum_head[2:3] + gain_acc[1:2, 0:128], jnp.zeros((13, 128), F32)), axis=0)
+    tops = jnp.broadcast_to(tops.astype(BF16)[None, None], (n // 2, 2, 16, 128))
+    g_early[:, :, chan:] = tops
+    first = small_flow(me, g_early, *small_early, out_early, fs, fr)
+    next(first)
     next(adjoint)
     weight_grad(k_units, k_gvalue, grads[4], total)
-    steps(4, 1)
+    steps(4)
     next(adjoint)
+    steps(0, 1)
 
     def units_step(i, carry):
         at = pl.multiple_of(i * CHUNK, CHUNK)
@@ -1220,8 +1212,8 @@
         )
         if row < 3:
             next(ends)
-        if row < count - 1:
-            steps(*range(N_BIG))
+        next(first, None)
+        steps(*TURNS[row])
 
     def own_rows(row, carry):
         here = pl.ds(pl.multiple_of(row * length, length), length)
@@ -1241,13 +1233,8 @@
         block = [part[lane * 16 : lane * 16 + 16] for part in parts]
         block += [omega_acc[lane : lane + 1], gain_acc[0:1, cut], sum_wide[0:1, cut], jnp.zeros((61, 128), F32)]
         block = jnp.concatenate(block, axis=0).T.astype(BF16)
-        g_small[lane * per : (lane + 1) * per, :, 0:chan] = block.reshape(per, 2, chan, 128)
-    block = tn(k_activ[...], k_gs[...]).astype(BF16)
-    g_small[:, :, chan : 2 * chan] = block.reshape(n // 2, 2, chan, 128)
-    heads = jnp.concatenate((sum_head[0:2], sum_head[2:3] + gain_acc[1:2, 0:128], jnp.zeros((13, 128), F32)), axis=0)
-    heads = jnp.broadcast_to(heads.astype(BF16)[None, None], (n // 2, 2, 16, 128))
-    g_small[:, :, 2 * chan :] = heads
-    little = small_flow(me, g_small, *small, out_small, small_send, small_recv)
+        g_late[lane * per : (lane + 1) * per] = block.reshape(per, 2, chan, 128)
+    little = small_flow(me, g_late, *small_late, out_late, small_send, small_recv)
     next(little)
     for _ in ends:
         pass
@@ -1286,11 +1273,11 @@
     total = own + sets * length
     chan, hv = weights[0].shape
     rows_b = weights[3].shape[0]
-    small_rows = 2 * chan + 16
-    wide, tall = (n // 2, 2, chan, hv), (n // 2, 2, rows_b, width)
+    early_rows = chan + 16
+    wide, tall = (nq, 2, 2, chan, hv), (nq, 2, 2, rows_b, width)
     shapes = [tall, wide, tall, wide, wide]
     piece = (sets, length // 4)
-    outs = [shape((own, width), BF16)] * 2 + [shape(part[2:], BF16) for part in shapes] + [shape((small_rows, 128), BF16)]
+    outs = [shape((own, width), BF16)] * 2 + [shape(part[3:], BF16) for part in shapes] + [shape((early_rows, 128), BF16), shape((chan, 128), BF16)]
     scratch = [
         vm((own, width), BF16), vm((14, 64, 128), F32), vm((512, 128), F32), vm((512, 128), F32), vm((8, width), F32), vm((8, 128), F32),
         vm((total // 2, 128), F32), vm((n, chan, 128), BF16),
@@ -1301,7 +1288,7 @@
     scratch += [
         vm((n, 32, 128), BF16), vm((5, 16, 128), F32), vm((own, width), BF16), vm((sets, length, width), BF16),
         vm((total * 4, 128), F32), vm((total * 4, 128), F32), vm((total * 4, 128), F32), vm((total // 2, 128), F32),
-        vm((n, 2 * chan, hv), BF16), vm((n, rows_b, width), BF16), vm((n, chan, hv), BF16), vm((n, rows_b, width), BF16),
+        vm((n, 2 * chan, hv), BF16), vm((n, 2 * rows_b + 2 * chan, width), BF16),
         vm((2 * length, hv), BF16), vm((2 * length, hv), BF16),
         vm((sets, length, hv), BF16), vm((sets, length, hv), BF16), vm((sets, length, 128), BF16),
         vm((sets, length, hv), F32), vm((sets, length, 128), F32),
@@ -1309,25 +1296,25 @@
         vm((own, hv), BF16), vm((own, width), BF16), vm((own, hv), BF16), vm((own, hv), BF16), vm((total, hv), BF16),
     ]
     scratch += [vm((own * 4, 128), F32)] * 3 + [vm((own, 128), BF16), vm((own // 2, 128), F32)]
-    scratch += [vm((64, 128), F32)] * 3 + [vm((128, 8, 128), F32), vm((8, 128), F32), vm((8, width), F32)]
+    scratch += [vm((64, 128), F32)] * 3 + [vm((SUB * 11, 8, 128), F32), vm((8, 128), F32), vm((8, width), F32)]
     scratch += [
         vm((2, 2, *piece, 128), BF16), vm((2, 2, *piece, width), BF16),
-        vm((2, 2, *piece, width), BF16), vm((n // 2, 2, small_rows, 128), BF16),
+        vm((2, 2, *piece, width), BF16), vm((n // 2, 2, early_rows, 128), BF16), vm((n // 2, 2, chan, 128), BF16),
     ]
     for i, part in enumerate(shapes):
-        scratch += big_scratch(nq, groups, ORDERS[i], *part[2:])
-    scratch += small_scratch(nq, groups, small_rows)
+        scratch += big_scratch(nq, groups, ORDERS[i], *part[3:])
+    scratch += small_scratch(nq, groups, early_rows) + small_scratch(nq, groups, chan)
     scratch += tail_scratch(nq, (*piece, 128)) + tail_scratch(nq, (*piece, width))
     scratch += [vm((3, 2, 64, 128), BF16)] * 4 + [vm((2, 3, 64, 128), BF16), vm((nq, 2, 3, 64, 128), BF16)]
     scratch += [vm((3, 2, 64, 128), BF16)] * 2 + [vm((2, 3, 2, 64, 128), BF16)] * 2
     scratch += [vm((2, 3, 64, 128), BF16), vm((nq + 1, 3, 64, 128), BF16)]
     scratch += [dma((18,)), dma((n - 1,)), dma((n - 1,)), dma((n - 1,)), dma((n - 1,)), dma((nq + 5,)), dma((5,))]
-    scratch += gather_sems(nq, 1) + gather_sems(nq, 3)
+    scratch += gather_sems(nq, 1) + gather_sems(nq, 1)
     scratch += [dma((2,)), dma((2,)), dma((nq - 1,)), dma((nq - 1,)), dma((nq - 1,)), dma((1,))]
-    sems = 2 * nq + 3 + max(groups.bit_length() - 2, 1)
+    sems = nq + 3 + max(groups.bit_length() - 2, 1)
     small_sems = 2 * nq + groups.bit_length() - 1
     scratch += [
-        dma((N_BIG, sems)), dma((N_BIG, sems)), dma((small_sems,)), dma((small_sems,)), dma((3,)), dma((nq + 4,)),
+        dma((N_BIG, sems)), dma((N_BIG, sems)), dma((small_sems,)), dma((small_sems,)), dma((small_sems,)), dma((small_sems,)), dma((3,)), dma((nq + 4,)),
         dma((3,)), dma((nq + 4,)), dma((2,)), dma((2,)), dma((nq - 1,)), dma((nq - 1,)),
     ]
     return pl.pallas_call(
@@ -1341,39 +1328,41 @@
     )(*rates, *vectors, resumed, cot, tokens, *weights)
 
 
-def finish_kernel(heads, grad_in, *refs):
-    sums, small, grad_out = refs[:N_BIG], refs[N_BIG], refs[N_BIG + 1]
+def finish_kernel(heads, result_in, grad_in, *refs):
+    sums, early, late, result_out, grad_out = refs[:N_BIG], *refs[N_BIG : N_BIG + 4]
+    refs = refs[2:]
     outs = refs[N_BIG + 2 : 2 * N_BIG + 2]
     shared, rates, vecs = refs[2 * N_BIG + 2], refs[2 * N_BIG + 3 : 2 * N_BIG + 7], refs[2 * N_BIG + 7 : 2 * N_BIG + 13]
+    result_out[...] = result_in[...]
     grad_out[...] = grad_in[...]
     for src, dst in zip(sums, outs):
         dst[...] = src[...].astype(F32)
     chan = shared.shape[0]
-    shared[...] = small[chan : 2 * chan].astype(F32)
-    block = small[0:chan].astype(F32).T
+    shared[...] = early[0:chan].astype(F32)
+    block = late[...].astype(F32).T
     for i, ref in enumerate(rates):
         ref[...] = block[16 * i : 16 * i + 16]
     for i in range(3):
         vecs[i][...] = block[64 + i : 65 + i]
     mine = lax.axis_index("seq") * heads
-    rows = pltpu.roll(small[2 * chan : 2 * chan + 16].astype(F32), (128 - mine) % 128, 1)
+    rows = pltpu.roll(early[chan : chan + 16].astype(F32), (128 - mine) % 128, 1)
     for i in range(3):
         vecs[3 + i][...] = rows[i : i + 1, 0:heads]
 
 
-def finish_call(n, heads, input_grad, sums, small):
+def finish_call(n, heads, result, input_grad, sums, early, late):
     shape = jax.ShapeDtypeStruct
-    chan = (small.shape[0] - 16) // 2
-    outs = [shape(input_grad.shape, BF16)] + [shape(part.shape, F32) for part in sums] + [shape((chan, 128), F32)]
+    chan = late.shape[0]
+    outs = [shape(input_grad.shape, BF16)] * 2 + [shape(part.shape, F32) for part in sums] + [shape((chan, 128), F32)]
     outs += [shape((16, chan), F32)] * 4 + [shape((1, chan), F32)] * 3 + [shape((1, heads), F32)] * 3
     return pl.pallas_call(
         functools.partial(finish_kernel, heads),
         out_shape=outs,
-        in_specs=[VMEM] * (N_BIG + 2),
+        in_specs=[VMEM] * (N_BIG + 4),
         out_specs=[VMEM] * len(outs),
         compiler_params=pltpu.CompilerParams(vmem_limit_bytes=60 << 20),
         name="finish",
-    )(input_grad, *sums, small)
+    )(result, input_grad, *sums, early, late)
 
 
 def local(
@@ -1386,12 +1375,12 @@
     heads = query_scale.shape[0]
     own_rows = sets * kinds * length
     vectors = (norm_gain, ffn_gain, ema_omega, query_scale, query_shift, key_scale)
-    result, input_grad, *sums, d_small = layer_call(
+    result, input_grad, *sums, early, late = layer_call(
         n, groups, [part.T for part in (ema_alpha, ema_delta, ema_beta, ema_eta)], [part[None] for part in vectors],
         cont_prompt, cotangent[0].reshape(own_rows, width), hidden_in[0],
         (value_proj, reset_proj, inner_proj, hidden_proj, outer_proj, shared_proj),
     )
-    wide = finish_call(n, heads, input_grad, sums, d_small)
+    result, *wide = finish_call(n, heads, result, input_grad, sums, early, late)
     input_grad, d_outer, d_inner, d_hidden, d_reset, d_value, d_shared = wide[:7]
     rates = [part.T for part in wide[7:11]]
     vecs = [part.reshape(part.shape[1]) for part in wide[11:17]]

time: 154 us -> 137 us (0.89)
  Pallas kernels: 153 us -> 136 us
    pallas_call x1, Pallas kernels: 150 us -> 133 us  [layer_call(): pl.pallas_call(functools.partial(layer_kernel, n, groups), out_shape=outs...]
where the time goes in v5:
time: 137 us
  Pallas kernels  136 us (99%)
    pallas_call x1, Pallas kernels, layer_call(): pl.pallas_call(functools.partial(layer_kernel, n, groups), out_shape=outs...  133 us
    pallas_call x1, Pallas kernels, finish_call(): pl.pallas_call(functools.partial(finish_kernel, heads), out_shape=outs, i...  2.91 us

profile of v5, /device:TPU:0, one launch (start us, length us, event | category | flops | bytes accessed | tf_op | source)
XLA Modules:
  0.0 137.1 jit_solution(11559620314158941998)
XLA Ops:
  0.7 133.4 %layer.1 = (bf16[768,512]{1,0:T(8,128)(2,1)}, bf16[768,512]{1,0:T(8,128)(2,1)}, bf16[64,512]{1,0:T(8,128)(2,1)}, bf16[32,1024]{1,0:T(8,128)(2,1)}, bf16[64,512]{...) custom-call(bf16[16,32]{1,0:T(8,128)(2,1)} %bitcast.26, ...), custom_call_target="tpu_custom_call" | custom-call | tf_op jit(solution)/shard_map/layer/pallas_call | solution.py:1320
  134.0 2.9 %finish.1 = (bf16[768,512]{1,0:T(8,128)(2,1)}, bf16[768,512]{1,0:T(8,128)(2,1)}, f32[64,512]{1,0:T(8,128)}, f32[32,1024]{1,0:T(8,128)}, f32[64,512]{1,0:T(8,128)...) custom-call(bf16[768,512]{1,0:T(8,128)(2,1)} %get-tuple-element.45.r, ...), custom_call_target="tpu_custom_call" | custom-call | tf_op jit(solution)/shard_map/finish/pallas_call | solution.py:1358

commit v6 on v5

--- a/solution.py
+++ b/solution.py
@@ -728,7 +728,7 @@
 
 ORDERS = (True, True, True, True, True)
 N_BIG = 5
-TURNS = ((0, 1), (2, 3), (0, 1, 4), (2, 3), (0, 1, 4), (2, 3))
+TURNS = ((2,), (0, 3), (1, 4), (0, 2), (1, 3), (0, 2, 4))
 
 
 def layer_kernel(n, groups, *refs):
@@ -922,9 +922,9 @@
             for _ in late:
                 pass
         elif name == "tail":
+            step(late)
+        elif name == "reset":
             step(late, late)
-        elif name == "reset":
-            step(late)
 
     gain_one, gain_two = vec_wide[0:1], vec_wide[1:2]
     q_mul, q_add, k_mul = vec_head[0:1], vec_head[1:2], vec_head[2:3]

time: 137 us -> 134 us (0.978)
  Pallas kernels: 136 us -> 133 us
    pallas_call x1, Pallas kernels: 133 us -> 130 us  [layer_call(): pl.pallas_call(functools.partial(layer_kernel, n, groups), out_shape=outs...]
where the time goes in v6:
time: 134 us; the launch traced here: 133 us
  Pallas kernels  133 us (99%)
    pallas_call x1, Pallas kernels, layer_call(): pl.pallas_call(functools.partial(layer_kernel, n, groups), out_shape=outs...  130 us
    pallas_call x1, Pallas kernels, finish_call(): pl.pallas_call(functools.partial(finish_kernel, heads), out_shape=outs, i...  2.91 us

profile of v6, /device:TPU:0, one launch (start us, length us, event | category | flops | bytes accessed | tf_op | source)
XLA Modules:
  0.0 133.4 jit_solution(1858009652559375421)
XLA Ops:
  0.7 129.7 %layer.1 = (bf16[768,512]{1,0:T(8,128)(2,1)}, bf16[768,512]{1,0:T(8,128)(2,1)}, bf16[64,512]{1,0:T(8,128)(2,1)}, bf16[32,1024]{1,0:T(8,128)(2,1)}, bf16[64,512]{...) custom-call(bf16[16,32]{1,0:T(8,128)(2,1)} %bitcast.26, ...), custom_call_target="tpu_custom_call" | custom-call | tf_op jit(solution)/shard_map/layer/pallas_call | solution.py:1320
  130.4 2.9 %finish.1 = (bf16[768,512]{1,0:T(8,128)(2,1)}, bf16[768,512]{1,0:T(8,128)(2,1)}, f32[64,512]{1,0:T(8,128)}, f32[32,1024]{1,0:T(8,128)}, f32[64,512]{1,0:T(8,128)...) custom-call(bf16[768,512]{1,0:T(8,128)(2,1)} %get-tuple-element.45.r, ...), custom_call_target="tpu_custom_call" | custom-call | tf_op jit(solution)/shard_map/finish/pallas_call | solution.py:1358
